TPU v7x, 32 devices: a whole 2x2x4 slice. The times are simulated.
32 devices in a mesh: groups: 2 (over x), tm: 16 (over z, y, core).
Axes of the slice: x: 2, y: 2, z: 4, core: 2. Of those that a mesh axis runs over, the one named last changes fastest.
Arguments:
- loglik: float32 [4, 1024, 512], P('groups', None, 'tm'), parts along dimension 0, may hold values from -105 to 105
- trans_weight: float32 [256, 256], replicated, may hold values from 0 to 1, as said below
- block_mask: int32 [4, 4], replicated, may hold values from 0 to 1, as said below
- init_weight: float32 [256], replicated, may hold values from 0.01 to 1
- lengths: int32 [4], P('groups'), parts along dimension 0, may hold values from 512 to 1024, as said below
- pdf_map: int32 [256], replicated, may hold values from 0 to 511
Outputs:
- log_forward: float32 [4, 1024, 256], P('groups', 'tm'), parts along dimension 0
- log_gain: float32 [4, 1024], P('groups', 'tm'), parts along dimension 0
There are 2 independent parts, one for each index of `groups`. A program takes and returns all parts, laid end to end along the dimension named above; an argument that names none is the same for every part. Nothing has to cross between parts.
Inputs may be any that keep to these rules, and one draw needn't show every extreme that they name: `block_mask`: the diagonal blocks are always allowed. `lengths`: some utterance has all 1024 frames. `trans_weight`: every entry is positive.
All inputs are finite; a program needn't handle non-finite values.
Results may differ from a plain program's by a relative error of at most 0.0003.
Values sent between devices are 32-bit elements; how exact they have to be, the bound alone decides.
No kernel may reach another device: no remote copies, remote signals or barrier semaphores. Data moves between devices by JAX's collectives and lax.ppermute only.
A program may use at most 128 MiB of HBM per device.

v0:
```python
import jax
import jax.numpy as jnp
from jax import lax
from jax.sharding import PartitionSpec as P


def carried_in(part, axis, combine, identity):
    place = lax.axis_index(axis)
    gathered = lax.all_gather(part, axis)
    state = jnp.zeros_like(part) + jnp.asarray(identity, part.dtype)

    def one(turn, state):
        return combine(state, lax.dynamic_index_in_dim(gathered, turn, 0, False))

    return lax.fori_loop(0, place, one, state)


def transitions(trans_weight, block_mask):
    width = trans_weight.shape[0] // block_mask.shape[0]
    expanded = jnp.repeat(jnp.repeat(block_mask, width, axis=0), width, axis=1).astype(jnp.float32)
    masked = trans_weight * expanded
    return masked / jnp.sum(masked, axis=1, keepdims=True)


def rescale(matrix):
    return matrix / jnp.max(matrix, axis=(1, 2), keepdims=True)


def chain_product(earlier, later):
    joined = jnp.einsum("uij,ujk->uik", earlier, later, precision=lax.Precision.HIGHEST)
    return rescale(joined)


def shards(loglik, trans_weight, block_mask, init_weight, lengths, pdf_map):
    trans = transitions(trans_weight, block_mask)
    states = trans.shape[0]
    utts = loglik.shape[0]
    start = init_weight / jnp.sum(init_weight)
    g_vals = jnp.take(
        lax.all_to_all(loglik, "tm", split_axis=1, concat_axis=2, tiled=True), pdf_map, axis=2
    )
    top = jnp.max(g_vals, axis=2, keepdims=True)
    factors = jnp.exp(g_vals - top)
    tops = top[..., 0]
    frame_count = factors.shape[1]
    offset = lax.axis_index("tm") * frame_count
    frame_ids = offset + jnp.arange(frame_count, dtype=jnp.int32)
    live = frame_ids[None, :] < lengths[:, None]
    seq_factors = jnp.moveaxis(factors, 1, 0)
    seq_tops = jnp.moveaxis(tops, 1, 0)
    seq_live = jnp.moveaxis(live, 1, 0)
    identity = jnp.broadcast_to(jnp.eye(states, dtype=jnp.float32), (utts, states, states))

    def extend(index, matrices):
        factor = lax.dynamic_index_in_dim(factors, index, 1, keepdims=False)
        alive = lax.dynamic_index_in_dim(live, index, 1, keepdims=False)
        step_op = jnp.where(alive[:, None, None], trans[None, :, :] * factor[:, None, :], identity)
        return chain_product(matrices, step_op)

    local_op = lax.fori_loop(0, frame_count, extend, identity)
    earlier_op = carried_in(local_op, "tm", chain_product, identity)
    incoming = jnp.einsum("i,uik->uk", start, earlier_op, precision=lax.Precision.HIGHEST)
    incoming = incoming / jnp.sum(incoming, axis=1, keepdims=True)

    def advance(alpha, inputs):
        factor, top, alive = inputs
        v_new = jnp.dot(alpha, trans, precision=lax.Precision.HIGHEST) * factor
        total = jnp.sum(v_new, axis=1, keepdims=True)
        fresh = jnp.where(alive[:, None], v_new / total, alpha)
        gain = jnp.where(alive, jnp.log(total[:, 0]) + top, jnp.float32(0.0))
        return (fresh, (fresh, gain))

    _, (occupied, gains) = lax.scan(advance, incoming, (seq_factors, seq_tops, seq_live))
    return (jnp.log(jnp.moveaxis(occupied, 0, 1)), jnp.moveaxis(gains, 0, 1))


def solution(mesh):
    return jax.shard_map(
        shards,
        mesh=mesh,
        in_specs=(P("groups", None, "tm"), P(), P(), P(), P("groups"), P()),
        out_specs=(P("groups", "tm", None), P("groups", "tm")),
        check_vma=False,
    )
```

profile of v0, /device:TPU:29, one launch (start us, length us, event | category | flops | bytes accessed | tf_op | source)
XLA Modules:
  0.0 243.3 jit_solution(11408980057508970936)
XLA Ops:
  7.2 1.4 copy.32
  8.6 1.7 reshape.49
  10.3 6.3 %all-to-all-start = ((f32[16,1,4096]{2,1,0:T(1,128)}), f32[16,1,4096]{2,1,0:T(1,128)S(1)}, u32[]{:S(2)}, u32[]{:S(2)}) async-start(f32[16,1,4096]{2,1,0:T(1,128)} %reshape.49), calls=%async_computation | async-start | bytes 524288 | tf_op jit(solution)/shard_map/all_to_all | solution.py:40
  17.4 1.1 copy.31
  21.0 2.7 %all-to-all-done = f32[16,1,4096]{2,1,0:T(1,128)S(1)} async-done(((f32[16,1,4096]{2,1,0:T(1,128)}), f32[16,1,4096]{2,1,0:T(1,128)S(1)}, u32[]{:S(2)}, u32[]{:S(2)}) %all-to-all-start) | async-done | bytes 262176 | tf_op jit(solution)/shard_map/all_to_all | solution.py:40
  24.2 1.3 reduce.2
  25.5 0.9 reshape.50
  27.3 1.0 gather_fusion
  29.2 61.0 %while.40 = (s32[]{:T(128)}, f32[2,256,256]{1,2,0:T(8,128)S(1)}, pred[2,64]{0,1:T(8,128)(4,1)S(1)}, f32[256,256]{0,1:T(8,128)S(1)}, f32[2,64,256]{2,0,1:T(2,128)S(1)}, /*index=5*/f32[256,256]{0,1:T(8,128)S(1)}, s32[]{:T(128)}) while((s32[]{:T(128)}, f32[2,256,256]{1,2,0:T(8,128)S(1)}, pred[2,64]{0,1:T(8,128)(4,1)S(1)}, ...), condition=%wide.region_5.6_spmd.clone, body=%wide.region_3.5_spmd.clone.sunk | while | flops 403177472 | bytes 2627691 | solution.py:60
  29.2 0.8 fusion.48
  30.2 0.8 fusion.48
  31.1 0.8 fusion.48
  32.1 0.8 fusion.48
  34.0 0.8 fusion.48
  37.8 0.8 fusion.48
  38.8 0.8 fusion.48
  42.6 0.8 fusion.48
  47.4 0.8 fusion.48
  52.1 0.8 fusion.48
  55.9 0.8 fusion.48
  56.9 0.8 fusion.48
  60.7 0.8 fusion.48
  65.5 0.8 fusion.48
  70.2 0.8 fusion.48
  74.1 0.8 fusion.48
  75.0 0.8 fusion.48
  78.8 0.8 fusion.48
  83.6 0.8 fusion.48
  88.4 0.8 fusion.48
  90.2 1.0 copy.36
  93.4 71.4 %all-gather.3.cloned.1.call-done = f32[32,256,256]{2,1,0:T(8,128)} async-done(((f32[2,256,256]{2,1,0:T(8,128)}), f32[32,256,256]{2,1,0:T(8,128)}) %all-gather.3.cloned.1.call-update) | async-done | bytes 8388624 | tf_op jit(solution)/shard_map/all_gather | solution.py:9
  164.8 34.2 %while.38 = (s32[]{:T(128)}, f32[2,256,256]{1,2,0:T(8,128)S(1)}, s32[]{:T(128)}, f32[16,2,256,256]{3,2,1,0:T(8,128)}, s32[]{:T(128)}, /*index=5*/s32[]{:T(128)}, s32[]{:T(128)}) while((s32[]{:T(128)}, f32[2,256,256]{1,2,0:T(8,128)S(1)}, s32[]{:T(128)}, f32[16,2,256,256]{3,2,1,0:T(8,128)}, s32[]{:T(128)}, /*index=5*/s32[]{:T(128)}, ...), condition=%wide.region_8.9_spmd, body=%wide.region_6.8_spmd.sunk | while | flops 402915328 | bytes 2621571 | solution.py:15
  164.8 2.1 fusion.41
  167.1 2.1 fusion.41
  169.4 2.1 fusion.41
  171.7 2.1 fusion.41
  173.9 2.1 fusion.41
  176.2 2.1 fusion.41
  178.5 2.1 fusion.41
  180.8 2.1 fusion.41
  183.1 2.1 fusion.41
  185.3 2.1 fusion.41
  187.6 2.1 fusion.41
  189.9 2.1 fusion.41
  192.2 2.1 fusion.41
  194.5 2.1 fusion.41
  196.8 2.1 fusion.41
  199.7 35.4 %while.39 = (s32[]{:T(128)}, f32[2,256]{1,0:T(2,128)S(1)}, f32[64,2,256]{2,0,1:T(8,128)S(1)}, f32[64,2]{1,0:T(8,128)S(1)}, pred[64,2]{1,0:T(8,128)(4,1)S(1)}, /*...) while((s32[]{:T(128)}, f32[2,256]{1,0:T(2,128)S(1)}, ...), condition=%wide.region_12.13_spmd, body=%wide.region_10.12_spmd.sunk | while | flops 1574916 | bytes 282809 | solution.py:73
  (739 shorter events, 87.3 us)
Async XLA Ops:
  10.3 13.4 %all-to-all-start = ((f32[16,1,4096]{2,1,0:T(1,128)}), f32[16,1,4096]{2,1,0:T(1,128)S(1)}, u32[]{:S(2)}, u32[]{:S(2)}) async-start(f32[16,1,4096]{2,1,0:T(1,128)} %reshape.49), calls=%async_computation | async-start | bytes 524288 | tf_op jit(solution)/shard_map/all_to_all | solution.py:40
  16.7 148.1 %all-gather.3.cloned.1.call-start = ((), (), s32[]{:S(2)}) async-start(), calls=%async_computation.1 | async-start | bytes 8912896 | tf_op jit(solution)/shard_map/all_gather | solution.py:9
  29.0 62.5 %copy-start = (f32[256]{0:T(256)S(1)}, f32[256]{0:T(256)}, u32[]{:S(2)}) copy-start(f32[256]{0:T(256)} %param.15) | copy-start | bytes 3076
  29.0 63.7 %copy-start.1 = (s32[2]{0:T(128)S(1)}, s32[2]{0:T(128)}, u32[]{:S(2)}) copy-start(s32[2]{0:T(128)} %param.16) | copy-start | bytes 28
Sparse Core Ops, SparseCore 0:
  91.4 73.2 all-gather.2
where the time goes:
time: 244 us; the launch traced here: 243 us
  matrix products  104 us (43%)
  waiting for transfers between devices  74.1 us (30%)
  other arithmetic  21.8 us (9%)
  local copies, waits for them, and re-layouts  17.6 us (7%)
  between operations  14.2 us (6%)
  starting transfers between devices  6.37 us (3%)
  loops' own time  5.33 us (2%)
    dot_general x79, matrix products, chain_product(): jnp.einsum('uij,ujk->uik', earlier, later, precision=lax.Precision.HIGHEST)  82 us
    all_gather x1, waiting for transfers between devices, carried_in(): gathered = lax.all_gather(part, axis)  71.4 us
    dot_general x64, matrix products, advance(): v_new = jnp.dot(alpha, trans, precision=lax.Precision.HIGHEST) * factor  21.3 us
    div x79, other arithmetic, rescale(): return matrix / jnp.max(matrix, axis=(1, 2), keepdims=True)  8.92 us
    all_to_all x1, starting transfers between devices, shards(): lax.all_to_all(loglik, 'tm', split_axis=1, concat_axis=2, tiled=True)  6.33 us
    unnamed x9, local copies, waits for them, and re-layouts  5.28 us
    select_n x64, other arithmetic, advance(): fresh = jnp.where(alive[:, None], v_new / total, alpha)  5.19 us
  transfers between devices with their start and end apart: 2, of which 2 were waited for; matrix products, arithmetic and copies ran while one was open for 3% of the time, Pallas kernels for 0%

commit v1 on v0

v1 whole, which is shorter than its diff:
```python
import functools
import jax
import jax.numpy as jnp
from jax import lax
from jax.experimental import pallas as pl
from jax.experimental.pallas import tpu as pltpu
from jax.sharding import PartitionSpec as P

F32 = jnp.float32
BF16 = jnp.bfloat16
SUB = 8


def halves(x):
    high = x.astype(BF16)
    return high, (x - high.astype(F32)).astype(BF16)


def dot(a, b):
    return jnp.dot(a, b, preferred_element_type=F32)


def dot3(a_high, a_low, b_high, b_low):
    return dot(a_high, b_high) + dot(a_low, b_high) + dot(a_high, b_low)


def transfer_kernel(
    frames,
    lengths_ref,
    mask_ref,
    cols_ref,
    weight_ref,
    map_ref,
    chip_ref,
    pre_ref,
    e_ref,
    top_ref,
    th_ref,
    tl_ref,
    g_scr,
    e_scr,
    t_scr,
    ah,
    al,
    bh,
    bl,
):
    states = weight_ref.shape[0]
    half = frames // 2
    rows = states // 2
    blocks = half // SUB
    core = lax.axis_index("tm") % 2
    first_frame = (lax.axis_index("tm") // 2) * frames
    alive = lengths_ref[core] - first_frame

    nb = mask_ref.shape[0]
    width = states // nb
    lane = lax.broadcasted_iota(jnp.int32, (1, states), 1) // width
    for r in range(nb):
        row = jnp.zeros((1, states), F32)
        for c in range(nb):
            row = jnp.where(lane == c, mask_ref[r, c].astype(F32), row)
        part = weight_ref[r * width : (r + 1) * width, :] * row
        t_scr[r * width : (r + 1) * width, :] = part / jnp.sum(part, axis=1, keepdims=True)
    th, tl = halves(t_scr[...])
    th_ref[...] = th
    tl_ref[...] = tl

    cols = cols_ref[...].T
    pick = (lax.broadcasted_iota(jnp.int32, (cols.shape[1], states), 0) == map_ref[...]).astype(F32).astype(BF16)
    p1 = cols.astype(BF16)
    rest = cols - p1.astype(F32)
    p2, p3 = halves(rest)
    depth = 256
    pieces = cols.shape[1] // depth

    def gather(*accs):
        for k in range(pieces):
            cut = slice(k * depth, (k + 1) * depth)
            pltpu.matmul_push_rhs(pick[cut, :], 0, k % 2)
            pltpu.matmul_acc_lhs(accs[k % 2], p1[:, cut], 0)
            pltpu.matmul_acc_lhs(accs[k % 2], p2[:, cut], None)
            pltpu.matmul_acc_lhs(accs[k % 2], p3[:, cut], None)
        g_scr[...] = pltpu.matmul_pop(accs[0]) + pltpu.matmul_pop(accs[1])

    pl.run_scoped(gather, pltpu.ACC(0)((frames, states), F32), pltpu.ACC(1)((frames, states), F32))
    g = g_scr[...]
    top = jnp.max(g, axis=1, keepdims=True)
    e = jnp.exp(g - top)
    e_scr[...] = e
    for k in range(states // 128):
        e_ref[k] = e[:, k * 128 : (k + 1) * 128]
    top_ref[...] = jnp.broadcast_to(top, (frames, 128))

    eye = (
        lax.broadcasted_iota(jnp.int32, (states, states), 0) == lax.broadcasted_iota(jnp.int32, (states, states), 1)
    ).astype(F32)
    for mh, ml, off in ((ah, al, 0), (bh, bl, half)):
        h, l = halves(jnp.where(alive > off, t_scr[...] * e_scr[off : off + 1, :], eye))
        mh[0:states, :] = h
        ml[0:states, :] = l

    def body(a0, a1, b0, b1):
        accs = ((a0, a1), (b0, b1))
        mats = ((ah, al), (bh, bl))

        def issue_a(high_loaded):
            for m in range(2):
                sl = pl.ds(m * rows, rows)
                pltpu.matmul_acc_lhs(accs[0][m], ah[sl, :], high_loaded)
                pltpu.matmul_acc_lhs(accs[0][m], al[sl, :], None)
            for m in range(2):
                pltpu.matmul_push_rhs(tl_ref[...], 1, m)
            for m in range(2):
                pltpu.matmul_acc_lhs(accs[0][m], ah[pl.ds(m * rows, rows), :], 1)

        def issue_b():
            for m in range(2):
                pltpu.matmul_acc_lhs(accs[1][m], bh[pl.ds(m * rows, rows), :], None)
            for m in range(2):
                pltpu.matmul_push_rhs(th_ref[...], 0, m)
            for m in range(2):
                sl = pl.ds(m * rows, rows)
                pltpu.matmul_acc_lhs(accs[1][m], bh[sl, :], 0)
                pltpu.matmul_acc_lhs(accs[1][m], bl[sl, :], None)

        def post(k, s, peak):
            mh, ml = mats[k]
            frame = s + k * half
            er = e_scr[pl.ds(frame, 1), :] * (1.0 / jnp.max(peak.astype(F32), keepdims=True)[:, :1])
            base = jnp.where(frame < alive, 0, states)
            new = None
            for m in range(2):
                x = pltpu.matmul_pop(accs[k][m]) * er
                h, l = halves(x)
                at = pl.multiple_of(base + m * rows, rows)
                mh[pl.ds(at, rows), :] = h
                ml[pl.ds(at, rows), :] = l
                y = jnp.max(h.reshape(rows // 16, 16, states), axis=0)
                new = y if new is None else jnp.maximum(new, y)
            return new

        def keep(j):
            for k in range(2):
                for i in range(2):
                    pre_ref[k, j, i] = mats[k][i][0:states, :]

        for m in range(2):
            pltpu.matmul_push_rhs(th_ref[...], 0, m)
        issue_a(0)
        one = jnp.ones((16, states), BF16)

        def step(s, peaks, last=False):
            pa, pb = peaks
            issue_b()
            pa = post(0, s, pa)
            if not last:
                issue_a(None)
            pb = post(1, s, pb)
            return pa, pb

        def block(j, peaks):
            for r in range(1, SUB):
                peaks = step(j * SUB + r, peaks)
            keep(j)
            return step(j * SUB + SUB, peaks)

        peaks = lax.fori_loop(0, blocks - 1, block, (one, one))
        for r in range(1, SUB):
            peaks = step((blocks - 1) * SUB + r, peaks, r == SUB - 1)
        keep(blocks - 1)
        for m in range(2):
            sl = pl.ds(m * rows, rows)
            pltpu.matmul_push_rhs(bh[0:states, :], 0, m)
            pltpu.matmul_acc_lhs(accs[0][m], ah[sl, :], 0)
            pltpu.matmul_acc_lhs(accs[0][m], al[sl, :], None)
            pltpu.matmul_push_rhs(bl[0:states, :], 1, m)
            pltpu.matmul_acc_lhs(accs[0][m], ah[sl, :], 1)
        c = jnp.concatenate([pltpu.matmul_pop(accs[0][m]) for m in range(2)], axis=0)
        chip_ref[...] = c * (1.0 / jnp.max(c, keepdims=True)[:, :1])

    shape = (rows, states)
    pl.run_scoped(
        body,
        pltpu.ACC(0)(shape, F32),
        pltpu.ACC(1)(shape, F32),
        pltpu.ACC(0)(shape, F32),
        pltpu.ACC(1)(shape, F32),
    )


def vmem():
    return pl.BlockSpec(memory_space=pltpu.VMEM)


def smem():
    return pl.BlockSpec(memory_space=pltpu.SMEM)


def transfer(cols, weight, mask, lengths, pdf_map):
    columns, frames = cols.shape
    states = weight.shape[0]
    blocks = frames // 2 // SUB
    out = jax.ShapeDtypeStruct
    return pl.pallas_call(
        functools.partial(transfer_kernel, frames),
        out_shape=(
            out((states, states), F32),
            out((2, blocks, 2, states, states), BF16),
            out((states // 128, frames, 128), F32),
            out((frames, 128), F32),
            out((states, states), BF16),
            out((states, states), BF16),
        ),
        in_specs=[smem(), smem(), vmem(), vmem(), vmem()],
        out_specs=[vmem()] * 6,
        scratch_shapes=[pltpu.VMEM((frames, states), F32)] * 2
        + [pltpu.VMEM((states, states), F32)]
        + [pltpu.VMEM((2 * states, states), BF16)] * 4,
        compiler_params=pltpu.CompilerParams(vmem_limit_bytes=40 << 20),
        name="transfer",
    )(lengths, mask, cols, weight, pdf_map[None, :])


def row_dot(v, matrix_high, matrix_low):
    n = v.shape[0]
    vh, vl = halves(v)
    both = jnp.concatenate([vh, vl], axis=0)
    x = dot(both, matrix_high)
    return x[0:n] + x[n:] + dot(vh, matrix_low)


def unit(v):
    return v / jnp.sum(v, axis=1, keepdims=True)


def plane_kernel(own_ref, other_ref, init_ref, dh_ref, dl_ref, v_ref):
    chip = lax.axis_index("tm") // 2
    plane = chip // 2

    def product(left, right):
        d = dot3(*halves(left[...]), *halves(right[...]))
        h, l = halves(d * (1.0 / jnp.max(d, keepdims=True)[:, :1]))
        dh_ref[...] = h
        dl_ref[...] = l

    @pl.when(chip % 2 == 0)
    def _():
        product(own_ref, other_ref)

    @pl.when(chip % 2 == 1)
    def _():
        product(other_ref, own_ref)

    start = jnp.broadcast_to(unit(init_ref[...]), v_ref.shape)
    v_ref[...] = unit(row_dot(start, dh_ref[...], dl_ref[...]))


def plane_product(own, other, init):
    states = own.shape[0]
    out = jax.ShapeDtypeStruct
    return pl.pallas_call(
        plane_kernel,
        out_shape=(out((states, states), BF16), out((states, states), BF16), out((8, states), F32)),
        in_specs=[vmem()] * 3,
        out_specs=[vmem()] * 3,
        name="plane",
    )(own, other, init[None, :])


def hop_kernel(v_ref, dh_ref, dl_ref, out_ref):
    out_ref[...] = unit(row_dot(v_ref[...], dh_ref[...], dl_ref[...]))


def hop(v, dh, dl):
    return pl.pallas_call(
        hop_kernel,
        out_shape=jax.ShapeDtypeStruct(v.shape, F32),
        in_specs=[vmem()] * 3,
        out_specs=vmem(),
        name="hop",
    )(v, dh, dl)


def frames_kernel(
    frames,
    planes,
    lengths_ref,
    *refs,
):
    v_refs = refs[: planes - 1]
    init_ref, other_ref, pre_ref, e_ref, top_ref, th_ref, tl_ref, kept_ref, sent_ref, gain_ref, alpha_scr = refs[
        planes - 1 :
    ]
    states = th_ref.shape[0]
    half = frames // 2
    blocks = half // SUB
    subs = 2 * blocks
    index = lax.axis_index("tm")
    core = index % 2
    chip = index // 2
    alive = lengths_ref[core] - chip * frames

    v = jnp.broadcast_to(unit(init_ref[...]), (8, states))
    for g in range(1, planes):
        v = jnp.where(chip // 2 == g, v_refs[g - 1][...], v)
    oh, ol = halves(other_ref[...])
    v = jnp.where(chip % 2 == 1, unit(row_dot(v, oh, ol)), v)
    mid = unit(row_dot(v, pre_ref[0, blocks - 1, 0], pre_ref[0, blocks - 1, 1]))
    rows = [v[0:1]]
    for j in range(blocks - 1):
        rows.append(row_dot(v, pre_ref[0, j, 0], pre_ref[0, j, 1])[0:1])
    rows.append(mid[0:1])
    for j in range(blocks - 1):
        rows.append(row_dot(mid, pre_ref[1, j, 0], pre_ref[1, j, 1])[0:1])
    alpha = unit(jnp.concatenate(rows, axis=0))
    th, tl = th_ref[...], tl_ref[...]
    lane = lax.broadcasted_iota(jnp.int32, (subs, 128), 1)
    sub = lax.broadcasted_iota(jnp.int32, (subs, 128), 0)
    gains = jnp.zeros((subs, 128), F32)
    tiles = range(states // 128)
    for r in range(SUB):
        every = pl.ds(r, subs, stride=SUB)
        x = row_dot(alpha, th, tl) * jnp.concatenate([e_ref[k, every, :] for k in tiles], axis=1)
        total = jnp.sum(x, axis=1, keepdims=True)
        alpha = x / total
        for k in tiles:
            alpha_scr[k, every, :] = alpha[:, k * 128 : (k + 1) * 128]
        live = sub * SUB + r < alive
        gain = jnp.where(live, jnp.log(total) + top_ref[every, :], 0.0)
        gains = jnp.where(lane % SUB == r, gain, gains)
    end = pl.ds(jnp.clip(alive - 1, 0, frames - 1), 1)
    for which, ref in ((core, kept_ref), (1 - core, sent_ref)):
        at = pl.multiple_of(which * half, half)
        frame = at + lax.broadcasted_iota(jnp.int32, (half, 128), 0)
        for k in tiles:
            cut = slice(k * 128, (k + 1) * 128)
            final = jnp.where(alive > 0, alpha_scr[k, end, :], v[0:1, cut])
            ref[0:half, cut] = jnp.log(jnp.where(frame < alive, alpha_scr[k, pl.ds(at, half), :], final))
    picked = jnp.where(lane // SUB == sub % blocks, gains, 0.0)
    lines = [jnp.sum(picked[k * blocks : (k + 1) * blocks], axis=0, keepdims=True) for k in range(2)]
    gain_ref[...] = jnp.where(core == 0, lines[0], lines[1])
    line = jnp.where(core == 0, lines[1], lines[0])
    sent_ref[half : half + 8, :] = jnp.concatenate([jnp.broadcast_to(line, (8, 128))] * (states // 128), axis=1)


def frames_pass(lengths, vs, init, other, pre, e, top, th, tl):
    frames, states = top.shape[0], th.shape[0]
    half = frames // 2
    out = jax.ShapeDtypeStruct
    return pl.pallas_call(
        functools.partial(frames_kernel, frames, len(vs) + 1),
        out_shape=(out((half, states), F32), out((half + 8, states), F32), out((1, 128), F32)),
        in_specs=[smem()] + [vmem()] * (len(vs) + 7),
        out_specs=[vmem()] * 3,
        scratch_shapes=[pltpu.VMEM((states // 128, frames, 128), F32)],
        compiler_params=pltpu.CompilerParams(vmem_limit_bytes=40 << 20),
        name="frames",
    )(lengths, *vs, init[None, :], other, pre, e, top, th, tl)


def join_kernel(kept_ref, gain_ref, got_ref, log_ref, out_gain_ref):
    half = kept_ref.shape[0]
    core = lax.axis_index("tm") % 2
    log_ref[core] = kept_ref[...]
    log_ref[1 - core] = got_ref[0:half, :]
    own = gain_ref[0:1, 0:half]
    got = got_ref[half : half + 1, 0:half]
    out_gain_ref[0:1, :] = jnp.where(core == 0, own, got)
    out_gain_ref[1:2, :] = jnp.where(core == 0, got, own)


def join(kept, gain, got):
    half, states = kept.shape
    out = jax.ShapeDtypeStruct
    return pl.pallas_call(
        join_kernel,
        out_shape=(out((2, half, states), F32), out((2, half), F32)),
        in_specs=[vmem()] * 3,
        out_specs=[vmem()] * 2,
        name="join",
    )(kept, gain, got)


def shards(size, loglik, trans_weight, block_mask, init_weight, lengths, pdf_map):
    utts, total, local = loglik.shape
    chips = size // 2
    frames = total // chips
    planes = chips // 2
    x = jnp.transpose(loglik, (0, 2, 1)).reshape(utts, local, chips, frames)
    x = jnp.transpose(x, (2, 0, 1, 3)).reshape(size, local, frames)
    cols = lax.all_to_all(x, "tm", 0, 0, tiled=True).reshape(size * local, frames)
    chip, pre, e, top, th, tl = transfer(cols, trans_weight, block_mask, lengths, pdf_map)
    other = lax.ppermute(chip, "tm", [(i, i ^ 2) for i in range(size)])
    dh, dl, v = plane_product(chip, other, init_weight)
    vs = []
    for g in range(1, planes):
        got = lax.ppermute(v, "tm", [(4 * (g - 1) + i, 4 * g + i) for i in range(4)])
        vs.append(got)
        if g < planes - 1:
            v = hop(got, dh, dl)
    kept, sent, gain = frames_pass(lengths, vs, init_weight, other, pre, e, top, th, tl)
    got = lax.ppermute(sent, "tm", [(i, i ^ 1) for i in range(size)])
    return join(kept, gain, got)


def solution(mesh):
    return jax.shard_map(
        functools.partial(shards, mesh.shape["tm"]),
        mesh=mesh,
        in_specs=(P("groups", None, "tm"), P(), P(), P(), P("groups"), P()),
        out_specs=(P("groups", "tm", None), P("groups", "tm")),
        check_vma=False,
    )
```

time: 244 us -> 85.1 us (0.35)
  the two profiles are of different devices: /device:TPU:29 before, /device:TPU:27 now
where the time goes in v1:
time: 85.1 us; the launch traced here: 84.5 us
  Pallas kernels  30.6 us (36%)
  waiting for transfers between devices  17.1 us (20%)
  local copies, waits for them, and re-layouts  15.5 us (18%)
  blocking collectives  13.7 us (16%)
  starting transfers between devices  6.86 us (8%)
    pallas_call x1, Pallas kernels, transfer(): pl.pallas_call(functools.partial(transfer_kernel, frames), out_shape=(out...  19.6 us
    unnamed x37, local copies, waits for them, and re-layouts  15.4 us
    all_to_all x1, blocking collectives, shards(): lax.all_to_all(x, 'tm', 0, 0, tiled=True).reshape(size * local, frames)  13.7 us
    ppermute x3, waiting for transfers between devices, shards(): lax.ppermute(v, 'tm', [(4 * (g - 1) + i, 4 * g + i) for i in range(4)])  9.19 us
    ppermute x1, waiting for transfers between devices, shards(): other = lax.ppermute(chip, 'tm', [(i, i ^ 2) for i in range(size)])  6.96 us
    pallas_call x2, Pallas kernels, hop(): pl.pallas_call(hop_kernel, out_shape=jax.ShapeDtypeStruct(v.shape, F32),...  3.62 us
    ppermute x1, starting transfers between devices, shards(): got = lax.ppermute(sent, 'tm', [(i, i ^ 1) for i in range(size)])  3.56 us
    pallas_call x1, Pallas kernels, frames_pass(): pl.pallas_call(functools.partial(frames_kernel, frames, len(vs) + 1), out...  3.42 us
  transfers between devices with their start and end apart: 5, of which 3 were waited for; matrix products, arithmetic and copies ran while one was open for 0% of the time, Pallas kernels for 0%

profile of v1, /device:TPU:27, one launch (start us, length us, event | category | flops | bytes accessed | tf_op | source)
XLA Modules:
  0.0 84.5 jit_solution(1489716651164910146)
XLA Ops:
  0.6 1.0 %copy.9 = f32[8,8,8,128]{3,2,1,0:T(8,128)S(1)} copy(f32[8,8,8,128]{3,1,2,0:T(8,128)} %bitcast.19) | data formatting | bytes 524288
  1.7 0.1 copy.8
  1.7 13.7 %all_to_all.5 = f32[16,32,128]{2,1,0:T(8,128)S(1)} all-to-all(f32[16,32,128]{2,1,0:T(8,128)S(1)} %bitcast.17), channel_id=1, replica_groups=mesh['groups'=2,'tm'=16] {'tm'}, dimensions={0} | all-to-all | bytes 524288 | tf_op jit(solution)/shard_map/all_to_all | solution.py:392
  15.4 0.0 copy-start.4
  15.4 0.9 %copy-done.4 = f32[256,256]{1,0:T(8,128)S(1)} copy-done((f32[256,256]{1,0:T(8,128)S(1)}, f32[256,256]{1,0:T(8,128)}, u32[]{:S(2)}) %copy-start.4) | copy-done | bytes 262168
  16.4 0.0 copy-start.12
  16.4 0.7 copy-done.12
  17.0 0.7 copy-done.13
  17.7 0.0 copy-start.15
  17.7 0.7 copy-done.15
  18.4 19.6 %transfer.1 = (f32[256,256]{1,0:T(8,128)S(1)}, bf16[2,8,2,256,256]{4,3,2,1,0:T(8,128)(2,1)S(1)}, f32[2,128,128]{2,1,0:T(8,128)S(1)}, f32[128,128]{1,0:T(8,128)S(...) custom-call(s32[2]{0:T(128)S(1)} %copy-done.13, s32[4,4]{1,0:T(4,128)S(1)} %copy-done.12, ...), custom_call_target="tpu_custom_call" | custom-call | tf_op jit(solution)/shard_map/transfer/pallas_call | solution.py:205
  38.0 0.0 copy-start
  38.0 1.9 %copy-done = bf16[2,8,2,256,256]{4,3,2,1,0:T(8,128)(2,1)} copy-done((bf16[2,8,2,256,256]{4,3,2,1,0:T(8,128)(2,1)}, bf16[2,8,2,256,256]{4,3,2,1,0:T(8,128)(2,1)S(1)}, u32[]{:S(2)}) %copy-start) | copy-done | bytes 4194328
  40.0 0.0 copy-start.5
  40.0 0.7 collective-permute-start
  40.7 7.0 %collective-permute-done.other_ref.refs_4_ = f32[256,256]{1,0:T(8,128)S(1)} collective-permute-done((f32[256,256]{1,0:T(8,128)S(1)}, f32[256,256]{1,0:T(8,128)S(1)}, u32[]{:S(2)}, u32[]{:S(2)}) %collective-permute-start) | collective-permute-done | bytes 262176 | tf_op jit(solution)/shard_map/ppermute | solution.py:394
  47.6 0.0 copy-start.2
  47.6 0.0 copy-done.5
  47.6 0.7 copy-done.2
  48.4 2.4 %plane.1 = (bf16[256,256]{1,0:T(8,128)(2,1)}, bf16[256,256]{1,0:T(8,128)(2,1)}, f32[8,256]{1,0:T(8,128)}) custom-call(f32[256,256]{1,0:T(8,128)} %copy-done.5, f32[256,256]{1,0:T(8,128)} %copy-done.2, f32[1,256]{1,0:T(1,128)} %bitcast.14), custom_call_target="tpu_custom_call" | custom-call | tf_op jit(solution)/shard_map/plane/pallas_call | solution.py:262
  50.7 0.6 collective-permute-start.1
  51.4 0.0 collective-permute-done.1.v_ref.refs_0_
  51.4 0.0 copy-start.7
  51.4 0.6 copy-done.7
  52.0 1.8 %hop.2 = f32[8,256]{1,0:T(8,128)} custom-call(f32[8,256]{1,0:T(8,128)} %copy-done.7, bf16[256,256]{1,0:T(8,128)(2,1)} %get-tuple-element.16.dh_ref, bf16[256,256]{1,0:T(8,128)(2,1)} %get-tuple-element.17.dl_ref), custom_call_target="tpu_custom_call" | custom-call | tf_op jit(solution)/shard_map/hop/pallas_call | solution.py:276
  53.8 0.6 collective-permute-start.2
  54.4 0.0 collective-permute-done.2.v_ref.refs_1_
  54.5 0.0 copy-start.9
  54.5 0.6 copy-done.9
  55.1 1.8 %hop.3 = f32[8,256]{1,0:T(8,128)} custom-call(f32[8,256]{1,0:T(8,128)} %copy-done.9, bf16[256,256]{1,0:T(8,128)(2,1)} %get-tuple-element.16.dh_ref, bf16[256,256]{1,0:T(8,128)(2,1)} %get-tuple-element.17.dl_ref), custom_call_target="tpu_custom_call" | custom-call | tf_op jit(solution)/shard_map/hop/pallas_call | solution.py:276
  56.9 1.3 %collective-permute-start.3 = (f32[8,256]{1,0:T(8,128)}, f32[8,256]{1,0:T(8,128)S(1)}, u32[]{:S(2)}, u32[]{:S(2)}) collective-permute-start(f32[8,256]{1,0:T(8,128)} %hop.3), channel_id=1, source_target_pairs={{8,12},{9,13},{10,14},{11,15},{24,28},{25,29},{26,30},{27,31}} | collective-permute-start | bytes 24584 | tf_op jit(solution)/shard_map/ppermute | solution.py:398
  58.2 9.2 %collective-permute-done.3.refs_2_ = f32[8,256]{1,0:T(8,128)S(1)} collective-permute-done((f32[8,256]{1,0:T(8,128)}, f32[8,256]{1,0:T(8,128)S(1)}, u32[]{:S(2)}, u32[]{:S(2)}) %collective-permute-start.3) | collective-permute-done | bytes 8224 | tf_op jit(solution)/shard_map/ppermute | solution.py:398
  67.3 2.2 %copy-done.1 = bf16[2,8,2,256,256]{4,3,2,1,0:T(8,128)(2,1)S(1)} copy-done((bf16[2,8,2,256,256]{4,3,2,1,0:T(8,128)(2,1)S(1)}, bf16[2,8,2,256,256]{4,3,2,1,0:T(8,128)(2,1)}, u32[]{:S(2)}) %copy-start.1) | copy-done | bytes 4194328
  69.5 0.0 copy-start.3
  69.5 0.9 %copy-done.3 = f32[256,256]{1,0:T(8,128)S(1)} copy-done((f32[256,256]{1,0:T(8,128)S(1)}, f32[256,256]{1,0:T(8,128)}, u32[]{:S(2)}) %copy-start.3) | copy-done | bytes 262168
  70.5 0.0 copy-start.8
  70.5 0.7 copy-done.8
  71.2 0.7 copy-done.10
  71.9 0.7 copy-done.11
  72.6 0.7 copy-done.14
  73.2 3.4 %frames.1 = (f32[64,256]{1,0:T(8,128)S(1)}, f32[72,256]{1,0:T(8,128)S(1)}, f32[1,128]{1,0:T(1,128)S(1)}) custom-call(s32[2]{0:T(128)S(1)} %copy-done.14, f32[8,256]{1,0:T(8,128)S(1)} %copy-done.8, f32[8,256]{1,0:T(8,128)S(1)} %copy-done.10, f32[8,256]{1,0:T(8,128)S(1)} %collective-permute-done.3.refs_2_, f32[1,256]{1,0:T(1,128)S(1)} %bitcast.15, ...), custom_call_target="tpu_custom_call" | custom-call | tf_op jit(solution)/shard_map/frames/pallas_call | solution.py:351
  76.6 0.0 copy-start.6
  76.6 0.6 copy-done.6
  77.3 0.5 copy-done.16
  77.8 3.6 %collective-permute-start.4 = (f32[72,256]{1,0:T(8,128)S(1)}, f32[72,256]{1,0:T(8,128)S(1)}, u32[]{:S(2)}, u32[]{:S(2)}) collective-permute-start(f32[72,256]{1,0:T(8,128)S(1)} %get-tuple-element.25), channel_id=1, source_target_pairs={{0,1},{1,0},{2,3},{3,2},{4,5},{5,4},{6,7},{7,6},{8,9},{9,8},{10,11... | collective-permute-start | bytes 221192 | tf_op jit(solution)/shard_map/ppermute | solution.py:403
  81.4 0.9 %collective-permute-done.4.got_ref = f32[72,256]{1,0:T(8,128)S(1)} collective-permute-done((f32[72,256]{1,0:T(8,128)S(1)}, f32[72,256]{1,0:T(8,128)S(1)}, u32[]{:S(2)}, u32[]{:S(2)}) %collective-permute-start.4) | collective-permute-done | bytes 73760 | tf_op jit(solution)/shard_map/ppermute | solution.py:403
  82.3 0.6 copy-done.17
  82.9 1.6 %join.1 = (f32[2,64,256]{2,1,0:T(8,128)}, f32[2,64]{1,0:T(2,128)}) custom-call(f32[64,256]{1,0:T(8,128)} %copy-done.6, f32[1,128]{1,0:T(1,128)} %copy-done.16, f32[72,256]{1,0:T(8,128)} %copy-done.17), custom_call_target="tpu_custom_call" | custom-call | tf_op jit(solution)/shard_map/join/pallas_call | solution.py:376
  (8 shorter events, 0.0 us)
Async XLA Ops:
  15.4 1.0 %copy-start.4 = (f32[256,256]{1,0:T(8,128)S(1)}, f32[256,256]{1,0:T(8,128)}, u32[]{:S(2)}) copy-start(f32[256,256]{1,0:T(8,128)} %weight_ref.1) | copy-start | bytes 786436
  16.4 0.7 copy-start.12
  17.0 0.7 copy-start.13
  17.7 0.7 copy-start.15
  38.0 1.9 %copy-start = (bf16[2,8,2,256,256]{4,3,2,1,0:T(8,128)(2,1)}, bf16[2,8,2,256,256]{4,3,2,1,0:T(8,128)(2,1)S(1)}, u32[]{:S(2)}) copy-start(bf16[2,8,2,256,256]{4,3,2,1,0:T(8,128)(2,1)S(1)} %get-tuple-element.18.refs_5_) | copy-start | bytes 12582916
  40.0 7.7 %copy-start.5 = (f32[256,256]{1,0:T(8,128)}, f32[256,256]{1,0:T(8,128)S(1)}, u32[]{:S(2)}) copy-start(f32[256,256]{1,0:T(8,128)S(1)} %get-tuple-element.14.own_ref) | copy-start | bytes 786436
  40.0 7.7 %collective-permute-start = (f32[256,256]{1,0:T(8,128)S(1)}, f32[256,256]{1,0:T(8,128)S(1)}, u32[]{:S(2)}, u32[]{:S(2)}) collective-permute-start(f32[256,256]{1,0:T(8,128)S(1)} %get-tuple-element.14.own_ref), channel_id=1, source_target_pairs={{0,2},{1,3},{2,0},{3,1},{4,6},{5,7},{6,4},{7,5},{8,10},{9,11},{10,... | collective-permute-start | bytes 786440 | tf_op jit(solution)/shard_map/ppermute | solution.py:394
  47.6 0.7 copy-start.2
  50.7 0.7 collective-permute-start.1
  51.4 0.6 copy-start.7
  53.8 0.7 collective-permute-start.2
  54.5 0.6 copy-start.9
  56.9 10.5 %collective-permute-start.3 = (f32[8,256]{1,0:T(8,128)}, f32[8,256]{1,0:T(8,128)S(1)}, u32[]{:S(2)}, u32[]{:S(2)}) collective-permute-start(f32[8,256]{1,0:T(8,128)} %hop.3), channel_id=1, source_target_pairs={{8,12},{9,13},{10,14},{11,15},{24,28},{25,29},{26,30},{27,31}} | collective-permute-start | bytes 24584 | tf_op jit(solution)/shard_map/ppermute | solution.py:398
  67.3 2.2 %copy-start.1 = (bf16[2,8,2,256,256]{4,3,2,1,0:T(8,128)(2,1)S(1)}, bf16[2,8,2,256,256]{4,3,2,1,0:T(8,128)(2,1)}, u32[]{:S(2)}) copy-start(bf16[2,8,2,256,256]{4,3,2,1,0:T(8,128)(2,1)} %copy-done) | copy-start | bytes 12582916
  69.5 0.9 %copy-start.3 = (f32[256,256]{1,0:T(8,128)S(1)}, f32[256,256]{1,0:T(8,128)}, u32[]{:S(2)}) copy-start(f32[256,256]{1,0:T(8,128)} %copy-done.2) | copy-start | bytes 786436
  70.5 0.7 copy-start.8
  71.2 0.7 copy-start.10
  71.9 0.7 copy-start.11
  72.6 0.7 copy-start.14
  76.6 0.6 copy-start.6
  77.3 0.5 copy-start.16
  77.8 4.5 %collective-permute-start.4 = (f32[72,256]{1,0:T(8,128)S(1)}, f32[72,256]{1,0:T(8,128)S(1)}, u32[]{:S(2)}, u32[]{:S(2)}) collective-permute-start(f32[72,256]{1,0:T(8,128)S(1)} %get-tuple-element.25), channel_id=1, source_target_pairs={{0,1},{1,0},{2,3},{3,2},{4,5},{5,4},{6,7},{7,6},{8,9},{9,8},{10,11... | collective-permute-start | bytes 221192 | tf_op jit(solution)/shard_map/ppermute | solution.py:403
  82.3 0.6 copy-start.17

commit v2 on v1

--- a/solution.py
+++ b/solution.py
@@ -26,11 +26,11 @@
 
 def transfer_kernel(
     frames,
-    lengths_ref,
-    mask_ref,
+    lengths_hbm,
+    mask_hbm,
+    weight_hbm,
+    map_hbm,
     cols_ref,
-    weight_ref,
-    map_ref,
     chip_ref,
     pre_ref,
     e_ref,
@@ -44,13 +44,60 @@
     al,
     bh,
     bl,
+    lengths_ref,
+    mask_ref,
+    weight_ref,
+    map_ref,
+    sems,
 ):
+    copies = [
+        pltpu.make_async_copy(src, dst, sems.at[i])
+        for i, (src, dst) in enumerate(
+            (
+                (map_hbm, map_ref),
+                (weight_hbm, weight_ref),
+                (mask_hbm, mask_ref),
+                (lengths_hbm, lengths_ref),
+            )
+        )
+    ]
+    for copy in copies:
+        copy.start()
     states = weight_ref.shape[0]
     half = frames // 2
     rows = states // 2
     blocks = half // SUB
     core = lax.axis_index("tm") % 2
     first_frame = (lax.axis_index("tm") // 2) * frames
+    cols = cols_ref[...].T
+    copies[0].wait()
+    pick = (lax.broadcasted_iota(jnp.int32, (cols.shape[1], states), 0) == map_ref[...]).astype(F32).astype(BF16)
+    p1 = cols.astype(BF16)
+    rest = cols - p1.astype(F32)
+    p2, p3 = halves(rest)
+    depth = 256
+    pieces = cols.shape[1] // depth
+
+    def gather(*accs):
+        for k in range(pieces):
+            cut = slice(k * depth, (k + 1) * depth)
+            pltpu.matmul_push_rhs(pick[cut, :], 0, k % 2)
+            pltpu.matmul_acc_lhs(accs[k % 2], p1[:, cut], 0)
+            pltpu.matmul_acc_lhs(accs[k % 2], p2[:, cut], None)
+            pltpu.matmul_acc_lhs(accs[k % 2], p3[:, cut], None)
+        g_scr[...] = pltpu.matmul_pop(accs[0]) + pltpu.matmul_pop(accs[1])
+
+    pl.run_scoped(gather, pltpu.ACC(0)((frames, states), F32), pltpu.ACC(1)((frames, states), F32))
+    g = g_scr[...]
+    top = jnp.max(g, axis=1, keepdims=True)
+    e = jnp.exp(g - top)
+    e_scr[...] = e
+    for k in range(states // 128):
+        e_ref[k] = e[:, k * 128 : (k + 1) * 128]
+    top_ref[...] = jnp.broadcast_to(top, (frames, 128))
+
+    for copy in copies[1:]:
+        copy.wait()
     alive = lengths_ref[core] - first_frame
 
     nb = mask_ref.shape[0]
@@ -65,32 +112,6 @@
     th, tl = halves(t_scr[...])
     th_ref[...] = th
     tl_ref[...] = tl
-
-    cols = cols_ref[...].T
-    pick = (lax.broadcasted_iota(jnp.int32, (cols.shape[1], states), 0) == map_ref[...]).astype(F32).astype(BF16)
-    p1 = cols.astype(BF16)
-    rest = cols - p1.astype(F32)
-    p2, p3 = halves(rest)
-    depth = 256
-    pieces = cols.shape[1] // depth
-
-    def gather(*accs):
-        for k in range(pieces):
-            cut = slice(k * depth, (k + 1) * depth)
-            pltpu.matmul_push_rhs(pick[cut, :], 0, k % 2)
-            pltpu.matmul_acc_lhs(accs[k % 2], p1[:, cut], 0)
-            pltpu.matmul_acc_lhs(accs[k % 2], p2[:, cut], None)
-            pltpu.matmul_acc_lhs(accs[k % 2], p3[:, cut], None)
-        g_scr[...] = pltpu.matmul_pop(accs[0]) + pltpu.matmul_pop(accs[1])
-
-    pl.run_scoped(gather, pltpu.ACC(0)((frames, states), F32), pltpu.ACC(1)((frames, states), F32))
-    g = g_scr[...]
-    top = jnp.max(g, axis=1, keepdims=True)
-    e = jnp.exp(g - top)
-    e_scr[...] = e
-    for k in range(states // 128):
-        e_ref[k] = e[:, k * 128 : (k + 1) * 128]
-    top_ref[...] = jnp.broadcast_to(top, (frames, 128))
 
     eye = (
         lax.broadcasted_iota(jnp.int32, (states, states), 0) == lax.broadcasted_iota(jnp.int32, (states, states), 1)
@@ -193,8 +214,12 @@
     return pl.BlockSpec(memory_space=pltpu.VMEM)
 
 
-def smem():
-    return pl.BlockSpec(memory_space=pltpu.SMEM)
+def hbm():
+    return pl.BlockSpec(memory_space=pltpu.MemorySpace.HBM)
+
+
+def pinned(x):
+    return pltpu.with_memory_space_constraint(x, pltpu.MemorySpace.HBM)
 
 
 def transfer(cols, weight, mask, lengths, pdf_map):
@@ -212,14 +237,21 @@
             out((states, states), BF16),
             out((states, states), BF16),
         ),
-        in_specs=[smem(), smem(), vmem(), vmem(), vmem()],
+        in_specs=[hbm()] * 4 + [vmem()],
         out_specs=[vmem()] * 6,
         scratch_shapes=[pltpu.VMEM((frames, states), F32)] * 2
         + [pltpu.VMEM((states, states), F32)]
-        + [pltpu.VMEM((2 * states, states), BF16)] * 4,
-        compiler_params=pltpu.CompilerParams(vmem_limit_bytes=40 << 20),
+        + [pltpu.VMEM((2 * states, states), BF16)] * 4
+        + [
+            pltpu.SMEM(lengths.shape, jnp.int32),
+            pltpu.SMEM(mask.shape, jnp.int32),
+            pltpu.VMEM(weight.shape, F32),
+            pltpu.VMEM((1, states), jnp.int32),
+            pltpu.SemaphoreType.DMA((4,)),
+        ],
+        compiler_params=pltpu.CompilerParams(vmem_limit_bytes=6 << 20),
         name="transfer",
-    )(lengths, mask, cols, weight, pdf_map[None, :])
+    )(*map(pinned, (lengths, mask, weight, pdf_map[None, :])), cols)
 
 
 def row_dot(v, matrix_high, matrix_low):
@@ -234,7 +266,9 @@
     return v / jnp.sum(v, axis=1, keepdims=True)
 
 
-def plane_kernel(own_ref, other_ref, init_ref, dh_ref, dl_ref, v_ref):
+def plane_kernel(init_hbm, own_ref, other_ref, dh_ref, dl_ref, v_ref, start_ref, init_ref, sem):
+    copy = pltpu.make_async_copy(init_hbm, init_ref, sem)
+    copy.start()
     chip = lax.axis_index("tm") // 2
     plane = chip // 2
 
@@ -252,7 +286,9 @@
     def _():
         product(other_ref, own_ref)
 
+    copy.wait()
     start = jnp.broadcast_to(unit(init_ref[...]), v_ref.shape)
+    start_ref[...] = start
     v_ref[...] = unit(row_dot(start, dh_ref[...], dl_ref[...]))
 
 
@@ -261,11 +297,13 @@
     out = jax.ShapeDtypeStruct
     return pl.pallas_call(
         plane_kernel,
-        out_shape=(out((states, states), BF16), out((states, states), BF16), out((8, states), F32)),
-        in_specs=[vmem()] * 3,
-        out_specs=[vmem()] * 3,
+        out_shape=(out((states, states), BF16),) * 2 + (out((8, states), F32),) * 2,
+        in_specs=[hbm()] + [vmem()] * 2,
+        out_specs=[vmem()] * 4,
+        scratch_shapes=[pltpu.VMEM((1, states), F32), pltpu.SemaphoreType.DMA],
+        compiler_params=pltpu.CompilerParams(vmem_limit_bytes=4 << 20),
         name="plane",
-    )(own, other, init[None, :])
+    )(pinned(init[None, :]), own, other)
 
 
 def hop_kernel(v_ref, dh_ref, dl_ref, out_ref):
@@ -278,6 +316,7 @@
         out_shape=jax.ShapeDtypeStruct(v.shape, F32),
         in_specs=[vmem()] * 3,
         out_specs=vmem(),
+        compiler_params=pltpu.CompilerParams(vmem_limit_bytes=4 << 20),
         name="hop",
     )(v, dh, dl)
 
@@ -285,13 +324,16 @@
 def frames_kernel(
     frames,
     planes,
-    lengths_ref,
+    lengths_hbm,
     *refs,
 ):
     v_refs = refs[: planes - 1]
-    init_ref, other_ref, pre_ref, e_ref, top_ref, th_ref, tl_ref, kept_ref, sent_ref, gain_ref, alpha_scr = refs[
+    start_ref, other_ref, pre_ref, e_ref, top_ref, th_ref, tl_ref, kept_ref, sent_ref, gain_ref, *scratch = refs[
         planes - 1 :
     ]
+    alpha_scr, lengths_ref, sem = scratch
+    copy = pltpu.make_async_copy(lengths_hbm, lengths_ref, sem)
+    copy.start()
     states = th_ref.shape[0]
     half = frames // 2
     blocks = half // SUB
@@ -299,9 +341,7 @@
     index = lax.axis_index("tm")
     core = index % 2
     chip = index // 2
-    alive = lengths_ref[core] - chip * frames
-
-    v = jnp.broadcast_to(unit(init_ref[...]), (8, states))
+    v = start_ref[...]
     for g in range(1, planes):
         v = jnp.where(chip // 2 == g, v_refs[g - 1][...], v)
     oh, ol = halves(other_ref[...])
@@ -318,6 +358,8 @@
     lane = lax.broadcasted_iota(jnp.int32, (subs, 128), 1)
     sub = lax.broadcasted_iota(jnp.int32, (subs, 128), 0)
     gains = jnp.zeros((subs, 128), F32)
+    copy.wait()
+    alive = lengths_ref[core] - chip * frames
     tiles = range(states // 128)
     for r in range(SUB):
         every = pl.ds(r, subs, stride=SUB)
@@ -344,19 +386,23 @@
     sent_ref[half : half + 8, :] = jnp.concatenate([jnp.broadcast_to(line, (8, 128))] * (states // 128), axis=1)
 
 
-def frames_pass(lengths, vs, init, other, pre, e, top, th, tl):
+def frames_pass(lengths, vs, start, other, pre, e, top, th, tl):
     frames, states = top.shape[0], th.shape[0]
     half = frames // 2
     out = jax.ShapeDtypeStruct
     return pl.pallas_call(
         functools.partial(frames_kernel, frames, len(vs) + 1),
         out_shape=(out((half, states), F32), out((half + 8, states), F32), out((1, 128), F32)),
-        in_specs=[smem()] + [vmem()] * (len(vs) + 7),
+        in_specs=[hbm()] + [vmem()] * (len(vs) + 7),
         out_specs=[vmem()] * 3,
-        scratch_shapes=[pltpu.VMEM((states // 128, frames, 128), F32)],
-        compiler_params=pltpu.CompilerParams(vmem_limit_bytes=40 << 20),
+        scratch_shapes=[
+            pltpu.VMEM((states // 128, frames, 128), F32),
+            pltpu.SMEM(lengths.shape, jnp.int32),
+            pltpu.SemaphoreType.DMA,
+        ],
+        compiler_params=pltpu.CompilerParams(vmem_limit_bytes=6 << 20),
         name="frames",
-    )(lengths, *vs, init[None, :], other, pre, e, top, th, tl)
+    )(pinned(lengths), *vs, start, other, pre, e, top, th, tl)
 
 
 def join_kernel(kept_ref, gain_ref, got_ref, log_ref, out_gain_ref):
@@ -378,6 +424,7 @@
         out_shape=(out((2, half, states), F32), out((2, half), F32)),
         in_specs=[vmem()] * 3,
         out_specs=[vmem()] * 2,
+        compiler_params=pltpu.CompilerParams(vmem_limit_bytes=4 << 20),
         name="join",
     )(kept, gain, got)
 
@@ -392,14 +439,14 @@
     cols = lax.all_to_all(x, "tm", 0, 0, tiled=True).reshape(size * local, frames)
     chip, pre, e, top, th, tl = transfer(cols, trans_weight, block_mask, lengths, pdf_map)
     other = lax.ppermute(chip, "tm", [(i, i ^ 2) for i in range(size)])
-    dh, dl, v = plane_product(chip, other, init_weight)
+    dh, dl, v, start = plane_product(chip, other, init_weight)
     vs = []
     for g in range(1, planes):
         got = lax.ppermute(v, "tm", [(4 * (g - 1) + i, 4 * g + i) for i in range(4)])
         vs.append(got)
         if g < planes - 1:
             v = hop(got, dh, dl)
-    kept, sent, gain = frames_pass(lengths, vs, init_weight, other, pre, e, top, th, tl)
+    kept, sent, gain = frames_pass(lengths, vs, start, other, pre, e, top, th, tl)
     got = lax.ppermute(sent, "tm", [(i, i ^ 1) for i in range(size)])
     return join(kept, gain, got)
 

time: 85.1 us -> 64.4 us (0.76)
  the two profiles are of different devices: /device:TPU:27 before, /device:TPU:25 now
where the time goes in v2:
time: 64.4 us; the launch traced here: 64.2 us
  Pallas kernels  25.3 us (39%)
  waiting for transfers between devices  16.4 us (25%)
  blocking collectives  13.7 us (21%)
  starting transfers between devices  7.01 us (11%)
  local copies, waits for them, and re-layouts  1.07 us (2%)
  between operations  0.71 us (1%)
    pallas_call x1, Pallas kernels, transfer(): pl.pallas_call(functools.partial(transfer_kernel, frames), out_shape=(out...  19.8 us
    all_to_all x1, blocking collectives, shards(): lax.all_to_all(x, 'tm', 0, 0, tiled=True).reshape(size * local, frames)  13.7 us
    ppermute x3, waiting for transfers between devices, shards(): lax.ppermute(v, 'tm', [(4 * (g - 1) + i, 4 * g + i) for i in range(4)])  8.52 us
    ppermute x1, waiting for transfers between devices, shards(): other = lax.ppermute(chip, 'tm', [(i, i ^ 2) for i in range(size)])  7 us
    ppermute x1, starting transfers between devices, shards(): got = lax.ppermute(sent, 'tm', [(i, i ^ 1) for i in range(size)])  3.63 us
    pallas_call x1, Pallas kernels, frames_pass(): pl.pallas_call(functools.partial(frames_kernel, frames, len(vs) + 1), out...  3.31 us
    ppermute x3, starting transfers between devices, shards(): lax.ppermute(v, 'tm', [(4 * (g - 1) + i, 4 * g + i) for i in range(4)])  2.62 us
  transfers between devices with their start and end apart: 5, of which 3 were waited for; matrix products, arithmetic and copies ran while one was open for 0% of the time, Pallas kernels for 0%

profile of v2, /device:TPU:25, one launch (start us, length us, event | category | flops | bytes accessed | tf_op | source)
XLA Modules:
  0.0 64.2 jit_solution(16228899182248272639)
XLA Ops:
  0.6 1.0 %copy.9 = f32[8,8,8,128]{3,2,1,0:T(8,128)S(1)} copy(f32[8,8,8,128]{3,1,2,0:T(8,128)} %bitcast.16) | data formatting | bytes 524288
  1.7 0.1 copy.8
  1.7 13.7 %all_to_all.5 = f32[16,32,128]{2,1,0:T(8,128)S(1)} all-to-all(f32[16,32,128]{2,1,0:T(8,128)S(1)} %bitcast.14), channel_id=1, replica_groups=mesh['groups'=2,'tm'=16] {'tm'}, dimensions={0} | all-to-all | bytes 524288 | tf_op jit(solution)/shard_map/all_to_all | solution.py:439
  15.4 19.8 %transfer.1 = (f32[256,256]{1,0:T(8,128)S(1)}, bf16[2,8,2,256,256]{4,3,2,1,0:T(8,128)(2,1)S(1)}, f32[2,128,128]{2,1,0:T(8,128)S(1)}, f32[128,128]{1,0:T(8,128)S(...) custom-call(s32[2]{0:T(128)} %lengths_hbm.3, s32[4,4]{1,0:T(4,128)} %mask_hbm.1, f32[256,256]{1,0:T(8,128)} %weight_hbm.1, ...), custom_call_target="tpu_custom_call" | custom-call | tf_op jit(solution)/shard_map/transfer/pallas_call | solution.py:230
  35.3 0.8 %collective-permute-start = (f32[256,256]{1,0:T(8,128)S(1)}, f32[256,256]{1,0:T(8,128)S(1)}, u32[]{:S(2)}, u32[]{:S(2)}) collective-permute-start(f32[256,256]{1,0:T(8,128)S(1)} %get-tuple-element.15.own_ref), channel_id=1, source_target_pairs={{0,2},{1,3},{2,0},{3,1},{4,6},{5,7},{6,4},{7,5},{8,10},{9,11},{10,... | collective-permute-start | bytes 786440 | tf_op jit(solution)/shard_map/ppermute | solution.py:441
  36.0 7.0 %collective-permute-done.other_ref.refs_4_ = f32[256,256]{1,0:T(8,128)S(1)} collective-permute-done((f32[256,256]{1,0:T(8,128)S(1)}, f32[256,256]{1,0:T(8,128)S(1)}, u32[]{:S(2)}, u32[]{:S(2)}) %collective-permute-start) | collective-permute-done | bytes 262176 | tf_op jit(solution)/shard_map/ppermute | solution.py:441
  43.0 1.0 %plane.1 = (bf16[256,256]{1,0:T(8,128)(2,1)S(1)}, bf16[256,256]{1,0:T(8,128)(2,1)S(1)}, f32[8,256]{1,0:T(8,128)S(1)}, f32[8,256]{1,0:T(8,128)S(1)}) custom-call(f32[1,256]{1,0:T(1,128)} %bitcast.18, f32[256,256]{1,0:T(8,128)S(1)} %get-tuple-element.15.own_ref, f32[256,256]{1,0:T(8,128)S(1)} %collective-permute-done.other_ref.refs_4_), custom_call_target="tpu_custom_call" | custom-call | tf_op jit(solution)/shard_map/plane/pallas_call | solution.py:298
  44.0 0.7 %collective-permute-start.1 = (f32[8,256]{1,0:T(8,128)S(1)}, f32[8,256]{1,0:T(8,128)S(1)}, u32[]{:S(2)}, u32[]{:S(2)}) collective-permute-start(f32[8,256]{1,0:T(8,128)S(1)} %get-tuple-element.16), channel_id=1, source_target_pairs={{0,4},{1,5},{2,6},{3,7},{16,20},{17,21},{18,22},{19,23}} | collective-permute-start | bytes 24584 | tf_op jit(solution)/shard_map/ppermute | solution.py:445
  44.7 0.0 collective-permute-done.1.v_ref.refs_0_
  44.7 0.2 hop.2
  44.9 0.7 %collective-permute-start.2 = (f32[8,256]{1,0:T(8,128)S(1)}, f32[8,256]{1,0:T(8,128)S(1)}, u32[]{:S(2)}, u32[]{:S(2)}) collective-permute-start(f32[8,256]{1,0:T(8,128)S(1)} %hop.2), channel_id=1, source_target_pairs={{4,8},{5,9},{6,10},{7,11},{20,24},{21,25},{22,26},{23,27}} | collective-permute-start | bytes 24584 | tf_op jit(solution)/shard_map/ppermute | solution.py:445
  45.6 0.0 collective-permute-done.2.v_ref.refs_1_
  45.6 0.2 hop.3
  45.8 1.3 %collective-permute-start.3 = (f32[8,256]{1,0:T(8,128)S(1)}, f32[8,256]{1,0:T(8,128)S(1)}, u32[]{:S(2)}, u32[]{:S(2)}) collective-permute-start(f32[8,256]{1,0:T(8,128)S(1)} %hop.3), channel_id=1, source_target_pairs={{8,12},{9,13},{10,14},{11,15},{24,28},{25,29},{26,30},{27,31}} | collective-permute-start | bytes 24584 | tf_op jit(solution)/shard_map/ppermute | solution.py:445
  47.1 8.5 %collective-permute-done.3.refs_2_ = f32[8,256]{1,0:T(8,128)S(1)} collective-permute-done((f32[8,256]{1,0:T(8,128)S(1)}, f32[8,256]{1,0:T(8,128)S(1)}, u32[]{:S(2)}, u32[]{:S(2)}) %collective-permute-start.3) | collective-permute-done | bytes 8224 | tf_op jit(solution)/shard_map/ppermute | solution.py:445
  55.6 3.3 %frames.1 = (f32[64,256]{1,0:T(8,128)S(1)}, f32[72,256]{1,0:T(8,128)S(1)}, f32[1,128]{1,0:T(1,128)S(1)}) custom-call(s32[2]{0:T(128)} %lengths_hbm.3, f32[8,256]{1,0:T(8,128)S(1)} %collective-permute-done.1.v_ref.refs_0_, f32[8,256]{1,0:T(8,128)S(1)} %collective-permute-done.2.v_ref.refs_1_, f32[8,256]{1,0:T(8,128)S(1)} %collective-permute-done.3.refs_2_, ...), custom_call_target="tpu_custom_call" | custom-call | tf_op jit(solution)/shard_map/frames/pallas_call | solution.py:393
  59.0 3.6 %collective-permute-start.4 = (f32[72,256]{1,0:T(8,128)S(1)}, f32[72,256]{1,0:T(8,128)S(1)}, u32[]{:S(2)}, u32[]{:S(2)}) collective-permute-start(f32[72,256]{1,0:T(8,128)S(1)} %get-tuple-element.27), channel_id=1, source_target_pairs={{0,1},{1,0},{2,3},{3,2},{4,5},{5,4},{6,7},{7,6},{8,9},{9,8},{10,11... | collective-permute-start | bytes 221192 | tf_op jit(solution)/shard_map/ppermute | solution.py:450
  62.6 0.9 %collective-permute-done.4.got_ref = f32[72,256]{1,0:T(8,128)S(1)} collective-permute-done((f32[72,256]{1,0:T(8,128)S(1)}, f32[72,256]{1,0:T(8,128)S(1)}, u32[]{:S(2)}, u32[]{:S(2)}) %collective-permute-start.4) | collective-permute-done | bytes 73760 | tf_op jit(solution)/shard_map/ppermute | solution.py:450
  63.5 0.7 %join.1 = (f32[2,64,256]{2,1,0:T(8,128)}, f32[2,64]{1,0:T(2,128)}) custom-call(f32[64,256]{1,0:T(8,128)S(1)} %get-tuple-element.25.kept_ref, f32[1,128]{1,0:T(1,128)S(1)} %get-tuple-element.26.gain_ref, f32[72,256]{1,0:T(8,128)S(1)} %collective-permute-done.4.got_ref), custom_call_target="tpu_custom_call" | custom-call | tf_op jit(solution)/shard_map/join/pallas_call | solution.py:422
  (1 shorter events, 0.0 us)
Async XLA Ops:
  35.3 7.8 %collective-permute-start = (f32[256,256]{1,0:T(8,128)S(1)}, f32[256,256]{1,0:T(8,128)S(1)}, u32[]{:S(2)}, u32[]{:S(2)}) collective-permute-start(f32[256,256]{1,0:T(8,128)S(1)} %get-tuple-element.15.own_ref), channel_id=1, source_target_pairs={{0,2},{1,3},{2,0},{3,1},{4,6},{5,7},{6,4},{7,5},{8,10},{9,11},{10,... | collective-permute-start | bytes 786440 | tf_op jit(solution)/shard_map/ppermute | solution.py:441
  44.0 0.7 %collective-permute-start.1 = (f32[8,256]{1,0:T(8,128)S(1)}, f32[8,256]{1,0:T(8,128)S(1)}, u32[]{:S(2)}, u32[]{:S(2)}) collective-permute-start(f32[8,256]{1,0:T(8,128)S(1)} %get-tuple-element.16), channel_id=1, source_target_pairs={{0,4},{1,5},{2,6},{3,7},{16,20},{17,21},{18,22},{19,23}} | collective-permute-start | bytes 24584 | tf_op jit(solution)/shard_map/ppermute | solution.py:445
  44.9 0.7 %collective-permute-start.2 = (f32[8,256]{1,0:T(8,128)S(1)}, f32[8,256]{1,0:T(8,128)S(1)}, u32[]{:S(2)}, u32[]{:S(2)}) collective-permute-start(f32[8,256]{1,0:T(8,128)S(1)} %hop.2), channel_id=1, source_target_pairs={{4,8},{5,9},{6,10},{7,11},{20,24},{21,25},{22,26},{23,27}} | collective-permute-start | bytes 24584 | tf_op jit(solution)/shard_map/ppermute | solution.py:445
  45.8 9.8 %collective-permute-start.3 = (f32[8,256]{1,0:T(8,128)S(1)}, f32[8,256]{1,0:T(8,128)S(1)}, u32[]{:S(2)}, u32[]{:S(2)}) collective-permute-start(f32[8,256]{1,0:T(8,128)S(1)} %hop.3), channel_id=1, source_target_pairs={{8,12},{9,13},{10,14},{11,15},{24,28},{25,29},{26,30},{27,31}} | collective-permute-start | bytes 24584 | tf_op jit(solution)/shard_map/ppermute | solution.py:445
  59.0 4.5 %collective-permute-start.4 = (f32[72,256]{1,0:T(8,128)S(1)}, f32[72,256]{1,0:T(8,128)S(1)}, u32[]{:S(2)}, u32[]{:S(2)}) collective-permute-start(f32[72,256]{1,0:T(8,128)S(1)} %get-tuple-element.27), channel_id=1, source_target_pairs={{0,1},{1,0},{2,3},{3,2},{4,5},{5,4},{6,7},{7,6},{8,9},{9,8},{10,11... | collective-permute-start | bytes 221192 | tf_op jit(solution)/shard_map/ppermute | solution.py:450

commit v3 on v2

--- a/solution.py
+++ b/solution.py
@@ -9,6 +9,7 @@
 F32 = jnp.float32
 BF16 = jnp.bfloat16
 SUB = 8
+LEAD = 4
 
 
 def halves(x):
@@ -266,70 +267,88 @@
     return v / jnp.sum(v, axis=1, keepdims=True)
 
 
-def plane_kernel(init_hbm, own_ref, other_ref, dh_ref, dl_ref, v_ref, start_ref, init_ref, sem):
+def first_kernel(init_hbm, own_ref, v_ref, start_ref, init_ref, sem):
     copy = pltpu.make_async_copy(init_hbm, init_ref, sem)
     copy.start()
-    chip = lax.axis_index("tm") // 2
-    plane = chip // 2
-
-    def product(left, right):
-        d = dot3(*halves(left[...]), *halves(right[...]))
-        h, l = halves(d * (1.0 / jnp.max(d, keepdims=True)[:, :1]))
-        dh_ref[...] = h
-        dl_ref[...] = l
-
-    @pl.when(chip % 2 == 0)
-    def _():
-        product(own_ref, other_ref)
-
-    @pl.when(chip % 2 == 1)
-    def _():
-        product(other_ref, own_ref)
-
+    high, low = halves(own_ref[...])
     copy.wait()
     start = jnp.broadcast_to(unit(init_ref[...]), v_ref.shape)
     start_ref[...] = start
-    v_ref[...] = unit(row_dot(start, dh_ref[...], dl_ref[...]))
-
-
-def plane_product(own, other, init):
+    v_ref[...] = unit(row_dot(start, high, low))
+
+
+def first(init, own):
     states = own.shape[0]
-    out = jax.ShapeDtypeStruct
-    return pl.pallas_call(
-        plane_kernel,
-        out_shape=(out((states, states), BF16),) * 2 + (out((8, states), F32),) * 2,
-        in_specs=[hbm()] + [vmem()] * 2,
-        out_specs=[vmem()] * 4,
+    return pl.pallas_call(
+        first_kernel,
+        out_shape=(jax.ShapeDtypeStruct((8, states), F32),) * 2,
+        in_specs=[hbm(), vmem()],
+        out_specs=[vmem()] * 2,
         scratch_shapes=[pltpu.VMEM((1, states), F32), pltpu.SemaphoreType.DMA],
         compiler_params=pltpu.CompilerParams(vmem_limit_bytes=4 << 20),
+        name="first",
+    )(pinned(init[None, :]), own)
+
+
+def plane_kernel(own_ref, other_ref, d_ref):
+    chip = lax.axis_index("tm") // 2
+
+    def product(left, right):
+        d = dot3(*halves(left[...]), *halves(right[...]))
+        d_ref[...] = d * (1.0 / jnp.max(d, keepdims=True)[:, :1])
+
+    @pl.when(jnp.logical_and(chip >= LEAD, chip % 2 == 0))
+    def _():
+        product(own_ref, other_ref)
+
+    @pl.when(jnp.logical_and(chip >= LEAD, chip % 2 == 1))
+    def _():
+        product(other_ref, own_ref)
+
+    @pl.when(chip < LEAD)
+    def _():
+        d_ref[...] = own_ref[...]
+
+
+def plane_product(own, other):
+    return pl.pallas_call(
+        plane_kernel,
+        out_shape=jax.ShapeDtypeStruct(own.shape, F32),
+        in_specs=[vmem()] * 2,
+        out_specs=vmem(),
+        compiler_params=pltpu.CompilerParams(vmem_limit_bytes=4 << 20),
         name="plane",
-    )(pinned(init[None, :]), own, other)
-
-
-def hop_kernel(v_ref, dh_ref, dl_ref, out_ref):
-    out_ref[...] = unit(row_dot(v_ref[...], dh_ref[...], dl_ref[...]))
-
-
-def hop(v, dh, dl):
+    )(own, other)
+
+
+def hop_kernel(m_ref, *refs):
+    *v_refs, out_ref = refs
+    v = v_refs[0][...]
+    for ref in v_refs[1:]:
+        v = v + ref[...]
+    out_ref[...] = unit(row_dot(v, *halves(m_ref[...])))
+
+
+def hop(m, *vs):
     return pl.pallas_call(
         hop_kernel,
-        out_shape=jax.ShapeDtypeStruct(v.shape, F32),
-        in_specs=[vmem()] * 3,
+        out_shape=jax.ShapeDtypeStruct(vs[0].shape, F32),
+        in_specs=[vmem()] * (len(vs) + 1),
         out_specs=vmem(),
         compiler_params=pltpu.CompilerParams(vmem_limit_bytes=4 << 20),
         name="hop",
-    )(v, dh, dl)
+    )(m, *vs)
 
 
 def frames_kernel(
     frames,
-    planes,
+    chips_of,
     lengths_hbm,
     *refs,
 ):
-    v_refs = refs[: planes - 1]
+    v_refs = refs[: len(chips_of)]
     start_ref, other_ref, pre_ref, e_ref, top_ref, th_ref, tl_ref, kept_ref, sent_ref, gain_ref, *scratch = refs[
-        planes - 1 :
+        len(chips_of) :
     ]
     alpha_scr, lengths_ref, sem = scratch
     copy = pltpu.make_async_copy(lengths_hbm, lengths_ref, sem)
@@ -342,10 +361,10 @@
     core = index % 2
     chip = index // 2
     v = start_ref[...]
-    for g in range(1, planes):
-        v = jnp.where(chip // 2 == g, v_refs[g - 1][...], v)
+    for low, high, ref in ((*pair, ref) for pair, ref in zip(chips_of, v_refs)):
+        v = jnp.where(jnp.logical_and(chip >= low, chip < high), ref[...], v)
     oh, ol = halves(other_ref[...])
-    v = jnp.where(chip % 2 == 1, unit(row_dot(v, oh, ol)), v)
+    v = jnp.where(jnp.logical_and(chip >= LEAD, chip % 2 == 1), unit(row_dot(v, oh, ol)), v)
     mid = unit(row_dot(v, pre_ref[0, blocks - 1, 0], pre_ref[0, blocks - 1, 1]))
     rows = [v[0:1]]
     for j in range(blocks - 1):
@@ -386,12 +405,12 @@
     sent_ref[half : half + 8, :] = jnp.concatenate([jnp.broadcast_to(line, (8, 128))] * (states // 128), axis=1)
 
 
-def frames_pass(lengths, vs, start, other, pre, e, top, th, tl):
+def frames_pass(lengths, chips_of, vs, start, other, pre, e, top, th, tl):
     frames, states = top.shape[0], th.shape[0]
     half = frames // 2
     out = jax.ShapeDtypeStruct
     return pl.pallas_call(
-        functools.partial(frames_kernel, frames, len(vs) + 1),
+        functools.partial(frames_kernel, frames, chips_of),
         out_shape=(out((half, states), F32), out((half + 8, states), F32), out((1, 128), F32)),
         in_specs=[hbm()] + [vmem()] * (len(vs) + 7),
         out_specs=[vmem()] * 3,
@@ -433,20 +452,28 @@
     utts, total, local = loglik.shape
     chips = size // 2
     frames = total // chips
-    planes = chips // 2
     x = jnp.transpose(loglik, (0, 2, 1)).reshape(utts, local, chips, frames)
     x = jnp.transpose(x, (2, 0, 1, 3)).reshape(size, local, frames)
     cols = lax.all_to_all(x, "tm", 0, 0, tiled=True).reshape(size * local, frames)
     chip, pre, e, top, th, tl = transfer(cols, trans_weight, block_mask, lengths, pdf_map)
-    other = lax.ppermute(chip, "tm", [(i, i ^ 2) for i in range(size)])
-    dh, dl, v, start = plane_product(chip, other, init_weight)
-    vs = []
-    for g in range(1, planes):
-        got = lax.ppermute(v, "tm", [(4 * (g - 1) + i, 4 * g + i) for i in range(4)])
+    other = lax.ppermute(chip, "tm", [(i, i ^ 2) for i in range(2 * LEAD, size)])
+    v, start = first(init_weight, chip)
+    chips_of, vs = [], []
+
+    def send(v, source, target, count=1):
+        got = lax.ppermute(v, "tm", [(2 * source + i, 2 * target + i) for i in range(2 * count)])
+        chips_of.append((target, target + count))
         vs.append(got)
-        if g < planes - 1:
-            v = hop(got, dh, dl)
-    kept, sent, gain = frames_pass(lengths, vs, start, other, pre, e, top, th, tl)
+        return got
+
+    for c in range(1, LEAD):
+        v = hop(chip, send(v, c - 1, c))
+    plane = plane_product(chip, other)
+    last = [send(v, LEAD - 1, LEAD), send(v, LEAD - 1, LEAD + 1)]
+    for c in range(LEAD + 2, chips, 2):
+        v = hop(plane, *last)
+        last = [send(v, c - 2, c, 2)]
+    kept, sent, gain = frames_pass(lengths, chips_of, vs, start, other, pre, e, top, th, tl)
     got = lax.ppermute(sent, "tm", [(i, i ^ 1) for i in range(size)])
     return join(kept, gain, got)
 

time: 64.4 us -> 66.1 us (1.026)
  starting transfers between devices: 7.01 us -> 11.1 us
  waiting for transfers between devices: 16.4 us -> 12.9 us
  Pallas kernels: 25.3 us -> 26.2 us
    ppermute x4 -> x7, starting transfers between devices: 3.38 us -> 7.19 us  [the longest x6 4.59 us: send(): lax.ppermute(v, 'tm', [(2 * source + i, 2 * target + i) for i in range(2...]
    ppermute x4 -> x7, waiting for transfers between devices: 15.5 us -> 12 us  [the longest x6 9.98 us: send(): lax.ppermute(v, 'tm', [(2 * source + i, 2 * target + i) for i in range(2...]
    pallas_call x4 -> x7, Pallas kernels: 4.74 us -> 5.63 us  [the longest x1 3.31 us: frames_pass(): pl.pallas_call(functools.partial(frames_kernel, frames, chips_of), out_sh...]
  transfers between devices with their start and end apart: 5 -> 8, of which waited for: 3 -> 3; matrix products, arithmetic and copies ran while one was open for 0% -> 0% of each run, Pallas kernels for 0% -> 3%
where the time goes in v3:
time: 66.1 us; the launch traced here: 65.8 us
  Pallas kernels  26.2 us (40%)
  blocking collectives  13.7 us (21%)
  waiting for transfers between devices  12.9 us (20%)
  starting transfers between devices  11.1 us (17%)
  local copies, waits for them, and re-layouts  1.07 us (2%)
  between operations  0.78 us (1%)
    pallas_call x1, Pallas kernels, transfer(): pl.pallas_call(functools.partial(transfer_kernel, frames), out_shape=(out...  19.9 us
    all_to_all x1, blocking collectives, shards(): lax.all_to_all(x, 'tm', 0, 0, tiled=True).reshape(size * local, frames)  13.7 us
    ppermute x6, waiting for transfers between devices, send(): lax.ppermute(v, 'tm', [(2 * source + i, 2 * target + i) for i in range(2...  9.98 us
    ppermute x6, starting transfers between devices, send(): lax.ppermute(v, 'tm', [(2 * source + i, 2 * target + i) for i in range(2...  4.59 us
    ppermute x1, starting transfers between devices, shards(): got = lax.ppermute(sent, 'tm', [(i, i ^ 1) for i in range(size)])  3.94 us
    pallas_call x1, Pallas kernels, frames_pass(): pl.pallas_call(functools.partial(frames_kernel, frames, chips_of), out_sh...  3.31 us
    ppermute x1, starting transfers between devices, shards(): lax.ppermute(chip, 'tm', [(i, i ^ 2) for i in range(2 * LEAD, size)])  2.59 us
    ppermute x1, waiting for transfers between devices, shards(): lax.ppermute(chip, 'tm', [(i, i ^ 2) for i in range(2 * LEAD, size)])  2.01 us
  transfers between devices with their start and end apart: 8, of which 3 were waited for; matrix products, arithmetic and copies ran while one was open for 0% of the time, Pallas kernels for 3%

profile of v3, /device:TPU:25, one launch (start us, length us, event | category | flops | bytes accessed | tf_op | source)
XLA Modules:
  0.0 65.8 jit_solution(13686245751727349264)
XLA Ops:
  0.6 1.0 %copy.9 = f32[8,8,8,128]{3,2,1,0:T(8,128)S(1)} copy(f32[8,8,8,128]{3,1,2,0:T(8,128)} %bitcast.16) | data formatting | bytes 524288
  1.7 0.1 copy.8
  1.7 13.7 %all_to_all.5 = f32[16,32,128]{2,1,0:T(8,128)S(1)} all-to-all(f32[16,32,128]{2,1,0:T(8,128)S(1)} %bitcast.14), channel_id=1, replica_groups=mesh['groups'=2,'tm'=16] {'tm'}, dimensions={0} | all-to-all | bytes 524288 | tf_op jit(solution)/shard_map/all_to_all | solution.py:457
  15.4 19.9 %transfer.1 = (f32[256,256]{1,0:T(8,128)S(1)}, bf16[2,8,2,256,256]{4,3,2,1,0:T(8,128)(2,1)S(1)}, f32[2,128,128]{2,1,0:T(8,128)S(1)}, f32[128,128]{1,0:T(8,128)S(...) custom-call(s32[2]{0:T(128)} %lengths_hbm.3, s32[4,4]{1,0:T(4,128)} %mask_hbm.1, f32[256,256]{1,0:T(8,128)} %weight_hbm.1, ...), custom_call_target="tpu_custom_call" | custom-call | tf_op jit(solution)/shard_map/transfer/pallas_call | solution.py:231
  35.3 2.6 %collective-permute-start.5 = (f32[256,256]{1,0:T(8,128)S(1)}, f32[256,256]{1,0:T(8,128)S(1)}, u32[]{:S(2)}, u32[]{:S(2)}) collective-permute-start(f32[256,256]{1,0:T(8,128)S(1)} %get-tuple-element.13.own_ref.m_ref), channel_id=1, source_target_pairs={{8,10},{9,11},{10,8},{11,9},{12,14},{13,15},{14,12},{15,13},{24,26... | collective-permute-start | bytes 786440 | tf_op jit(solution)/shard_map/ppermute | solution.py:459
  37.9 1.0 %first.1 = (f32[8,256]{1,0:T(8,128)S(1)}, f32[8,256]{1,0:T(8,128)S(1)}) custom-call(f32[1,256]{1,0:T(1,128)} %bitcast.18, f32[256,256]{1,0:T(8,128)S(1)} %get-tuple-element.13.own_ref.m_ref), custom_call_target="tpu_custom_call" | custom-call | tf_op jit(solution)/shard_map/first/pallas_call | solution.py:282
  38.9 0.7 %collective-permute-start = (f32[8,256]{1,0:T(8,128)S(1)}, f32[8,256]{1,0:T(8,128)S(1)}, u32[]{:S(2)}, u32[]{:S(2)}) collective-permute-start(f32[8,256]{1,0:T(8,128)S(1)} %get-tuple-element.14), channel_id=1, source_target_pairs={{0,2},{1,3},{16,18},{17,19}} | collective-permute-start | bytes 24584 | tf_op jit(solution)/shard_map/ppermute | solution.py:464
  39.6 0.0 collective-permute-done.refs_0_
  39.6 0.2 hop.4
  39.8 0.7 %collective-permute-start.1 = (f32[8,256]{1,0:T(8,128)S(1)}, f32[8,256]{1,0:T(8,128)S(1)}, u32[]{:S(2)}, u32[]{:S(2)}) collective-permute-start(f32[8,256]{1,0:T(8,128)S(1)} %hop.4), channel_id=1, source_target_pairs={{2,4},{3,5},{18,20},{19,21}} | collective-permute-start | bytes 24584 | tf_op jit(solution)/shard_map/ppermute | solution.py:464
  40.5 0.0 collective-permute-done.1.refs_0_.refs_1_
  40.5 0.2 hop.5
  40.7 0.7 %collective-permute-start.2 = (f32[8,256]{1,0:T(8,128)S(1)}, f32[8,256]{1,0:T(8,128)S(1)}, u32[]{:S(2)}, u32[]{:S(2)}) collective-permute-start(f32[8,256]{1,0:T(8,128)S(1)} %hop.5), channel_id=1, source_target_pairs={{4,6},{5,7},{20,22},{21,23}} | collective-permute-start | bytes 24584 | tf_op jit(solution)/shard_map/ppermute | solution.py:464
  41.4 0.0 collective-permute-done.2.refs_0_.refs_2_
  41.4 0.2 hop.6
  41.7 0.7 %collective-permute-start.4 = (f32[8,256]{1,0:T(8,128)S(1)}, f32[8,256]{1,0:T(8,128)S(1)}, u32[]{:S(2)}, u32[]{:S(2)}) collective-permute-start(f32[8,256]{1,0:T(8,128)S(1)} %hop.6), channel_id=1, source_target_pairs={{6,10},{7,11},{22,26},{23,27}} | collective-permute-start | bytes 24584 | tf_op jit(solution)/shard_map/ppermute | solution.py:464
  42.3 0.7 %collective-permute-start.3 = (f32[8,256]{1,0:T(8,128)S(1)}, f32[8,256]{1,0:T(8,128)S(1)}, u32[]{:S(2)}, u32[]{:S(2)}) collective-permute-start(f32[8,256]{1,0:T(8,128)S(1)} %hop.6), channel_id=1, source_target_pairs={{6,8},{7,9},{22,24},{23,25}} | collective-permute-start | bytes 24584 | tf_op jit(solution)/shard_map/ppermute | solution.py:464
  43.0 2.0 %collective-permute-done.5.other_ref.refs_7_ = f32[256,256]{1,0:T(8,128)S(1)} collective-permute-done((f32[256,256]{1,0:T(8,128)S(1)}, f32[256,256]{1,0:T(8,128)S(1)}, u32[]{:S(2)}, u32[]{:S(2)}) %collective-permute-start.5) | collective-permute-done | bytes 262176 | tf_op jit(solution)/shard_map/ppermute | solution.py:459
  45.0 0.4 plane.1.m_ref
  45.4 0.0 collective-permute-done.4.refs_1_.refs_4_
  45.4 0.0 collective-permute-done.3.refs_0_.refs_3_
  45.5 0.2 hop.7
  45.7 1.3 %collective-permute-start.6 = (f32[8,256]{1,0:T(8,128)S(1)}, f32[8,256]{1,0:T(8,128)S(1)}, u32[]{:S(2)}, u32[]{:S(2)}) collective-permute-start(f32[8,256]{1,0:T(8,128)S(1)} %hop.7), channel_id=1, source_target_pairs={{8,12},{9,13},{10,14},{11,15},{24,28},{25,29},{26,30},{27,31}} | collective-permute-start | bytes 24584 | tf_op jit(solution)/shard_map/ppermute | solution.py:464
  47.0 10.0 %collective-permute-done.6.refs_5_ = f32[8,256]{1,0:T(8,128)S(1)} collective-permute-done((f32[8,256]{1,0:T(8,128)S(1)}, f32[8,256]{1,0:T(8,128)S(1)}, u32[]{:S(2)}, u32[]{:S(2)}) %collective-permute-start.6) | collective-permute-done | bytes 8224 | tf_op jit(solution)/shard_map/ppermute | solution.py:464
  56.9 3.3 %frames.1 = (f32[64,256]{1,0:T(8,128)S(1)}, f32[72,256]{1,0:T(8,128)S(1)}, f32[1,128]{1,0:T(1,128)S(1)}) custom-call(s32[2]{0:T(128)} %lengths_hbm.3, f32[8,256]{1,0:T(8,128)S(1)} %collective-permute-done.refs_0_, f32[8,256]{1,0:T(8,128)S(1)} %collective-permute-done.1.refs_0_.refs_1_, f32[8,256]{1,0:T(8,128)S(1)} %collective-permute-done.2.refs_0_.refs_2_, ...), custom_call_target="tpu_custom_call" | custom-call | tf_op jit(solution)/shard_map/frames/pallas_call | solution.py:412
  60.3 3.9 %collective-permute-start.7 = (f32[72,256]{1,0:T(8,128)S(1)}, f32[72,256]{1,0:T(8,128)S(1)}, u32[]{:S(2)}, u32[]{:S(2)}) collective-permute-start(f32[72,256]{1,0:T(8,128)S(1)} %get-tuple-element.23), channel_id=1, source_target_pairs={{0,1},{1,0},{2,3},{3,2},{4,5},{5,4},{6,7},{7,6},{8,9},{9,8},{10,11... | collective-permute-start | bytes 221192 | tf_op jit(solution)/shard_map/ppermute | solution.py:477
  64.2 0.9 %collective-permute-done.7.got_ref = f32[72,256]{1,0:T(8,128)S(1)} collective-permute-done((f32[72,256]{1,0:T(8,128)S(1)}, f32[72,256]{1,0:T(8,128)S(1)}, u32[]{:S(2)}, u32[]{:S(2)}) %collective-permute-start.7) | collective-permute-done | bytes 73760 | tf_op jit(solution)/shard_map/ppermute | solution.py:477
  65.1 0.7 %join.1 = (f32[2,64,256]{2,1,0:T(8,128)}, f32[2,64]{1,0:T(2,128)}) custom-call(f32[64,256]{1,0:T(8,128)S(1)} %get-tuple-element.21.kept_ref, f32[1,128]{1,0:T(1,128)S(1)} %get-tuple-element.22.gain_ref, f32[72,256]{1,0:T(8,128)S(1)} %collective-permute-done.7.got_ref), custom_call_target="tpu_custom_call" | custom-call | tf_op jit(solution)/shard_map/join/pallas_call | solution.py:441
  (1 shorter events, 0.0 us)
Async XLA Ops:
  35.3 9.7 %collective-permute-start.5 = (f32[256,256]{1,0:T(8,128)S(1)}, f32[256,256]{1,0:T(8,128)S(1)}, u32[]{:S(2)}, u32[]{:S(2)}) collective-permute-start(f32[256,256]{1,0:T(8,128)S(1)} %get-tuple-element.13.own_ref.m_ref), channel_id=1, source_target_pairs={{8,10},{9,11},{10,8},{11,9},{12,14},{13,15},{14,12},{15,13},{24,26... | collective-permute-start | bytes 786440 | tf_op jit(solution)/shard_map/ppermute | solution.py:459
  38.9 0.7 %collective-permute-start = (f32[8,256]{1,0:T(8,128)S(1)}, f32[8,256]{1,0:T(8,128)S(1)}, u32[]{:S(2)}, u32[]{:S(2)}) collective-permute-start(f32[8,256]{1,0:T(8,128)S(1)} %get-tuple-element.14), channel_id=1, source_target_pairs={{0,2},{1,3},{16,18},{17,19}} | collective-permute-start | bytes 24584 | tf_op jit(solution)/shard_map/ppermute | solution.py:464
  39.8 0.7 %collective-permute-start.1 = (f32[8,256]{1,0:T(8,128)S(1)}, f32[8,256]{1,0:T(8,128)S(1)}, u32[]{:S(2)}, u32[]{:S(2)}) collective-permute-start(f32[8,256]{1,0:T(8,128)S(1)} %hop.4), channel_id=1, source_target_pairs={{2,4},{3,5},{18,20},{19,21}} | collective-permute-start | bytes 24584 | tf_op jit(solution)/shard_map/ppermute | solution.py:464
  40.7 0.7 %collective-permute-start.2 = (f32[8,256]{1,0:T(8,128)S(1)}, f32[8,256]{1,0:T(8,128)S(1)}, u32[]{:S(2)}, u32[]{:S(2)}) collective-permute-start(f32[8,256]{1,0:T(8,128)S(1)} %hop.5), channel_id=1, source_target_pairs={{4,6},{5,7},{20,22},{21,23}} | collective-permute-start | bytes 24584 | tf_op jit(solution)/shard_map/ppermute | solution.py:464
  41.7 3.8 %collective-permute-start.4 = (f32[8,256]{1,0:T(8,128)S(1)}, f32[8,256]{1,0:T(8,128)S(1)}, u32[]{:S(2)}, u32[]{:S(2)}) collective-permute-start(f32[8,256]{1,0:T(8,128)S(1)} %hop.6), channel_id=1, source_target_pairs={{6,10},{7,11},{22,26},{23,27}} | collective-permute-start | bytes 24584 | tf_op jit(solution)/shard_map/ppermute | solution.py:464
  42.3 3.1 %collective-permute-start.3 = (f32[8,256]{1,0:T(8,128)S(1)}, f32[8,256]{1,0:T(8,128)S(1)}, u32[]{:S(2)}, u32[]{:S(2)}) collective-permute-start(f32[8,256]{1,0:T(8,128)S(1)} %hop.6), channel_id=1, source_target_pairs={{6,8},{7,9},{22,24},{23,25}} | collective-permute-start | bytes 24584 | tf_op jit(solution)/shard_map/ppermute | solution.py:464
  45.7 11.3 %collective-permute-start.6 = (f32[8,256]{1,0:T(8,128)S(1)}, f32[8,256]{1,0:T(8,128)S(1)}, u32[]{:S(2)}, u32[]{:S(2)}) collective-permute-start(f32[8,256]{1,0:T(8,128)S(1)} %hop.7), channel_id=1, source_target_pairs={{8,12},{9,13},{10,14},{11,15},{24,28},{25,29},{26,30},{27,31}} | collective-permute-start | bytes 24584 | tf_op jit(solution)/shard_map/ppermute | solution.py:464
  60.3 4.9 %collective-permute-start.7 = (f32[72,256]{1,0:T(8,128)S(1)}, f32[72,256]{1,0:T(8,128)S(1)}, u32[]{:S(2)}, u32[]{:S(2)}) collective-permute-start(f32[72,256]{1,0:T(8,128)S(1)} %get-tuple-element.23), channel_id=1, source_target_pairs={{0,1},{1,0},{2,3},{3,2},{4,5},{5,4},{6,7},{7,6},{8,9},{9,8},{10,11... | collective-permute-start | bytes 221192 | tf_op jit(solution)/shard_map/ppermute | solution.py:477

commit v4 on v2

--- a/solution.py
+++ b/solution.py
@@ -11,6 +11,12 @@
 SUB = 8
 
 
+def place(half):
+    index = lax.axis_index("tm")
+    first = (index // 4) * 4 * half + (index % 2) * half
+    return (index // 2) % 2, (first, first + 2 * half)
+
+
 def halves(x):
     high = x.astype(BF16)
     return high, (x - high.astype(F32)).astype(BF16)
@@ -30,13 +36,15 @@
     mask_hbm,
     weight_hbm,
     map_hbm,
+    init_hbm,
     cols_ref,
-    chip_ref,
+    mats_ref,
     pre_ref,
     e_ref,
     top_ref,
     th_ref,
     tl_ref,
+    start_ref,
     g_scr,
     e_scr,
     t_scr,
@@ -48,6 +56,7 @@
     mask_ref,
     weight_ref,
     map_ref,
+    init_ref,
     sems,
 ):
     copies = [
@@ -58,6 +67,7 @@
                 (weight_hbm, weight_ref),
                 (mask_hbm, mask_ref),
                 (lengths_hbm, lengths_ref),
+                (init_hbm, init_ref),
             )
         )
     ]
@@ -67,8 +77,7 @@
     half = frames // 2
     rows = states // 2
     blocks = half // SUB
-    core = lax.axis_index("tm") % 2
-    first_frame = (lax.axis_index("tm") // 2) * frames
+    utt, slots = place(half)
     cols = cols_ref[...].T
     copies[0].wait()
     pick = (lax.broadcasted_iota(jnp.int32, (cols.shape[1], states), 0) == map_ref[...]).astype(F32).astype(BF16)
@@ -98,7 +107,8 @@
 
     for copy in copies[1:]:
         copy.wait()
-    alive = lengths_ref[core] - first_frame
+    alive = [lengths_ref[utt] - slot for slot in slots]
+    start_ref[...] = jnp.broadcast_to(unit(init_ref[...]), start_ref.shape)
 
     nb = mask_ref.shape[0]
     width = states // nb
@@ -116,8 +126,9 @@
     eye = (
         lax.broadcasted_iota(jnp.int32, (states, states), 0) == lax.broadcasted_iota(jnp.int32, (states, states), 1)
     ).astype(F32)
-    for mh, ml, off in ((ah, al, 0), (bh, bl, half)):
-        h, l = halves(jnp.where(alive > off, t_scr[...] * e_scr[off : off + 1, :], eye))
+    for k, (mh, ml) in enumerate(((ah, al), (bh, bl))):
+        off = k * half
+        h, l = halves(jnp.where(alive[k] > 0, t_scr[...] * e_scr[off : off + 1, :], eye))
         mh[0:states, :] = h
         ml[0:states, :] = l
 
@@ -147,9 +158,8 @@
 
         def post(k, s, peak):
             mh, ml = mats[k]
-            frame = s + k * half
-            er = e_scr[pl.ds(frame, 1), :] * (1.0 / jnp.max(peak.astype(F32), keepdims=True)[:, :1])
-            base = jnp.where(frame < alive, 0, states)
+            er = e_scr[pl.ds(s + k * half, 1), :] * (1.0 / jnp.max(peak.astype(F32), keepdims=True)[:, :1])
+            base = jnp.where(s < alive[k], 0, states)
             new = None
             for m in range(2):
                 x = pltpu.matmul_pop(accs[k][m]) * er
@@ -190,15 +200,8 @@
         for r in range(1, SUB):
             peaks = step((blocks - 1) * SUB + r, peaks, r == SUB - 1)
         keep(blocks - 1)
-        for m in range(2):
-            sl = pl.ds(m * rows, rows)
-            pltpu.matmul_push_rhs(bh[0:states, :], 0, m)
-            pltpu.matmul_acc_lhs(accs[0][m], ah[sl, :], 0)
-            pltpu.matmul_acc_lhs(accs[0][m], al[sl, :], None)
-            pltpu.matmul_push_rhs(bl[0:states, :], 1, m)
-            pltpu.matmul_acc_lhs(accs[0][m], ah[sl, :], 1)
-        c = jnp.concatenate([pltpu.matmul_pop(accs[0][m]) for m in range(2)], axis=0)
-        chip_ref[...] = c * (1.0 / jnp.max(c, keepdims=True)[:, :1])
+        for i, (mh, ml) in enumerate(mats):
+            mats_ref[i] = mh[0:states, :].astype(F32) + ml[0:states, :].astype(F32)
 
     shape = (rows, states)
     pl.run_scoped(
@@ -222,7 +225,7 @@
     return pltpu.with_memory_space_constraint(x, pltpu.MemorySpace.HBM)
 
 
-def transfer(cols, weight, mask, lengths, pdf_map):
+def transfer(cols, weight, mask, lengths, pdf_map, init):
     columns, frames = cols.shape
     states = weight.shape[0]
     blocks = frames // 2 // SUB
@@ -230,15 +233,16 @@
     return pl.pallas_call(
         functools.partial(transfer_kernel, frames),
         out_shape=(
-            out((states, states), F32),
+            out((2, states, states), F32),
             out((2, blocks, 2, states, states), BF16),
             out((states // 128, frames, 128), F32),
             out((frames, 128), F32),
             out((states, states), BF16),
             out((states, states), BF16),
+            out((8, states), F32),
         ),
-        in_specs=[hbm()] * 4 + [vmem()],
-        out_specs=[vmem()] * 6,
+        in_specs=[hbm()] * 5 + [vmem()],
+        out_specs=[vmem()] * 7,
         scratch_shapes=[pltpu.VMEM((frames, states), F32)] * 2
         + [pltpu.VMEM((states, states), F32)]
         + [pltpu.VMEM((2 * states, states), BF16)] * 4
@@ -247,11 +251,12 @@
             pltpu.SMEM(mask.shape, jnp.int32),
             pltpu.VMEM(weight.shape, F32),
             pltpu.VMEM((1, states), jnp.int32),
-            pltpu.SemaphoreType.DMA((4,)),
+            pltpu.VMEM((1, states), F32),
+            pltpu.SemaphoreType.DMA((5,)),
         ],
         compiler_params=pltpu.CompilerParams(vmem_limit_bytes=6 << 20),
         name="transfer",
-    )(*map(pinned, (lengths, mask, weight, pdf_map[None, :])), cols)
+    )(*map(pinned, (lengths, mask, weight, pdf_map[None, :], init[None, :])), cols)
 
 
 def row_dot(v, matrix_high, matrix_low):
@@ -266,70 +271,95 @@
     return v / jnp.sum(v, axis=1, keepdims=True)
 
 
-def plane_kernel(init_hbm, own_ref, other_ref, dh_ref, dl_ref, v_ref, start_ref, init_ref, sem):
-    copy = pltpu.make_async_copy(init_hbm, init_ref, sem)
+def pass_on(v, matrix):
+    return row_dot(v, *halves(matrix)) * (1.0 / jnp.sum(v, axis=1, keepdims=True))
+
+
+def in_order(own_ref, other_ref, do):
+    core = lax.axis_index("tm") % 2
+
+    @pl.when(core == 0)
+    def _():
+        do(own_ref.at[0], other_ref.at[0], own_ref.at[1], other_ref.at[1])
+
+    @pl.when(core == 1)
+    def _():
+        do(other_ref.at[0], own_ref.at[0], other_ref.at[1], own_ref.at[1])
+
+
+def first_kernel(start_ref, own_ref, other_ref, v_ref):
+    def do(*mats):
+        v = start_ref[...]
+        for m in mats:
+            v = pass_on(v, m[...])
+        v_ref[...] = v
+
+    in_order(own_ref, other_ref, do)
+
+
+def group_kernel(own_ref, other_ref, all_ref, mid_ref):
+    def times(left, right):
+        d = dot3(*halves(left), *halves(right))
+        return d * (1.0 / jnp.max(d, keepdims=True)[:, :1])
+
+    def do(*mats):
+        mid_ref[...] = times(mats[0][...], mats[1][...])
+        all_ref[...] = times(mid_ref[...], times(mats[2][...], mats[3][...]))
+
+    in_order(own_ref, other_ref, do)
+
+    @pl.when(lax.axis_index("tm") % 2 == 1)
+    def _():
+        mid_ref[...] = times(mid_ref[...], other_ref[1])
+
+
+def hop_kernel(v_ref, m_ref, out_ref):
+    out_ref[...] = pass_on(v_ref[...], m_ref[...])
+
+
+def small(kernel, name, outs, *args):
+    return pl.pallas_call(
+        kernel,
+        out_shape=tuple(jax.ShapeDtypeStruct(shape, F32) for shape in outs),
+        in_specs=[vmem()] * len(args),
+        out_specs=[vmem()] * len(outs),
+        compiler_params=pltpu.CompilerParams(vmem_limit_bytes=4 << 20),
+        name=name,
+    )(*args)
+
+
+def pack_kernel(x_hbm, out_ref, x_ref, sem):
+    copy = pltpu.make_async_copy(x_hbm, x_ref, sem)
     copy.start()
-    chip = lax.axis_index("tm") // 2
-    plane = chip // 2
-
-    def product(left, right):
-        d = dot3(*halves(left[...]), *halves(right[...]))
-        h, l = halves(d * (1.0 / jnp.max(d, keepdims=True)[:, :1]))
-        dh_ref[...] = h
-        dl_ref[...] = l
-
-    @pl.when(chip % 2 == 0)
-    def _():
-        product(own_ref, other_ref)
-
-    @pl.when(chip % 2 == 1)
-    def _():
-        product(other_ref, own_ref)
-
     copy.wait()
-    start = jnp.broadcast_to(unit(init_ref[...]), v_ref.shape)
-    start_ref[...] = start
-    v_ref[...] = unit(row_dot(start, dh_ref[...], dl_ref[...]))
-
-
-def plane_product(own, other, init):
-    states = own.shape[0]
-    out = jax.ShapeDtypeStruct
+    groups = out_ref.shape[0]
+    local = out_ref.shape[2]
+    low = lax.broadcasted_iota(jnp.int32, (local, 128), 1) < 64
+    for g in range(groups):
+        for u in range(2):
+            early = x_ref[u, :, g * 256 : g * 256 + 128]
+            late = x_ref[u, :, g * 256 + 128 : g * 256 + 256]
+            out_ref[g, 2 * u] = jnp.where(low, early, pltpu.roll(late, 64, 1))
+            out_ref[g, 2 * u + 1] = jnp.where(low, pltpu.roll(early, 64, 1), late)
+
+
+def pack(x, groups):
+    local = x.shape[1]
     return pl.pallas_call(
-        plane_kernel,
-        out_shape=(out((states, states), BF16),) * 2 + (out((8, states), F32),) * 2,
-        in_specs=[hbm()] + [vmem()] * 2,
-        out_specs=[vmem()] * 4,
-        scratch_shapes=[pltpu.VMEM((1, states), F32), pltpu.SemaphoreType.DMA],
+        pack_kernel,
+        out_shape=jax.ShapeDtypeStruct((groups, 4, local, 128), F32),
+        in_specs=[hbm()],
+        out_specs=vmem(),
+        scratch_shapes=[pltpu.VMEM(x.shape, F32), pltpu.SemaphoreType.DMA],
         compiler_params=pltpu.CompilerParams(vmem_limit_bytes=4 << 20),
-        name="plane",
-    )(pinned(init[None, :]), own, other)
-
-
-def hop_kernel(v_ref, dh_ref, dl_ref, out_ref):
-    out_ref[...] = unit(row_dot(v_ref[...], dh_ref[...], dl_ref[...]))
-
-
-def hop(v, dh, dl):
-    return pl.pallas_call(
-        hop_kernel,
-        out_shape=jax.ShapeDtypeStruct(v.shape, F32),
-        in_specs=[vmem()] * 3,
-        out_specs=vmem(),
-        compiler_params=pltpu.CompilerParams(vmem_limit_bytes=4 << 20),
-        name="hop",
-    )(v, dh, dl)
-
-
-def frames_kernel(
-    frames,
-    planes,
-    lengths_hbm,
-    *refs,
-):
-    v_refs = refs[: planes - 1]
-    start_ref, other_ref, pre_ref, e_ref, top_ref, th_ref, tl_ref, kept_ref, sent_ref, gain_ref, *scratch = refs[
-        planes - 1 :
+        name="pack",
+    )(pinned(x))
+
+
+def frames_kernel(frames, lengths_hbm, *refs):
+    start_ref, *v_refs = refs[:-13]
+    other_ref, mid_ref, pre_ref, e_ref, top_ref, th_ref, tl_ref, kept_ref, sent_ref, gain_ref, *scratch = refs[
+        len(v_refs) + 1 :
     ]
     alpha_scr, lengths_ref, sem = scratch
     copy = pltpu.make_async_copy(lengths_hbm, lengths_ref, sem)
@@ -339,14 +369,12 @@
     blocks = half // SUB
     subs = 2 * blocks
     index = lax.axis_index("tm")
-    core = index % 2
-    chip = index // 2
+    utt, slots = place(half)
     v = start_ref[...]
-    for g in range(1, planes):
-        v = jnp.where(chip // 2 == g, v_refs[g - 1][...], v)
-    oh, ol = halves(other_ref[...])
-    v = jnp.where(chip % 2 == 1, unit(row_dot(v, oh, ol)), v)
-    mid = unit(row_dot(v, pre_ref[0, blocks - 1, 0], pre_ref[0, blocks - 1, 1]))
+    for g, ref in enumerate(v_refs):
+        v = jnp.where(index // 4 == g + 1, ref[...], v)
+    mid = unit(pass_on(v, mid_ref[...]))
+    v = unit(jnp.where(index % 2 == 1, pass_on(v, other_ref[0]), v))
     rows = [v[0:1]]
     for j in range(blocks - 1):
         rows.append(row_dot(v, pre_ref[0, j, 0], pre_ref[0, j, 1])[0:1])
@@ -359,7 +387,7 @@
     sub = lax.broadcasted_iota(jnp.int32, (subs, 128), 0)
     gains = jnp.zeros((subs, 128), F32)
     copy.wait()
-    alive = lengths_ref[core] - chip * frames
+    alive = [lengths_ref[utt] - slot for slot in slots]
     tiles = range(states // 128)
     for r in range(SUB):
         every = pl.ds(r, subs, stride=SUB)
@@ -368,30 +396,32 @@
         alpha = x / total
         for k in tiles:
             alpha_scr[k, every, :] = alpha[:, k * 128 : (k + 1) * 128]
-        live = sub * SUB + r < alive
+        live = (sub % blocks) * SUB + r < jnp.where(sub < blocks, alive[0], alive[1])
         gain = jnp.where(live, jnp.log(total) + top_ref[every, :], 0.0)
         gains = jnp.where(lane % SUB == r, gain, gains)
-    end = pl.ds(jnp.clip(alive - 1, 0, frames - 1), 1)
-    for which, ref in ((core, kept_ref), (1 - core, sent_ref)):
+    for which, ref in ((utt, kept_ref), (1 - utt, sent_ref)):
         at = pl.multiple_of(which * half, half)
-        frame = at + lax.broadcasted_iota(jnp.int32, (half, 128), 0)
+        left = jnp.where(which == 0, alive[0], alive[1])
+        frame = lax.broadcasted_iota(jnp.int32, (half, 128), 0)
+        end = pl.ds(at + jnp.clip(left - 1, 0, half - 1), 1)
+        before = jnp.where(which == 0, v[0:1], mid[0:1])
         for k in tiles:
             cut = slice(k * 128, (k + 1) * 128)
-            final = jnp.where(alive > 0, alpha_scr[k, end, :], v[0:1, cut])
-            ref[0:half, cut] = jnp.log(jnp.where(frame < alive, alpha_scr[k, pl.ds(at, half), :], final))
+            final = jnp.where(left > 0, alpha_scr[k, end, :], before[:, cut])
+            ref[0:half, cut] = jnp.log(jnp.where(frame < left, alpha_scr[k, pl.ds(at, half), :], final))
     picked = jnp.where(lane // SUB == sub % blocks, gains, 0.0)
     lines = [jnp.sum(picked[k * blocks : (k + 1) * blocks], axis=0, keepdims=True) for k in range(2)]
-    gain_ref[...] = jnp.where(core == 0, lines[0], lines[1])
-    line = jnp.where(core == 0, lines[1], lines[0])
+    gain_ref[...] = jnp.where(utt == 0, lines[0], lines[1])
+    line = jnp.where(utt == 0, lines[1], lines[0])
     sent_ref[half : half + 8, :] = jnp.concatenate([jnp.broadcast_to(line, (8, 128))] * (states // 128), axis=1)
 
 
-def frames_pass(lengths, vs, start, other, pre, e, top, th, tl):
+def frames_pass(lengths, vs, other, mid, pre, e, top, th, tl):
     frames, states = top.shape[0], th.shape[0]
     half = frames // 2
     out = jax.ShapeDtypeStruct
     return pl.pallas_call(
-        functools.partial(frames_kernel, frames, len(vs) + 1),
+        functools.partial(frames_kernel, frames),
         out_shape=(out((half, states), F32), out((half + 8, states), F32), out((1, 128), F32)),
         in_specs=[hbm()] + [vmem()] * (len(vs) + 7),
         out_specs=[vmem()] * 3,
@@ -402,18 +432,18 @@
         ],
         compiler_params=pltpu.CompilerParams(vmem_limit_bytes=6 << 20),
         name="frames",
-    )(pinned(lengths), *vs, start, other, pre, e, top, th, tl)
+    )(pinned(lengths), *vs, other, mid, pre, e, top, th, tl)
 
 
 def join_kernel(kept_ref, gain_ref, got_ref, log_ref, out_gain_ref):
     half = kept_ref.shape[0]
-    core = lax.axis_index("tm") % 2
-    log_ref[core] = kept_ref[...]
-    log_ref[1 - core] = got_ref[0:half, :]
+    utt = (lax.axis_index("tm") // 2) % 2
+    log_ref[utt] = kept_ref[...]
+    log_ref[1 - utt] = got_ref[0:half, :]
     own = gain_ref[0:1, 0:half]
     got = got_ref[half : half + 1, 0:half]
-    out_gain_ref[0:1, :] = jnp.where(core == 0, own, got)
-    out_gain_ref[1:2, :] = jnp.where(core == 0, got, own)
+    out_gain_ref[0:1, :] = jnp.where(utt == 0, own, got)
+    out_gain_ref[1:2, :] = jnp.where(utt == 0, got, own)
 
 
 def join(kept, gain, got):
@@ -430,25 +460,32 @@
 
 
 def shards(size, loglik, trans_weight, block_mask, init_weight, lengths, pdf_map):
-    utts, total, local = loglik.shape
-    chips = size // 2
-    frames = total // chips
-    planes = chips // 2
-    x = jnp.transpose(loglik, (0, 2, 1)).reshape(utts, local, chips, frames)
-    x = jnp.transpose(x, (2, 0, 1, 3)).reshape(size, local, frames)
+    local = loglik.shape[2]
+    groups = size // 4
+    x = pack(jnp.transpose(loglik, (0, 2, 1)), groups)
+    frames = x.shape[3]
+    x = x.reshape(size, local, frames)
     cols = lax.all_to_all(x, "tm", 0, 0, tiled=True).reshape(size * local, frames)
-    chip, pre, e, top, th, tl = transfer(cols, trans_weight, block_mask, lengths, pdf_map)
-    other = lax.ppermute(chip, "tm", [(i, i ^ 2) for i in range(size)])
-    dh, dl, v, start = plane_product(chip, other, init_weight)
-    vs = []
-    for g in range(1, planes):
-        got = lax.ppermute(v, "tm", [(4 * (g - 1) + i, 4 * g + i) for i in range(4)])
-        vs.append(got)
-        if g < planes - 1:
-            v = hop(got, dh, dl)
-    kept, sent, gain = frames_pass(lengths, vs, start, other, pre, e, top, th, tl)
-    got = lax.ppermute(sent, "tm", [(i, i ^ 1) for i in range(size)])
+    own, pre, e, top, th, tl, start = transfer(cols, trans_weight, block_mask, lengths, pdf_map, init_weight)
+    other = lax.ppermute(own, "tm", [(i, i ^ 1) for i in range(size)])
+    (v,) = small(first_kernel, "first", [start.shape], start, own, other)
+    square = own.shape[1:]
+    whole, mid = small(group_kernel, "group", [square, square], own, other)
+    vs = [start]
+    for g in range(1, groups):
+        pairs = [(i, 4 * pair_of(i // 4, g, groups) + i % 4) for i in range(size)]
+        vs.append(lax.ppermute(v, "tm", pairs))
+        if g < groups - 1:
+            (v,) = small(hop_kernel, "hop", [v.shape], vs[-1], whole)
+    kept, sent, gain = frames_pass(lengths, vs, other, mid, pre, e, top, th, tl)
+    got = lax.ppermute(sent, "tm", [(i, i ^ 2) for i in range(size)])
     return join(kept, gain, got)
+
+
+def pair_of(group, turn, groups):
+    if turn % 2:
+        return group ^ 1
+    return (group - 1 if group % 2 == 0 else group + 1) % groups
 
 
 def solution(mesh):

time: 64.4 us -> 62.7 us (0.974)
  the two profiles are of different devices: /device:TPU:25 before, /device:TPU:0 now
where the time goes in v4:
time: 62.7 us; the launch traced here: 62.4 us
  Pallas kernels  26.5 us (42%)
  blocking collectives  17.2 us (27%)
  waiting for transfers between devices  16.4 us (26%)
  starting transfers between devices  1.65 us (3%)
  between operations  0.68 us (1%)
    pallas_call x1, Pallas kernels, transfer(): pl.pallas_call(functools.partial(transfer_kernel, frames), out_shape=(out...  19.4 us
    all_to_all x1, blocking collectives, shards(): lax.all_to_all(x, 'tm', 0, 0, tiled=True).reshape(size * local, frames)  17.2 us
    ppermute x3, waiting for transfers between devices, shards(): vs.append(lax.ppermute(v, 'tm', pairs))  10.3 us
    ppermute x1, waiting for transfers between devices, shards(): got = lax.ppermute(sent, 'tm', [(i, i ^ 2) for i in range(size)])  4.19 us
    pallas_call x1, Pallas kernels, frames_pass(): pl.pallas_call(functools.partial(frames_kernel, frames), out_shape=(out((...  3.31 us
    pallas_call x4, Pallas kernels, small(): pl.pallas_call(kernel, out_shape=tuple((jax.ShapeDtypeStruct(shape, F32)...  1.93 us
    ppermute x1, waiting for transfers between devices, shards(): other = lax.ppermute(own, 'tm', [(i, i ^ 1) for i in range(size)])  1.9 us
    ppermute x3, starting transfers between devices, shards(): vs.append(lax.ppermute(v, 'tm', pairs))  1.35 us
  transfers between devices with their start and end apart: 5, of which 5 were waited for; matrix products, arithmetic and copies ran while one was open for 0% of the time, Pallas kernels for 2%

profile of v4, /device:TPU:0, one launch (start us, length us, event | category | flops | bytes accessed | tf_op | source)
XLA Modules:
  0.0 62.4 jit_solution(15935497645242675861)
XLA Ops:
  0.6 1.1 %pack.1 = f32[4,4,32,128]{3,2,1,0:T(8,128)S(1)} custom-call(f32[2,32,1024]{2,1,0:T(8,128)} %bitcast.7), custom_call_target="tpu_custom_call" | custom-call | tf_op jit(solution)/shard_map/pack/pallas_call | solution.py:348
  1.7 17.2 %all_to_all.5 = f32[16,32,128]{2,1,0:T(8,128)S(1)} all-to-all(f32[16,32,128]{2,1,0:T(8,128)S(1)} %bitcast.6), channel_id=1, replica_groups=mesh['groups'=2,'tm'=16] {'tm'}, dimensions={0} | all-to-all | bytes 524288 | tf_op jit(solution)/shard_map/all_to_all | solution.py:468
  19.0 19.4 %transfer.1 = (f32[2,256,256]{2,1,0:T(8,128)S(1)}, bf16[2,8,2,256,256]{4,3,2,1,0:T(8,128)(2,1)S(1)}, f32[2,128,128]{2,1,0:T(8,128)S(1)}, f32[128,128]{1,0:T(8,12...) custom-call(s32[2]{0:T(128)} %lengths_hbm.3, s32[4,4]{1,0:T(4,128)} %mask_hbm.1, ...), custom_call_target="tpu_custom_call" | custom-call | tf_op jit(solution)/shard_map/transfer/pallas_call | solution.py:233
  38.4 0.1 collective-permute-start
  38.5 1.9 %collective-permute-done.other_ref.refs_4_ = f32[2,256,256]{2,1,0:T(8,128)S(1)} collective-permute-done((f32[2,256,256]{2,1,0:T(8,128)S(1)}, f32[2,256,256]{2,1,0:T(8,128)S(1)}, u32[]{:S(2)}, u32[]{:S(2)}) %collective-permute-start) | collective-permute-done | bytes 524320 | tf_op jit(solution)/shard_map/ppermute | solution.py:470
  40.4 0.5 first.1
  40.9 0.4 collective-permute-start.1
  41.3 1.1 %group.1 = (f32[256,256]{1,0:T(8,128)S(1)}, f32[256,256]{1,0:T(8,128)S(1)}) custom-call(f32[2,256,256]{2,1,0:T(8,128)S(1)} %get-tuple-element.15.own_ref, f32[2,256,256]{2,1,0:T(8,128)S(1)} %collective-permute-done.other_ref.refs_4_), custom_call_target="tpu_custom_call" | custom-call | tf_op jit(solution)/shard_map/group/pallas_call | solution.py:321
  42.4 2.2 %collective-permute-done.1.v_ref.refs_1_ = f32[8,256]{1,0:T(8,128)S(1)} collective-permute-done((f32[8,256]{1,0:T(8,128)S(1)}, f32[8,256]{1,0:T(8,128)S(1)}, u32[]{:S(2)}, u32[]{:S(2)}) %collective-permute-start.1) | collective-permute-done | bytes 8224 | tf_op jit(solution)/shard_map/ppermute | solution.py:477
  44.6 0.1 hop.2
  44.7 0.9 %collective-permute-start.2 = (f32[8,256]{1,0:T(8,128)S(1)}, f32[8,256]{1,0:T(8,128)S(1)}, u32[]{:S(2)}, u32[]{:S(2)}) collective-permute-start(f32[8,256]{1,0:T(8,128)S(1)} %hop.2), channel_id=1, source_target_pairs={{0,12},{1,13},{2,14},{3,15},{4,8},{5,9},{6,10},{7,11},{8,4},{9,5},... | collective-permute-start | bytes 24584 | tf_op jit(solution)/shard_map/ppermute | solution.py:477
  45.7 4.5 %collective-permute-done.2.v_ref.refs_2_ = f32[8,256]{1,0:T(8,128)S(1)} collective-permute-done((f32[8,256]{1,0:T(8,128)S(1)}, f32[8,256]{1,0:T(8,128)S(1)}, u32[]{:S(2)}, u32[]{:S(2)}) %collective-permute-start.2) | collective-permute-done | bytes 8224 | tf_op jit(solution)/shard_map/ppermute | solution.py:477
  50.2 0.1 hop.3
  50.4 0.0 collective-permute-start.3
  50.4 3.7 %collective-permute-done.3.refs_3_ = f32[8,256]{1,0:T(8,128)S(1)} collective-permute-done((f32[8,256]{1,0:T(8,128)S(1)}, f32[8,256]{1,0:T(8,128)S(1)}, u32[]{:S(2)}, u32[]{:S(2)}) %collective-permute-start.3) | collective-permute-done | bytes 8224 | tf_op jit(solution)/shard_map/ppermute | solution.py:477
  54.0 3.3 %frames.1 = (f32[64,256]{1,0:T(8,128)S(1)}, f32[72,256]{1,0:T(8,128)S(1)}, f32[1,128]{1,0:T(1,128)S(1)}) custom-call(s32[2]{0:T(128)} %lengths_hbm.3, f32[8,256]{1,0:T(8,128)S(1)} %get-tuple-element.14.start_ref.refs_0_, f32[8,256]{1,0:T(8,128)S(1)} %collective-permute-done.1.v_ref.refs_1_, f32[8,256]{1,0:T(8,128)S(1)} %collective-permute-done.2.v_ref.refs_2_, ...), custom_call_target="tpu_custom_call" | custom-call | tf_op jit(solution)/shard_map/frames/pallas_call | solution.py:423
  57.4 0.2 collective-permute-start.4
  57.6 4.2 %collective-permute-done.4.got_ref = f32[72,256]{1,0:T(8,128)S(1)} collective-permute-done((f32[72,256]{1,0:T(8,128)S(1)}, f32[72,256]{1,0:T(8,128)S(1)}, u32[]{:S(2)}, u32[]{:S(2)}) %collective-permute-start.4) | collective-permute-done | bytes 73760 | tf_op jit(solution)/shard_map/ppermute | solution.py:481
  61.8 0.7 %join.1 = (f32[2,64,256]{2,1,0:T(8,128)}, f32[2,64]{1,0:T(2,128)}) custom-call(f32[64,256]{1,0:T(8,128)S(1)} %get-tuple-element.23.kept_ref, f32[1,128]{1,0:T(1,128)S(1)} %get-tuple-element.24.gain_ref, f32[72,256]{1,0:T(8,128)S(1)} %collective-permute-done.4.got_ref), custom_call_target="tpu_custom_call" | custom-call | tf_op jit(solution)/shard_map/join/pallas_call | solution.py:452
Async XLA Ops:
  38.4 2.0 %collective-permute-start = (f32[2,256,256]{2,1,0:T(8,128)S(1)}, f32[2,256,256]{2,1,0:T(8,128)S(1)}, u32[]{:S(2)}, u32[]{:S(2)}) collective-permute-start(f32[2,256,256]{2,1,0:T(8,128)S(1)} %get-tuple-element.15.own_ref), channel_id=1, source_target_pairs={{0,1},{1,0},{2,3},{3,2},{4,5},{5,4},{6,7},{7,6},{8,9},{9,8},{10,11... | collective-permute-start | bytes 1572872 | tf_op jit(solution)/shard_map/ppermute | solution.py:470
  40.9 3.7 %collective-permute-start.1 = (f32[8,256]{1,0:T(8,128)S(1)}, f32[8,256]{1,0:T(8,128)S(1)}, u32[]{:S(2)}, u32[]{:S(2)}) collective-permute-start(f32[8,256]{1,0:T(8,128)S(1)} %first.1), channel_id=1, source_target_pairs={{0,4},{1,5},{2,6},{3,7},{4,0},{5,1},{6,2},{7,3},{8,12},{9,13},{10,... | collective-permute-start | bytes 24584 | tf_op jit(solution)/shard_map/ppermute | solution.py:477
  44.7 5.5 %collective-permute-start.2 = (f32[8,256]{1,0:T(8,128)S(1)}, f32[8,256]{1,0:T(8,128)S(1)}, u32[]{:S(2)}, u32[]{:S(2)}) collective-permute-start(f32[8,256]{1,0:T(8,128)S(1)} %hop.2), channel_id=1, source_target_pairs={{0,12},{1,13},{2,14},{3,15},{4,8},{5,9},{6,10},{7,11},{8,4},{9,5},... | collective-permute-start | bytes 24584 | tf_op jit(solution)/shard_map/ppermute | solution.py:477
  50.4 3.7 %collective-permute-start.3 = (f32[8,256]{1,0:T(8,128)S(1)}, f32[8,256]{1,0:T(8,128)S(1)}, u32[]{:S(2)}, u32[]{:S(2)}) collective-permute-start(f32[8,256]{1,0:T(8,128)S(1)} %hop.3), channel_id=1, source_target_pairs={{0,4},{1,5},{2,6},{3,7},{4,0},{5,1},{6,2},{7,3},{8,12},{9,13},{10,... | collective-permute-start | bytes 24584 | tf_op jit(solution)/shard_map/ppermute | solution.py:477
  57.4 4.4 %collective-permute-start.4 = (f32[72,256]{1,0:T(8,128)S(1)}, f32[72,256]{1,0:T(8,128)S(1)}, u32[]{:S(2)}, u32[]{:S(2)}) collective-permute-start(f32[72,256]{1,0:T(8,128)S(1)} %get-tuple-element.25), channel_id=1, source_target_pairs={{0,2},{1,3},{2,0},{3,1},{4,6},{5,7},{6,4},{7,5},{8,10},{9,11},{10,... | collective-permute-start | bytes 221192 | tf_op jit(solution)/shard_map/ppermute | solution.py:481

commit v5 on v4

--- a/solution.py
+++ b/solution.py
@@ -156,20 +156,23 @@
                 pltpu.matmul_acc_lhs(accs[1][m], bh[sl, :], 0)
                 pltpu.matmul_acc_lhs(accs[1][m], bl[sl, :], None)
 
-        def post(k, s, peak):
+        def post(k, s, peak, look):
             mh, ml = mats[k]
-            er = e_scr[pl.ds(s + k * half, 1), :] * (1.0 / jnp.max(peak.astype(F32), keepdims=True)[:, :1])
-            base = jnp.where(s < alive[k], 0, states)
+            er = e_scr[pl.ds(s + k * half, 1), :]
+            if not look:
+                er = er * (1.0 / jnp.max(peak.astype(F32), keepdims=True)[:, :1])
+            live = s < alive[k]
             new = None
             for m in range(2):
                 x = pltpu.matmul_pop(accs[k][m]) * er
                 h, l = halves(x)
-                at = pl.multiple_of(base + m * rows, rows)
-                mh[pl.ds(at, rows), :] = h
-                ml[pl.ds(at, rows), :] = l
-                y = jnp.max(h.reshape(rows // 16, 16, states), axis=0)
-                new = y if new is None else jnp.maximum(new, y)
-            return new
+                sl = pl.ds(m * rows, rows)
+                mh[sl, :] = jnp.where(live, h, mh[sl, :])
+                ml[sl, :] = jnp.where(live, l, ml[sl, :])
+                if look:
+                    y = jnp.max(h.reshape(rows // 16, 16, states), axis=0)
+                    new = y if new is None else jnp.maximum(new, y)
+            return new if look else peak
 
         def keep(j):
             for k in range(2):
@@ -181,24 +184,25 @@
         issue_a(0)
         one = jnp.ones((16, states), BF16)
 
-        def step(s, peaks, last=False):
+        def step(s, r, peaks, last=False):
             pa, pb = peaks
+            odd = r % 2 == 1
             issue_b()
-            pa = post(0, s, pa)
+            pa = post(0, s, pa, odd)
             if not last:
                 issue_a(None)
-            pb = post(1, s, pb)
+            pb = post(1, s, pb, not odd)
             return pa, pb
 
         def block(j, peaks):
             for r in range(1, SUB):
-                peaks = step(j * SUB + r, peaks)
+                peaks = step(j * SUB + r, r, peaks)
             keep(j)
-            return step(j * SUB + SUB, peaks)
+            return step(j * SUB + SUB, SUB, peaks)
 
         peaks = lax.fori_loop(0, blocks - 1, block, (one, one))
         for r in range(1, SUB):
-            peaks = step((blocks - 1) * SUB + r, peaks, r == SUB - 1)
+            peaks = step((blocks - 1) * SUB + r, r, peaks, r == SUB - 1)
         keep(blocks - 1)
         for i, (mh, ml) in enumerate(mats):
             mats_ref[i] = mh[0:states, :].astype(F32) + ml[0:states, :].astype(F32)
@@ -245,7 +249,7 @@
         out_specs=[vmem()] * 7,
         scratch_shapes=[pltpu.VMEM((frames, states), F32)] * 2
         + [pltpu.VMEM((states, states), F32)]
-        + [pltpu.VMEM((2 * states, states), BF16)] * 4
+        + [pltpu.VMEM((states, states), BF16)] * 4
         + [
             pltpu.SMEM(lengths.shape, jnp.int32),
             pltpu.SMEM(mask.shape, jnp.int32),
@@ -373,15 +377,17 @@
     v = start_ref[...]
     for g, ref in enumerate(v_refs):
         v = jnp.where(index // 4 == g + 1, ref[...], v)
-    mid = unit(pass_on(v, mid_ref[...]))
-    v = unit(jnp.where(index % 2 == 1, pass_on(v, other_ref[0]), v))
+    mid = pass_on(v, mid_ref[...])
+    v = jnp.where(index % 2 == 1, pass_on(v, other_ref[0]), v)
     rows = [v[0:1]]
     for j in range(blocks - 1):
         rows.append(row_dot(v, pre_ref[0, j, 0], pre_ref[0, j, 1])[0:1])
     rows.append(mid[0:1])
     for j in range(blocks - 1):
         rows.append(row_dot(mid, pre_ref[1, j, 0], pre_ref[1, j, 1])[0:1])
-    alpha = unit(jnp.concatenate(rows, axis=0))
+    x = jnp.concatenate(rows, axis=0)
+    total = jnp.sum(x, axis=1, keepdims=True)
+    v, mid = unit(v), unit(mid)
     th, tl = th_ref[...], tl_ref[...]
     lane = lax.broadcasted_iota(jnp.int32, (subs, 128), 1)
     sub = lax.broadcasted_iota(jnp.int32, (subs, 128), 0)
@@ -391,9 +397,10 @@
     tiles = range(states // 128)
     for r in range(SUB):
         every = pl.ds(r, subs, stride=SUB)
-        x = row_dot(alpha, th, tl) * jnp.concatenate([e_ref[k, every, :] for k in tiles], axis=1)
+        factor = jnp.concatenate([e_ref[k, every, :] for k in tiles], axis=1) * (1.0 / total)
+        x = row_dot(x, th, tl) * factor
         total = jnp.sum(x, axis=1, keepdims=True)
-        alpha = x / total
+        alpha = x * (1.0 / total)
         for k in tiles:
             alpha_scr[k, every, :] = alpha[:, k * 128 : (k + 1) * 128]
         live = (sub % blocks) * SUB + r < jnp.where(sub < blocks, alive[0], alive[1])
@@ -473,7 +480,7 @@
     whole, mid = small(group_kernel, "group", [square, square], own, other)
     vs = [start]
     for g in range(1, groups):
-        pairs = [(i, 4 * pair_of(i // 4, g, groups) + i % 4) for i in range(size)]
+        pairs = [(i, partner(i, g, groups)) for i in range(size)]
         vs.append(lax.ppermute(v, "tm", pairs))
         if g < groups - 1:
             (v,) = small(hop_kernel, "hop", [v.shape], vs[-1], whole)
@@ -482,10 +489,12 @@
     return join(kept, gain, got)
 
 
-def pair_of(group, turn, groups):
-    if turn % 2:
-        return group ^ 1
-    return (group - 1 if group % 2 == 0 else group + 1) % groups
+def partner(index, turn, groups):
+    group = index // 4
+    other = group ^ 1 if turn % 2 else (group - 1 if group % 2 == 0 else group + 1)
+    if 0 <= other < groups:
+        return 4 * other + index % 4
+    return index ^ 2
 
 
 def solution(mesh):

time: 62.7 us -> 57.4 us (0.915)
  Pallas kernels: 26.5 us -> 23 us
  waiting for transfers between devices: 16.4 us -> 15 us
    pallas_call x1, Pallas kernels: 19.4 us -> 16.7 us  [transfer(): pl.pallas_call(functools.partial(transfer_kernel, frames), out_shape=(out...]
    ppermute x3, waiting for transfers between devices: 10.3 us -> 8.95 us  [shards(): vs.append(lax.ppermute(v, 'tm', pairs))]
    pallas_call x1, Pallas kernels: 3.31 us -> 2.65 us  [frames_pass(): pl.pallas_call(functools.partial(frames_kernel, frames), out_shape=(out((...]
where the time goes in v5:
time: 57.4 us; the launch traced here: 57.2 us
  Pallas kernels  23 us (40%)
  blocking collectives  17.2 us (30%)
  waiting for transfers between devices  15 us (26%)
  starting transfers between devices  1.24 us (2%)
  between operations  0.68 us (1%)
    all_to_all x1, blocking collectives, shards(): lax.all_to_all(x, 'tm', 0, 0, tiled=True).reshape(size * local, frames)  17.2 us
    pallas_call x1, Pallas kernels, transfer(): pl.pallas_call(functools.partial(transfer_kernel, frames), out_shape=(out...  16.7 us
    ppermute x3, waiting for transfers between devices, shards(): vs.append(lax.ppermute(v, 'tm', pairs))  8.95 us
    ppermute x1, waiting for transfers between devices, shards(): got = lax.ppermute(sent, 'tm', [(i, i ^ 2) for i in range(size)])  4.18 us
    pallas_call x1, Pallas kernels, frames_pass(): pl.pallas_call(functools.partial(frames_kernel, frames), out_shape=(out((...  2.65 us
    pallas_call x4, Pallas kernels, small(): pl.pallas_call(kernel, out_shape=tuple((jax.ShapeDtypeStruct(shape, F32)...  1.93 us
    ppermute x1, waiting for transfers between devices, shards(): other = lax.ppermute(own, 'tm', [(i, i ^ 1) for i in range(size)])  1.9 us
  transfers between devices with their start and end apart: 5, of which 5 were waited for; matrix products, arithmetic and copies ran while one was open for 0% of the time, Pallas kernels for 2%

profile of v5, /device:TPU:0, one launch (start us, length us, event | category | flops | bytes accessed | tf_op | source)
XLA Modules:
  0.0 57.2 jit_solution(5892999064092529346)
XLA Ops:
  0.6 1.1 %pack.1 = f32[4,4,32,128]{3,2,1,0:T(8,128)S(1)} custom-call(f32[2,32,1024]{2,1,0:T(8,128)} %bitcast.7), custom_call_target="tpu_custom_call" | custom-call | tf_op jit(solution)/shard_map/pack/pallas_call | solution.py:352
  1.7 17.2 %all_to_all.5 = f32[16,32,128]{2,1,0:T(8,128)S(1)} all-to-all(f32[16,32,128]{2,1,0:T(8,128)S(1)} %bitcast.6), channel_id=1, replica_groups=mesh['groups'=2,'tm'=16] {'tm'}, dimensions={0} | all-to-all | bytes 524288 | tf_op jit(solution)/shard_map/all_to_all | solution.py:475
  19.0 16.7 %transfer.1 = (f32[2,256,256]{2,1,0:T(8,128)S(1)}, bf16[2,8,2,256,256]{4,3,2,1,0:T(8,128)(2,1)S(1)}, f32[2,128,128]{2,1,0:T(8,128)S(1)}, f32[128,128]{1,0:T(8,12...) custom-call(s32[2]{0:T(128)} %lengths_hbm.3, s32[4,4]{1,0:T(4,128)} %mask_hbm.1, ...), custom_call_target="tpu_custom_call" | custom-call | tf_op jit(solution)/shard_map/transfer/pallas_call | solution.py:237
  35.7 0.1 collective-permute-start
  35.7 1.9 %collective-permute-done.other_ref.refs_4_ = f32[2,256,256]{2,1,0:T(8,128)S(1)} collective-permute-done((f32[2,256,256]{2,1,0:T(8,128)S(1)}, f32[2,256,256]{2,1,0:T(8,128)S(1)}, u32[]{:S(2)}, u32[]{:S(2)}) %collective-permute-start) | collective-permute-done | bytes 524320 | tf_op jit(solution)/shard_map/ppermute | solution.py:477
  37.6 0.5 first.1
  38.1 0.4 collective-permute-start.1
  38.5 1.1 %group.1 = (f32[256,256]{1,0:T(8,128)S(1)}, f32[256,256]{1,0:T(8,128)S(1)}) custom-call(f32[2,256,256]{2,1,0:T(8,128)S(1)} %get-tuple-element.15.own_ref, f32[2,256,256]{2,1,0:T(8,128)S(1)} %collective-permute-done.other_ref.refs_4_), custom_call_target="tpu_custom_call" | custom-call | tf_op jit(solution)/shard_map/group/pallas_call | solution.py:325
  39.7 2.2 %collective-permute-done.1.v_ref.refs_1_ = f32[8,256]{1,0:T(8,128)S(1)} collective-permute-done((f32[8,256]{1,0:T(8,128)S(1)}, f32[8,256]{1,0:T(8,128)S(1)}, u32[]{:S(2)}, u32[]{:S(2)}) %collective-permute-start.1) | collective-permute-done | bytes 8224 | tf_op jit(solution)/shard_map/ppermute | solution.py:484
  41.8 0.1 hop.2
  42.0 0.2 collective-permute-start.2
  42.2 3.5 %collective-permute-done.2.v_ref.refs_2_ = f32[8,256]{1,0:T(8,128)S(1)} collective-permute-done((f32[8,256]{1,0:T(8,128)S(1)}, f32[8,256]{1,0:T(8,128)S(1)}, u32[]{:S(2)}, u32[]{:S(2)}) %collective-permute-start.2) | collective-permute-done | bytes 8224 | tf_op jit(solution)/shard_map/ppermute | solution.py:484
  45.6 0.1 hop.3
  45.8 0.4 collective-permute-start.3
  46.1 3.3 %collective-permute-done.3.refs_3_ = f32[8,256]{1,0:T(8,128)S(1)} collective-permute-done((f32[8,256]{1,0:T(8,128)S(1)}, f32[8,256]{1,0:T(8,128)S(1)}, u32[]{:S(2)}, u32[]{:S(2)}) %collective-permute-start.3) | collective-permute-done | bytes 8224 | tf_op jit(solution)/shard_map/ppermute | solution.py:484
  49.5 2.6 %frames.1 = (f32[64,256]{1,0:T(8,128)S(1)}, f32[72,256]{1,0:T(8,128)S(1)}, f32[1,128]{1,0:T(1,128)S(1)}) custom-call(s32[2]{0:T(128)} %lengths_hbm.3, f32[8,256]{1,0:T(8,128)S(1)} %get-tuple-element.14.start_ref.refs_0_, f32[8,256]{1,0:T(8,128)S(1)} %collective-permute-done.1.v_ref.refs_1_, f32[8,256]{1,0:T(8,128)S(1)} %collective-permute-done.2.v_ref.refs_2_, ...), custom_call_target="tpu_custom_call" | custom-call | tf_op jit(solution)/shard_map/frames/pallas_call | solution.py:430
  52.1 0.2 collective-permute-start.4
  52.3 4.2 %collective-permute-done.4.got_ref = f32[72,256]{1,0:T(8,128)S(1)} collective-permute-done((f32[72,256]{1,0:T(8,128)S(1)}, f32[72,256]{1,0:T(8,128)S(1)}, u32[]{:S(2)}, u32[]{:S(2)}) %collective-permute-start.4) | collective-permute-done | bytes 73760 | tf_op jit(solution)/shard_map/ppermute | solution.py:488
  56.5 0.7 %join.1 = (f32[2,64,256]{2,1,0:T(8,128)}, f32[2,64]{1,0:T(2,128)}) custom-call(f32[64,256]{1,0:T(8,128)S(1)} %get-tuple-element.23.kept_ref, f32[1,128]{1,0:T(1,128)S(1)} %get-tuple-element.24.gain_ref, f32[72,256]{1,0:T(8,128)S(1)} %collective-permute-done.4.got_ref), custom_call_target="tpu_custom_call" | custom-call | tf_op jit(solution)/shard_map/join/pallas_call | solution.py:459
Async XLA Ops:
  35.7 2.0 %collective-permute-start = (f32[2,256,256]{2,1,0:T(8,128)S(1)}, f32[2,256,256]{2,1,0:T(8,128)S(1)}, u32[]{:S(2)}, u32[]{:S(2)}) collective-permute-start(f32[2,256,256]{2,1,0:T(8,128)S(1)} %get-tuple-element.15.own_ref), channel_id=1, source_target_pairs={{0,1},{1,0},{2,3},{3,2},{4,5},{5,4},{6,7},{7,6},{8,9},{9,8},{10,11... | collective-permute-start | bytes 1572872 | tf_op jit(solution)/shard_map/ppermute | solution.py:477
  38.1 3.7 %collective-permute-start.1 = (f32[8,256]{1,0:T(8,128)S(1)}, f32[8,256]{1,0:T(8,128)S(1)}, u32[]{:S(2)}, u32[]{:S(2)}) collective-permute-start(f32[8,256]{1,0:T(8,128)S(1)} %first.1), channel_id=1, source_target_pairs={{0,4},{1,5},{2,6},{3,7},{4,0},{5,1},{6,2},{7,3},{8,12},{9,13},{10,... | collective-permute-start | bytes 24584 | tf_op jit(solution)/shard_map/ppermute | solution.py:484
  42.0 3.7 %collective-permute-start.2 = (f32[8,256]{1,0:T(8,128)S(1)}, f32[8,256]{1,0:T(8,128)S(1)}, u32[]{:S(2)}, u32[]{:S(2)}) collective-permute-start(f32[8,256]{1,0:T(8,128)S(1)} %hop.2), channel_id=1, source_target_pairs={{0,2},{1,3},{2,0},{3,1},{4,8},{5,9},{6,10},{7,11},{8,4},{9,5},{10,... | collective-permute-start | bytes 24584 | tf_op jit(solution)/shard_map/ppermute | solution.py:484
  45.8 3.7 %collective-permute-start.3 = (f32[8,256]{1,0:T(8,128)S(1)}, f32[8,256]{1,0:T(8,128)S(1)}, u32[]{:S(2)}, u32[]{:S(2)}) collective-permute-start(f32[8,256]{1,0:T(8,128)S(1)} %hop.3), channel_id=1, source_target_pairs={{0,4},{1,5},{2,6},{3,7},{4,0},{5,1},{6,2},{7,3},{8,12},{9,13},{10,... | collective-permute-start | bytes 24584 | tf_op jit(solution)/shard_map/ppermute | solution.py:484
  52.1 4.4 %collective-permute-start.4 = (f32[72,256]{1,0:T(8,128)S(1)}, f32[72,256]{1,0:T(8,128)S(1)}, u32[]{:S(2)}, u32[]{:S(2)}) collective-permute-start(f32[72,256]{1,0:T(8,128)S(1)} %get-tuple-element.25), channel_id=1, source_target_pairs={{0,2},{1,3},{2,0},{3,1},{4,6},{5,7},{6,4},{7,5},{8,10},{9,11},{10,... | collective-permute-start | bytes 221192 | tf_op jit(solution)/shard_map/ppermute | solution.py:488

commit v6 on v5

--- a/solution.py
+++ b/solution.py
@@ -101,9 +101,10 @@
     top = jnp.max(g, axis=1, keepdims=True)
     e = jnp.exp(g - top)
     e_scr[...] = e
-    for k in range(states // 128):
-        e_ref[k] = e[:, k * 128 : (k + 1) * 128]
-    top_ref[...] = jnp.broadcast_to(top, (frames, 128))
+    for i in range(2):
+        for k in range(states // 128):
+            e_ref[i, k] = e[i * half : (i + 1) * half, k * 128 : (k + 1) * 128]
+        top_ref[i] = jnp.broadcast_to(top[i * half : (i + 1) * half], (half, 128))
 
     for copy in copies[1:]:
         copy.wait()
@@ -156,10 +157,11 @@
                 pltpu.matmul_acc_lhs(accs[1][m], bh[sl, :], 0)
                 pltpu.matmul_acc_lhs(accs[1][m], bl[sl, :], None)
 
-        def post(k, s, peak, look):
+        def post(k, s, r, peak, freeze):
+            look, use = r % 4 == 1 + 2 * k, r % 4 == (2 + 2 * k) % 4
             mh, ml = mats[k]
             er = e_scr[pl.ds(s + k * half, 1), :]
-            if not look:
+            if use:
                 er = er * (1.0 / jnp.max(peak.astype(F32), keepdims=True)[:, :1])
             live = s < alive[k]
             new = None
@@ -167,8 +169,11 @@
                 x = pltpu.matmul_pop(accs[k][m]) * er
                 h, l = halves(x)
                 sl = pl.ds(m * rows, rows)
-                mh[sl, :] = jnp.where(live, h, mh[sl, :])
-                ml[sl, :] = jnp.where(live, l, ml[sl, :])
+                if freeze:
+                    h = jnp.where(live, h, mh[sl, :])
+                    l = jnp.where(live, l, ml[sl, :])
+                mh[sl, :] = h
+                ml[sl, :] = l
                 if look:
                     y = jnp.max(h.reshape(rows // 16, 16, states), axis=0)
                     new = y if new is None else jnp.maximum(new, y)
@@ -184,25 +189,28 @@
         issue_a(0)
         one = jnp.ones((16, states), BF16)
 
-        def step(s, r, peaks, last=False):
+        def step(s, r, peaks, freeze, last=False):
             pa, pb = peaks
-            odd = r % 2 == 1
             issue_b()
-            pa = post(0, s, pa, odd)
+            pa = post(0, s, r, pa, freeze)
             if not last:
                 issue_a(None)
-            pb = post(1, s, pb, not odd)
+            pb = post(1, s, r, pb, freeze)
             return pa, pb
 
+        def eight(j, peaks, freeze):
+            for r in range(1, SUB):
+                peaks = step(j * SUB + r, r, peaks, freeze)
+            keep(j)
+            return step(j * SUB + SUB, SUB, peaks, freeze)
+
         def block(j, peaks):
-            for r in range(1, SUB):
-                peaks = step(j * SUB + r, r, peaks)
-            keep(j)
-            return step(j * SUB + SUB, SUB, peaks)
+            full = jnp.minimum(alive[0], alive[1]) > j * SUB + SUB
+            return lax.cond(full, lambda p: eight(j, p, False), lambda p: eight(j, p, True), peaks)
 
         peaks = lax.fori_loop(0, blocks - 1, block, (one, one))
         for r in range(1, SUB):
-            peaks = step((blocks - 1) * SUB + r, r, peaks, r == SUB - 1)
+            peaks = step((blocks - 1) * SUB + r, r, peaks, True, r == SUB - 1)
         keep(blocks - 1)
         for i, (mh, ml) in enumerate(mats):
             mats_ref[i] = mh[0:states, :].astype(F32) + ml[0:states, :].astype(F32)
@@ -239,8 +247,8 @@
         out_shape=(
             out((2, states, states), F32),
             out((2, blocks, 2, states, states), BF16),
-            out((states // 128, frames, 128), F32),
-            out((frames, 128), F32),
+            out((2, states // 128, frames // 2, 128), F32),
+            out((2, frames // 2, 128), F32),
             out((states, states), BF16),
             out((states, states), BF16),
             out((8, states), F32),
@@ -360,110 +368,84 @@
     )(pinned(x))
 
 
-def frames_kernel(frames, lengths_hbm, *refs):
-    start_ref, *v_refs = refs[:-13]
-    other_ref, mid_ref, pre_ref, e_ref, top_ref, th_ref, tl_ref, kept_ref, sent_ref, gain_ref, *scratch = refs[
-        len(v_refs) + 1 :
-    ]
+def slot_kernel(sent, lengths_hbm, *refs):
+    start_ref, *v_refs = refs[:-11]
+    other_ref, mid_ref, pre_ref, e_ref, top_ref, th_ref, tl_ref, out_ref, *scratch = refs[len(v_refs) + 1 :]
     alpha_scr, lengths_ref, sem = scratch
     copy = pltpu.make_async_copy(lengths_hbm, lengths_ref, sem)
     copy.start()
     states = th_ref.shape[0]
-    half = frames // 2
+    half = top_ref.shape[1]
     blocks = half // SUB
-    subs = 2 * blocks
     index = lax.axis_index("tm")
     utt, slots = place(half)
+    slot = 1 - utt if sent else utt
+
     v = start_ref[...]
     for g, ref in enumerate(v_refs):
         v = jnp.where(index // 4 == g + 1, ref[...], v)
-    mid = pass_on(v, mid_ref[...])
-    v = jnp.where(index % 2 == 1, pass_on(v, other_ref[0]), v)
+    before = jnp.where(index % 2 == 1, pass_on(v, other_ref[0]), v)
+    v = jnp.where(slot == 1, pass_on(v, mid_ref[...]), before)
     rows = [v[0:1]]
     for j in range(blocks - 1):
-        rows.append(row_dot(v, pre_ref[0, j, 0], pre_ref[0, j, 1])[0:1])
-    rows.append(mid[0:1])
-    for j in range(blocks - 1):
-        rows.append(row_dot(mid, pre_ref[1, j, 0], pre_ref[1, j, 1])[0:1])
+        rows.append(row_dot(v, pre_ref[slot, j, 0], pre_ref[slot, j, 1])[0:1])
     x = jnp.concatenate(rows, axis=0)
     total = jnp.sum(x, axis=1, keepdims=True)
-    v, mid = unit(v), unit(mid)
     th, tl = th_ref[...], tl_ref[...]
-    lane = lax.broadcasted_iota(jnp.int32, (subs, 128), 1)
-    sub = lax.broadcasted_iota(jnp.int32, (subs, 128), 0)
-    gains = jnp.zeros((subs, 128), F32)
+    lane = lax.broadcasted_iota(jnp.int32, (blocks, 128), 1)
+    sub = lax.broadcasted_iota(jnp.int32, (blocks, 128), 0)
+    gains = jnp.zeros((blocks, 128), F32)
     copy.wait()
-    alive = [lengths_ref[utt] - slot for slot in slots]
+    left = lengths_ref[utt] - jnp.where(slot == 0, slots[0], slots[1])
     tiles = range(states // 128)
     for r in range(SUB):
-        every = pl.ds(r, subs, stride=SUB)
-        factor = jnp.concatenate([e_ref[k, every, :] for k in tiles], axis=1) * (1.0 / total)
+        every = pl.ds(r, blocks, stride=SUB)
+        factor = jnp.concatenate([e_ref[slot, k, every, :] for k in tiles], axis=1) * (1.0 / total)
         x = row_dot(x, th, tl) * factor
         total = jnp.sum(x, axis=1, keepdims=True)
         alpha = x * (1.0 / total)
         for k in tiles:
             alpha_scr[k, every, :] = alpha[:, k * 128 : (k + 1) * 128]
-        live = (sub % blocks) * SUB + r < jnp.where(sub < blocks, alive[0], alive[1])
-        gain = jnp.where(live, jnp.log(total) + top_ref[every, :], 0.0)
+        live = sub * SUB + r < left
+        gain = jnp.where(live, jnp.log(total) + top_ref[slot, every, :], 0.0)
         gains = jnp.where(lane % SUB == r, gain, gains)
-    for which, ref in ((utt, kept_ref), (1 - utt, sent_ref)):
-        at = pl.multiple_of(which * half, half)
-        left = jnp.where(which == 0, alive[0], alive[1])
-        frame = lax.broadcasted_iota(jnp.int32, (half, 128), 0)
-        end = pl.ds(at + jnp.clip(left - 1, 0, half - 1), 1)
-        before = jnp.where(which == 0, v[0:1], mid[0:1])
-        for k in tiles:
-            cut = slice(k * 128, (k + 1) * 128)
-            final = jnp.where(left > 0, alpha_scr[k, end, :], before[:, cut])
-            ref[0:half, cut] = jnp.log(jnp.where(frame < left, alpha_scr[k, pl.ds(at, half), :], final))
-    picked = jnp.where(lane // SUB == sub % blocks, gains, 0.0)
-    lines = [jnp.sum(picked[k * blocks : (k + 1) * blocks], axis=0, keepdims=True) for k in range(2)]
-    gain_ref[...] = jnp.where(utt == 0, lines[0], lines[1])
-    line = jnp.where(utt == 0, lines[1], lines[0])
-    sent_ref[half : half + 8, :] = jnp.concatenate([jnp.broadcast_to(line, (8, 128))] * (states // 128), axis=1)
-
-
-def frames_pass(lengths, vs, other, mid, pre, e, top, th, tl):
-    frames, states = top.shape[0], th.shape[0]
-    half = frames // 2
-    out = jax.ShapeDtypeStruct
+    v = unit(v)
+    frame = lax.broadcasted_iota(jnp.int32, (half, 128), 0)
+    end = pl.ds(jnp.clip(left - 1, 0, half - 1), 1)
+    for k in tiles:
+        cut = slice(k * 128, (k + 1) * 128)
+        final = jnp.where(left > 0, alpha_scr[k, end, :], v[0:1, cut])
+        out_ref[0:half, cut] = jnp.log(jnp.where(frame < left, alpha_scr[k], final))
+    line = jnp.sum(jnp.where(lane // SUB == sub, gains, 0.0), axis=0, keepdims=True)
+    out_ref[half : half + 8, :] = jnp.concatenate([jnp.broadcast_to(line, (8, 128))] * (states // 128), axis=1)
+
+
+def slot_pass(sent, lengths, vs, other, mid, pre, e, top, th, tl):
+    half, states = top.shape[1], th.shape[0]
     return pl.pallas_call(
-        functools.partial(frames_kernel, frames),
-        out_shape=(out((half, states), F32), out((half + 8, states), F32), out((1, 128), F32)),
+        functools.partial(slot_kernel, sent),
+        out_shape=jax.ShapeDtypeStruct((half + 8, states), F32),
         in_specs=[hbm()] + [vmem()] * (len(vs) + 7),
-        out_specs=[vmem()] * 3,
+        out_specs=vmem(),
         scratch_shapes=[
-            pltpu.VMEM((states // 128, frames, 128), F32),
+            pltpu.VMEM((states // 128, half, 128), F32),
             pltpu.SMEM(lengths.shape, jnp.int32),
             pltpu.SemaphoreType.DMA,
         ],
         compiler_params=pltpu.CompilerParams(vmem_limit_bytes=6 << 20),
-        name="frames",
+        name="sent" if sent else "kept",
     )(pinned(lengths), *vs, other, mid, pre, e, top, th, tl)
 
 
-def join_kernel(kept_ref, gain_ref, got_ref, log_ref, out_gain_ref):
-    half = kept_ref.shape[0]
+def join_kernel(kept_ref, got_ref, log_ref, gain_ref):
+    half = log_ref.shape[1]
     utt = (lax.axis_index("tm") // 2) % 2
-    log_ref[utt] = kept_ref[...]
+    log_ref[utt] = kept_ref[0:half, :]
     log_ref[1 - utt] = got_ref[0:half, :]
-    own = gain_ref[0:1, 0:half]
+    own = kept_ref[half : half + 1, 0:half]
     got = got_ref[half : half + 1, 0:half]
-    out_gain_ref[0:1, :] = jnp.where(utt == 0, own, got)
-    out_gain_ref[1:2, :] = jnp.where(utt == 0, got, own)
-
-
-def join(kept, gain, got):
-    half, states = kept.shape
-    out = jax.ShapeDtypeStruct
-    return pl.pallas_call(
-        join_kernel,
-        out_shape=(out((2, half, states), F32), out((2, half), F32)),
-        in_specs=[vmem()] * 3,
-        out_specs=[vmem()] * 2,
-        compiler_params=pltpu.CompilerParams(vmem_limit_bytes=4 << 20),
-        name="join",
-    )(kept, gain, got)
+    gain_ref[0:1, :] = jnp.where(utt == 0, own, got)
+    gain_ref[1:2, :] = jnp.where(utt == 0, got, own)
 
 
 def shards(size, loglik, trans_weight, block_mask, init_weight, lengths, pdf_map):
@@ -484,17 +466,20 @@
         vs.append(lax.ppermute(v, "tm", pairs))
         if g < groups - 1:
             (v,) = small(hop_kernel, "hop", [v.shape], vs[-1], whole)
-    kept, sent, gain = frames_pass(lengths, vs, other, mid, pre, e, top, th, tl)
+    given = (lengths, vs, other, mid, pre, e, top, th, tl)
+    sent = slot_pass(True, *given)
     got = lax.ppermute(sent, "tm", [(i, i ^ 2) for i in range(size)])
-    return join(kept, gain, got)
+    kept = slot_pass(False, *given)
+    half, states = kept.shape[0] - 8, kept.shape[1]
+    return small(join_kernel, "join", [(2, half, states), (2, half)], kept, got)
 
 
 def partner(index, turn, groups):
     group = index // 4
     other = group ^ 1 if turn % 2 else (group - 1 if group % 2 == 0 else group + 1)
     if 0 <= other < groups:
-        return 4 * other + index % 4
-    return index ^ 2
+        return (4 * other + index % 4) ^ 1
+    return index ^ 3
 
 
 def solution(mesh):

time: 57.4 us -> 53.8 us (0.937)
  waiting for transfers between devices: 15 us -> 11.6 us
    ppermute x1, waiting for transfers between devices: 4.18 us -> 2.36 us  [shards(): got = lax.ppermute(sent, 'tm', [(i, i ^ 2) for i in range(size)])]
    ppermute x3, waiting for transfers between devices: 8.95 us -> 7.34 us  [shards(): vs.append(lax.ppermute(v, 'tm', pairs))]
    pallas_call x1, Pallas kernels: 16.7 us -> 15.6 us  [transfer(): pl.pallas_call(functools.partial(transfer_kernel, frames), out_shape=(out...]
    pallas_call x4 -> x5, Pallas kernels: 1.93 us -> 2.6 us  [small(): pl.pallas_call(kernel, out_shape=tuple((jax.ShapeDtypeStruct(shape, F32)...]
  transfers between devices with their start and end apart: 5 -> 5, of which waited for: 5 -> 5; matrix products, arithmetic and copies ran while one was open for 0% -> 0% of each run, Pallas kernels for 2% -> 5%
where the time goes in v6:
time: 53.8 us; the launch traced here: 53.6 us
  Pallas kernels  23 us (43%)
  blocking collectives  17.2 us (32%)
  waiting for transfers between devices  11.6 us (22%)
  starting transfers between devices  1.13 us (2%)
  between operations  0.68 us (1%)
    all_to_all x1, blocking collectives, shards(): lax.all_to_all(x, 'tm', 0, 0, tiled=True).reshape(size * local, frames)  17.2 us
    pallas_call x1, Pallas kernels, transfer(): pl.pallas_call(functools.partial(transfer_kernel, frames), out_shape=(out...  15.6 us
    ppermute x3, waiting for transfers between devices, shards(): vs.append(lax.ppermute(v, 'tm', pairs))  7.34 us
    pallas_call x2, Pallas kernels, slot_pass(): pl.pallas_call(functools.partial(slot_kernel, sent), out_shape=jax.ShapeD...  3.63 us
    pallas_call x5, Pallas kernels, small(): pl.pallas_call(kernel, out_shape=tuple((jax.ShapeDtypeStruct(shape, F32)...  2.6 us
    ppermute x1, waiting for transfers between devices, shards(): got = lax.ppermute(sent, 'tm', [(i, i ^ 2) for i in range(size)])  2.36 us
    ppermute x1, waiting for transfers between devices, shards(): other = lax.ppermute(own, 'tm', [(i, i ^ 1) for i in range(size)])  1.9 us
    pallas_call x1, Pallas kernels, pack(): pl.pallas_call(pack_kernel, out_shape=jax.ShapeDtypeStruct((groups, 4, lo...  1.09 us
  transfers between devices with their start and end apart: 5, of which 5 were waited for; matrix products, arithmetic and copies ran while one was open for 0% of the time, Pallas kernels for 5%

profile of v6, /device:TPU:0, one launch (start us, length us, event | category | flops | bytes accessed | tf_op | source)
XLA Modules:
  0.0 53.6 jit_solution(17452697395996896608)
XLA Ops:
  0.6 1.1 %pack.1 = f32[4,4,32,128]{3,2,1,0:T(8,128)S(1)} custom-call(f32[2,32,1024]{2,1,0:T(8,128)} %bitcast.7), custom_call_target="tpu_custom_call" | custom-call | tf_op jit(solution)/shard_map/pack/pallas_call | solution.py:360
  1.7 17.2 %all_to_all.5 = f32[16,32,128]{2,1,0:T(8,128)S(1)} all-to-all(f32[16,32,128]{2,1,0:T(8,128)S(1)} %bitcast.6), channel_id=1, replica_groups=mesh['groups'=2,'tm'=16] {'tm'}, dimensions={0} | all-to-all | bytes 524288 | tf_op jit(solution)/shard_map/all_to_all | solution.py:457
  19.0 15.6 %transfer.1 = (f32[2,256,256]{2,1,0:T(8,128)S(1)}, bf16[2,8,2,256,256]{4,3,2,1,0:T(8,128)(2,1)S(1)}, f32[2,2,64,128]{3,2,1,0:T(8,128)S(1)}, f32[2,64,128]{2,1,0:...) custom-call(s32[2]{0:T(128)} %lengths_hbm.5, s32[4,4]{1,0:T(4,128)} %mask_hbm.1, ...), custom_call_target="tpu_custom_call" | custom-call | tf_op jit(solution)/shard_map/transfer/pallas_call | solution.py:245
  34.6 0.1 collective-permute-start
  34.7 1.9 %collective-permute-done.other_ref.refs_4_ = f32[2,256,256]{2,1,0:T(8,128)S(1)} collective-permute-done((f32[2,256,256]{2,1,0:T(8,128)S(1)}, f32[2,256,256]{2,1,0:T(8,128)S(1)}, u32[]{:S(2)}, u32[]{:S(2)}) %collective-permute-start) | collective-permute-done | bytes 524320 | tf_op jit(solution)/shard_map/ppermute | solution.py:459
  36.6 0.5 first.1
  37.1 0.4 collective-permute-start.1
  37.5 1.1 %group.1 = (f32[256,256]{1,0:T(8,128)S(1)}, f32[256,256]{1,0:T(8,128)S(1)}) custom-call(f32[2,256,256]{2,1,0:T(8,128)S(1)} %get-tuple-element.12.own_ref, f32[2,256,256]{2,1,0:T(8,128)S(1)} %collective-permute-done.other_ref.refs_4_), custom_call_target="tpu_custom_call" | custom-call | tf_op jit(solution)/shard_map/group/pallas_call | solution.py:333
  38.6 1.6 %collective-permute-done.1.v_ref.refs_1_ = f32[8,256]{1,0:T(8,128)S(1)} collective-permute-done((f32[8,256]{1,0:T(8,128)S(1)}, f32[8,256]{1,0:T(8,128)S(1)}, u32[]{:S(2)}, u32[]{:S(2)}) %collective-permute-start.1) | collective-permute-done | bytes 8224 | tf_op jit(solution)/shard_map/ppermute | solution.py:466
  40.2 0.1 hop.2
  40.4 0.1 collective-permute-start.2
  40.5 3.0 %collective-permute-done.2.v_ref.refs_2_ = f32[8,256]{1,0:T(8,128)S(1)} collective-permute-done((f32[8,256]{1,0:T(8,128)S(1)}, f32[8,256]{1,0:T(8,128)S(1)}, u32[]{:S(2)}, u32[]{:S(2)}) %collective-permute-start.2) | collective-permute-done | bytes 8224 | tf_op jit(solution)/shard_map/ppermute | solution.py:466
  43.5 0.1 hop.3
  43.6 0.3 collective-permute-start.3
  43.9 2.8 %collective-permute-done.3.refs_3_ = f32[8,256]{1,0:T(8,128)S(1)} collective-permute-done((f32[8,256]{1,0:T(8,128)S(1)}, f32[8,256]{1,0:T(8,128)S(1)}, u32[]{:S(2)}, u32[]{:S(2)}) %collective-permute-start.3) | collective-permute-done | bytes 8224 | tf_op jit(solution)/shard_map/ppermute | solution.py:466
  46.7 1.8 %sent.1 = f32[72,256]{1,0:T(8,128)S(1)} custom-call(s32[2]{0:T(128)} %lengths_hbm.5, f32[8,256]{1,0:T(8,128)S(1)} %get-tuple-element.11.start_ref.refs_0_, f32[8,256]{1,0:T(8,128)S(1)} %collective-permute-done.1.v_ref.refs_1_, f32[8,256]{1,0:T(8,128)S(1)} %collective-permute-done.2.v_ref.refs_2_, f32[8,256]{1,0:T(8,128)S(1)} %collective-permute-done.3.refs_3_, ...), custom_call_target="tpu_custom_call" | custom-call | tf_op jit(solution)/shard_map/sent/pallas_call | solution.py:425
  48.5 0.2 collective-permute-start.4
  48.7 1.8 %kept.1.kept_ref = f32[72,256]{1,0:T(8,128)S(1)} custom-call(s32[2]{0:T(128)} %lengths_hbm.5, f32[8,256]{1,0:T(8,128)S(1)} %get-tuple-element.11.start_ref.refs_0_, f32[8,256]{1,0:T(8,128)S(1)} %collective-permute-done.1.v_ref.refs_1_, f32[8,256]{1,0:T(8,128)S(1)} %collective-permute-done.2.v_ref.refs_2_, f32[8,256]{1,0:T(8,128)S(1)} %collective-permute-done.3.refs_3_, ...), custom_call_target="tpu_custom_call" | custom-call | tf_op jit(solution)/shard_map/kept/pallas_call | solution.py:425
  50.6 2.4 %collective-permute-done.4.got_ref = f32[72,256]{1,0:T(8,128)S(1)} collective-permute-done((f32[72,256]{1,0:T(8,128)S(1)}, f32[72,256]{1,0:T(8,128)S(1)}, u32[]{:S(2)}, u32[]{:S(2)}) %collective-permute-start.4) | collective-permute-done | bytes 73760 | tf_op jit(solution)/shard_map/ppermute | solution.py:471
  52.9 0.7 %join.1 = (f32[2,64,256]{2,1,0:T(8,128)}, f32[2,64]{1,0:T(2,128)}) custom-call(f32[72,256]{1,0:T(8,128)S(1)} %kept.1.kept_ref, f32[72,256]{1,0:T(8,128)S(1)} %collective-permute-done.4.got_ref), custom_call_target="tpu_custom_call" | custom-call | tf_op jit(solution)/shard_map/join/pallas_call | solution.py:333
Async XLA Ops:
  34.6 2.0 %collective-permute-start = (f32[2,256,256]{2,1,0:T(8,128)S(1)}, f32[2,256,256]{2,1,0:T(8,128)S(1)}, u32[]{:S(2)}, u32[]{:S(2)}) collective-permute-start(f32[2,256,256]{2,1,0:T(8,128)S(1)} %get-tuple-element.12.own_ref), channel_id=1, source_target_pairs={{0,1},{1,0},{2,3},{3,2},{4,5},{5,4},{6,7},{7,6},{8,9},{9,8},{10,11... | collective-permute-start | bytes 1572872 | tf_op jit(solution)/shard_map/ppermute | solution.py:459
  37.1 3.1 %collective-permute-start.1 = (f32[8,256]{1,0:T(8,128)S(1)}, f32[8,256]{1,0:T(8,128)S(1)}, u32[]{:S(2)}, u32[]{:S(2)}) collective-permute-start(f32[8,256]{1,0:T(8,128)S(1)} %first.1), channel_id=1, source_target_pairs={{0,5},{1,4},{2,7},{3,6},{4,1},{5,0},{6,3},{7,2},{8,13},{9,12},{10,... | collective-permute-start | bytes 24584 | tf_op jit(solution)/shard_map/ppermute | solution.py:466
  40.4 3.1 %collective-permute-start.2 = (f32[8,256]{1,0:T(8,128)S(1)}, f32[8,256]{1,0:T(8,128)S(1)}, u32[]{:S(2)}, u32[]{:S(2)}) collective-permute-start(f32[8,256]{1,0:T(8,128)S(1)} %hop.2), channel_id=1, source_target_pairs={{0,3},{1,2},{2,1},{3,0},{4,9},{5,8},{6,11},{7,10},{8,5},{9,4},{10,... | collective-permute-start | bytes 24584 | tf_op jit(solution)/shard_map/ppermute | solution.py:466
  43.6 3.1 %collective-permute-start.3 = (f32[8,256]{1,0:T(8,128)S(1)}, f32[8,256]{1,0:T(8,128)S(1)}, u32[]{:S(2)}, u32[]{:S(2)}) collective-permute-start(f32[8,256]{1,0:T(8,128)S(1)} %hop.3), channel_id=1, source_target_pairs={{0,5},{1,4},{2,7},{3,6},{4,1},{5,0},{6,3},{7,2},{8,13},{9,12},{10,... | collective-permute-start | bytes 24584 | tf_op jit(solution)/shard_map/ppermute | solution.py:466
  48.5 4.4 %collective-permute-start.4 = (f32[72,256]{1,0:T(8,128)S(1)}, f32[72,256]{1,0:T(8,128)S(1)}, u32[]{:S(2)}, u32[]{:S(2)}) collective-permute-start(f32[72,256]{1,0:T(8,128)S(1)} %sent.1), channel_id=1, source_target_pairs={{0,2},{1,3},{2,0},{3,1},{4,6},{5,7},{6,4},{7,5},{8,10},{9,11},{10,... | collective-permute-start | bytes 221192 | tf_op jit(solution)/shard_map/ppermute | solution.py:471

commit v7 on v6

--- a/solution.py
+++ b/solution.py
@@ -35,9 +35,9 @@
     lengths_hbm,
     mask_hbm,
     weight_hbm,
-    map_hbm,
     init_hbm,
     cols_ref,
+    map_ref,
     mats_ref,
     pre_ref,
     e_ref,
@@ -55,7 +55,6 @@
     lengths_ref,
     mask_ref,
     weight_ref,
-    map_ref,
     init_ref,
     sems,
 ):
@@ -63,7 +62,6 @@
         pltpu.make_async_copy(src, dst, sems.at[i])
         for i, (src, dst) in enumerate(
             (
-                (map_hbm, map_ref),
                 (weight_hbm, weight_ref),
                 (mask_hbm, mask_ref),
                 (lengths_hbm, lengths_ref),
@@ -79,7 +77,6 @@
     blocks = half // SUB
     utt, slots = place(half)
     cols = cols_ref[...].T
-    copies[0].wait()
     pick = (lax.broadcasted_iota(jnp.int32, (cols.shape[1], states), 0) == map_ref[...]).astype(F32).astype(BF16)
     p1 = cols.astype(BF16)
     rest = cols - p1.astype(F32)
@@ -106,7 +103,7 @@
             e_ref[i, k] = e[i * half : (i + 1) * half, k * 128 : (k + 1) * 128]
         top_ref[i] = jnp.broadcast_to(top[i * half : (i + 1) * half], (half, 128))
 
-    for copy in copies[1:]:
+    for copy in copies:
         copy.wait()
     alive = [lengths_ref[utt] - slot for slot in slots]
     start_ref[...] = jnp.broadcast_to(unit(init_ref[...]), start_ref.shape)
@@ -237,7 +234,7 @@
     return pltpu.with_memory_space_constraint(x, pltpu.MemorySpace.HBM)
 
 
-def transfer(cols, weight, mask, lengths, pdf_map, init):
+def transfer(cols, columns_of, weight, mask, lengths, init):
     columns, frames = cols.shape
     states = weight.shape[0]
     blocks = frames // 2 // SUB
@@ -253,7 +250,7 @@
             out((states, states), BF16),
             out((8, states), F32),
         ),
-        in_specs=[hbm()] * 5 + [vmem()],
+        in_specs=[hbm()] * 4 + [vmem()] * 2,
         out_specs=[vmem()] * 7,
         scratch_shapes=[pltpu.VMEM((frames, states), F32)] * 2
         + [pltpu.VMEM((states, states), F32)]
@@ -262,13 +259,12 @@
             pltpu.SMEM(lengths.shape, jnp.int32),
             pltpu.SMEM(mask.shape, jnp.int32),
             pltpu.VMEM(weight.shape, F32),
-            pltpu.VMEM((1, states), jnp.int32),
             pltpu.VMEM((1, states), F32),
-            pltpu.SemaphoreType.DMA((5,)),
+            pltpu.SemaphoreType.DMA((4,)),
         ],
         compiler_params=pltpu.CompilerParams(vmem_limit_bytes=6 << 20),
         name="transfer",
-    )(*map(pinned, (lengths, mask, weight, pdf_map[None, :], init[None, :])), cols)
+    )(*map(pinned, (lengths, mask, weight, init[None, :])), cols, columns_of)
 
 
 def row_dot(v, matrix_high, matrix_low):
@@ -340,10 +336,13 @@
     )(*args)
 
 
-def pack_kernel(x_hbm, out_ref, x_ref, sem):
-    copy = pltpu.make_async_copy(x_hbm, x_ref, sem)
+def pack_kernel(x_hbm, map_hbm, out_ref, map_ref, x_ref, sems):
+    map_copy = pltpu.make_async_copy(map_hbm, map_ref, sems.at[1])
+    copy = pltpu.make_async_copy(x_hbm, x_ref, sems.at[0])
     copy.start()
+    map_copy.start()
     copy.wait()
+    map_copy.wait()
     groups = out_ref.shape[0]
     local = out_ref.shape[2]
     low = lax.broadcasted_iota(jnp.int32, (local, 128), 1) < 64
@@ -355,17 +354,20 @@
             out_ref[g, 2 * u + 1] = jnp.where(low, pltpu.roll(early, 64, 1), late)
 
 
-def pack(x, groups):
+def pack(x, pdf_map, groups):
     local = x.shape[1]
     return pl.pallas_call(
         pack_kernel,
-        out_shape=jax.ShapeDtypeStruct((groups, 4, local, 128), F32),
-        in_specs=[hbm()],
-        out_specs=vmem(),
-        scratch_shapes=[pltpu.VMEM(x.shape, F32), pltpu.SemaphoreType.DMA],
+        out_shape=(
+            jax.ShapeDtypeStruct((groups, 4, local, 128), F32),
+            jax.ShapeDtypeStruct((1, pdf_map.shape[0]), jnp.int32),
+        ),
+        in_specs=[hbm()] * 2,
+        out_specs=[vmem()] * 2,
+        scratch_shapes=[pltpu.VMEM(x.shape, F32), pltpu.SemaphoreType.DMA((2,))],
         compiler_params=pltpu.CompilerParams(vmem_limit_bytes=4 << 20),
         name="pack",
-    )(pinned(x))
+    )(pinned(x), pinned(pdf_map[None, :]))
 
 
 def slot_kernel(sent, lengths_hbm, *refs):
@@ -381,43 +383,67 @@
     utt, slots = place(half)
     slot = 1 - utt if sent else utt
 
-    v = start_ref[...]
-    for g, ref in enumerate(v_refs):
-        v = jnp.where(index // 4 == g + 1, ref[...], v)
-    before = jnp.where(index % 2 == 1, pass_on(v, other_ref[0]), v)
-    v = jnp.where(slot == 1, pass_on(v, mid_ref[...]), before)
-    rows = [v[0:1]]
-    for j in range(blocks - 1):
-        rows.append(row_dot(v, pre_ref[slot, j, 0], pre_ref[slot, j, 1])[0:1])
-    x = jnp.concatenate(rows, axis=0)
-    total = jnp.sum(x, axis=1, keepdims=True)
-    th, tl = th_ref[...], tl_ref[...]
-    lane = lax.broadcasted_iota(jnp.int32, (blocks, 128), 1)
-    sub = lax.broadcasted_iota(jnp.int32, (blocks, 128), 0)
-    gains = jnp.zeros((blocks, 128), F32)
-    copy.wait()
-    left = lengths_ref[utt] - jnp.where(slot == 0, slots[0], slots[1])
-    tiles = range(states // 128)
-    for r in range(SUB):
-        every = pl.ds(r, blocks, stride=SUB)
-        factor = jnp.concatenate([e_ref[slot, k, every, :] for k in tiles], axis=1) * (1.0 / total)
-        x = row_dot(x, th, tl) * factor
+    def body(acc_high, acc_low):
+        def stacked(v):
+            return jnp.concatenate(halves(v), axis=0)
+
+        def load(high, low):
+            pltpu.matmul_push_rhs(high, 0, 0)
+            pltpu.matmul_push_rhs(low, 0, 1)
+
+        def times(v, fresh):
+            both = stacked(v)
+            stage = 0 if fresh else None
+            pltpu.matmul_acc_lhs(acc_high, both, stage)
+            pltpu.matmul_acc_lhs(acc_low, both, stage)
+            y = pltpu.matmul_pop(acc_high) + pltpu.matmul_pop(acc_low)
+            return y[0:8] + y[8:16]
+
+        def passed(v, matrix):
+            load(*halves(matrix))
+            return times(v, True) * (1.0 / jnp.sum(v, axis=1, keepdims=True))
+
+        v = start_ref[...]
+        for g, ref in enumerate(v_refs):
+            v = jnp.where(index // 4 == g + 1, ref[...], v)
+        before = jnp.where(index % 2 == 1, passed(v, other_ref[0]), v)
+        v = jnp.where(slot == 1, passed(v, mid_ref[...]), before)
+        rows = [v[0:1]]
+        for j in range(blocks - 1):
+            load(pre_ref[slot, j, 0], pre_ref[slot, j, 1])
+            rows.append(times(v, True)[0:1])
+        x = jnp.concatenate(rows, axis=0)
         total = jnp.sum(x, axis=1, keepdims=True)
-        alpha = x * (1.0 / total)
+        load(th_ref[...], tl_ref[...])
+        lane = lax.broadcasted_iota(jnp.int32, (blocks, 128), 1)
+        sub = lax.broadcasted_iota(jnp.int32, (blocks, 128), 0)
+        gains = jnp.zeros((blocks, 128), F32)
+        copy.wait()
+        left = lengths_ref[utt] - jnp.where(slot == 0, slots[0], slots[1])
+        tiles = range(states // 128)
+        for r in range(SUB):
+            every = pl.ds(r, blocks, stride=SUB)
+            factor = jnp.concatenate([e_ref[slot, k, every, :] for k in tiles], axis=1) * (1.0 / total)
+            x = times(x, r == 0) * factor
+            total = jnp.sum(x, axis=1, keepdims=True)
+            alpha = x * (1.0 / total)
+            for k in tiles:
+                alpha_scr[k, every, :] = alpha[:, k * 128 : (k + 1) * 128]
+            live = sub * SUB + r < left
+            gain = jnp.where(live, jnp.log(total) + top_ref[slot, every, :], 0.0)
+            gains = jnp.where(lane % SUB == r, gain, gains)
+        v = unit(v)
+        frame = lax.broadcasted_iota(jnp.int32, (half, 128), 0)
+        end = pl.ds(jnp.clip(left - 1, 0, half - 1), 1)
         for k in tiles:
-            alpha_scr[k, every, :] = alpha[:, k * 128 : (k + 1) * 128]
-        live = sub * SUB + r < left
-        gain = jnp.where(live, jnp.log(total) + top_ref[slot, every, :], 0.0)
-        gains = jnp.where(lane % SUB == r, gain, gains)
-    v = unit(v)
-    frame = lax.broadcasted_iota(jnp.int32, (half, 128), 0)
-    end = pl.ds(jnp.clip(left - 1, 0, half - 1), 1)
-    for k in tiles:
-        cut = slice(k * 128, (k + 1) * 128)
-        final = jnp.where(left > 0, alpha_scr[k, end, :], v[0:1, cut])
-        out_ref[0:half, cut] = jnp.log(jnp.where(frame < left, alpha_scr[k], final))
-    line = jnp.sum(jnp.where(lane // SUB == sub, gains, 0.0), axis=0, keepdims=True)
-    out_ref[half : half + 8, :] = jnp.concatenate([jnp.broadcast_to(line, (8, 128))] * (states // 128), axis=1)
+            cut = slice(k * 128, (k + 1) * 128)
+            final = jnp.where(left > 0, alpha_scr[k, end, :], v[0:1, cut])
+            out_ref[0:half, cut] = jnp.log(jnp.where(frame < left, alpha_scr[k], final))
+        line = jnp.sum(jnp.where(lane // SUB == sub, gains, 0.0), axis=0, keepdims=True)
+        out_ref[half : half + 8, :] = jnp.concatenate([jnp.broadcast_to(line, (8, 128))] * (states // 128), axis=1)
+
+    shape = (16, states)
+    pl.run_scoped(body, pltpu.ACC(0)(shape, F32), pltpu.ACC(1)(shape, F32))
 
 
 def slot_pass(sent, lengths, vs, other, mid, pre, e, top, th, tl):
@@ -451,11 +477,11 @@
 def shards(size, loglik, trans_weight, block_mask, init_weight, lengths, pdf_map):
     local = loglik.shape[2]
     groups = size // 4
-    x = pack(jnp.transpose(loglik, (0, 2, 1)), groups)
+    x, columns_of = pack(jnp.transpose(loglik, (0, 2, 1)), pdf_map, groups)
     frames = x.shape[3]
     x = x.reshape(size, local, frames)
     cols = lax.all_to_all(x, "tm", 0, 0, tiled=True).reshape(size * local, frames)
-    own, pre, e, top, th, tl, start = transfer(cols, trans_weight, block_mask, lengths, pdf_map, init_weight)
+    own, pre, e, top, th, tl, start = transfer(cols, columns_of, trans_weight, block_mask, lengths, init_weight)
     other = lax.ppermute(own, "tm", [(i, i ^ 1) for i in range(size)])
     (v,) = small(first_kernel, "first", [start.shape], start, own, other)
     square = own.shape[1:]

time: 53.8 us -> 54.7 us (1.017)
  Pallas kernels: 23 us -> 24.8 us
  waiting for transfers between devices: 11.6 us -> 10.6 us
    pallas_call x2, Pallas kernels: 3.63 us -> 5.48 us  [slot_pass(): pl.pallas_call(functools.partial(slot_kernel, sent), out_shape=jax.ShapeD...]
    ppermute x1, waiting for transfers between devices: 2.36 us -> 1.41 us  [shards(): got = lax.ppermute(sent, 'tm', [(i, i ^ 2) for i in range(size)])]
  transfers between devices with their start and end apart: 5 -> 5, of which waited for: 5 -> 5; matrix products, arithmetic and copies ran while one was open for 0% -> 0% of each run, Pallas kernels for 5% -> 7%
where the time goes in v7:
time: 54.7 us; the launch traced here: 54.5 us
  Pallas kernels  24.8 us (45%)
  blocking collectives  17.2 us (31%)
  waiting for transfers between devices  10.6 us (19%)
  starting transfers between devices  1.16 us (2%)
  between operations  0.68 us (1%)
    all_to_all x1, blocking collectives, shards(): lax.all_to_all(x, 'tm', 0, 0, tiled=True).reshape(size * local, frames)  17.2 us
    pallas_call x1, Pallas kernels, transfer(): pl.pallas_call(functools.partial(transfer_kernel, frames), out_shape=(out...  15.6 us
    ppermute x3, waiting for transfers between devices, shards(): vs.append(lax.ppermute(v, 'tm', pairs))  7.34 us
    pallas_call x2, Pallas kernels, slot_pass(): pl.pallas_call(functools.partial(slot_kernel, sent), out_shape=jax.ShapeD...  5.48 us
    pallas_call x5, Pallas kernels, small(): pl.pallas_call(kernel, out_shape=tuple((jax.ShapeDtypeStruct(shape, F32)...  2.6 us
    ppermute x1, waiting for transfers between devices, shards(): other = lax.ppermute(own, 'tm', [(i, i ^ 1) for i in range(size)])  1.9 us
    ppermute x1, waiting for transfers between devices, shards(): got = lax.ppermute(sent, 'tm', [(i, i ^ 2) for i in range(size)])  1.41 us
    pallas_call x1, Pallas kernels, pack(): pl.pallas_call(pack_kernel, out_shape=(jax.ShapeDtypeStruct((groups, 4, l...  1.1 us
  transfers between devices with their start and end apart: 5, of which 5 were waited for; matrix products, arithmetic and copies ran while one was open for 0% of the time, Pallas kernels for 7%

profile of v7, /device:TPU:0, one launch (start us, length us, event | category | flops | bytes accessed | tf_op | source)
XLA Modules:
  0.0 54.5 jit_solution(13722932568519104152)
XLA Ops:
  0.6 1.1 %pack.1 = (f32[4,4,32,128]{3,2,1,0:T(8,128)S(1)}, s32[1,256]{1,0:T(1,128)S(1)}) custom-call(f32[2,32,1024]{2,1,0:T(8,128)} %bitcast.7, s32[1,256]{1,0:T(1,128)} %bitcast.8), custom_call_target="tpu_custom_call" | custom-call | tf_op jit(solution)/shard_map/pack/pallas_call | solution.py:359
  1.7 17.2 %all_to_all.5 = f32[16,32,128]{2,1,0:T(8,128)S(1)} all-to-all(f32[16,32,128]{2,1,0:T(8,128)S(1)} %bitcast.6), channel_id=1, replica_groups=mesh['groups'=2,'tm'=16] {'tm'}, dimensions={0} | all-to-all | bytes 524288 | tf_op jit(solution)/shard_map/all_to_all | solution.py:483
  19.0 15.6 %transfer.1 = (f32[2,256,256]{2,1,0:T(8,128)S(1)}, bf16[2,8,2,256,256]{4,3,2,1,0:T(8,128)(2,1)S(1)}, f32[2,2,64,128]{3,2,1,0:T(8,128)S(1)}, f32[2,64,128]{2,1,0:...) custom-call(s32[2]{0:T(128)} %lengths_hbm.5, s32[4,4]{1,0:T(4,128)} %mask_hbm.1, ...), custom_call_target="tpu_custom_call" | custom-call | tf_op jit(solution)/shard_map/transfer/pallas_call | solution.py:242
  34.6 0.1 collective-permute-start
  34.7 1.9 %collective-permute-done.other_ref.refs_4_ = f32[2,256,256]{2,1,0:T(8,128)S(1)} collective-permute-done((f32[2,256,256]{2,1,0:T(8,128)S(1)}, f32[2,256,256]{2,1,0:T(8,128)S(1)}, u32[]{:S(2)}, u32[]{:S(2)}) %collective-permute-start) | collective-permute-done | bytes 524320 | tf_op jit(solution)/shard_map/ppermute | solution.py:485
  36.6 0.5 first.1
  37.1 0.4 collective-permute-start.1
  37.4 1.1 %group.1 = (f32[256,256]{1,0:T(8,128)S(1)}, f32[256,256]{1,0:T(8,128)S(1)}) custom-call(f32[2,256,256]{2,1,0:T(8,128)S(1)} %get-tuple-element.16.own_ref, f32[2,256,256]{2,1,0:T(8,128)S(1)} %collective-permute-done.other_ref.refs_4_), custom_call_target="tpu_custom_call" | custom-call | tf_op jit(solution)/shard_map/group/pallas_call | solution.py:329
  38.5 1.6 %collective-permute-done.1.v_ref.refs_1_ = f32[8,256]{1,0:T(8,128)S(1)} collective-permute-done((f32[8,256]{1,0:T(8,128)S(1)}, f32[8,256]{1,0:T(8,128)S(1)}, u32[]{:S(2)}, u32[]{:S(2)}) %collective-permute-start.1) | collective-permute-done | bytes 8224 | tf_op jit(solution)/shard_map/ppermute | solution.py:492
  40.2 0.1 hop.2
  40.3 0.2 collective-permute-start.2
  40.5 2.9 %collective-permute-done.2.v_ref.refs_2_ = f32[8,256]{1,0:T(8,128)S(1)} collective-permute-done((f32[8,256]{1,0:T(8,128)S(1)}, f32[8,256]{1,0:T(8,128)S(1)}, u32[]{:S(2)}, u32[]{:S(2)}) %collective-permute-start.2) | collective-permute-done | bytes 8224 | tf_op jit(solution)/shard_map/ppermute | solution.py:492
  43.4 0.1 hop.3
  43.6 0.3 collective-permute-start.3
  43.9 2.8 %collective-permute-done.3.refs_3_ = f32[8,256]{1,0:T(8,128)S(1)} collective-permute-done((f32[8,256]{1,0:T(8,128)S(1)}, f32[8,256]{1,0:T(8,128)S(1)}, u32[]{:S(2)}, u32[]{:S(2)}) %collective-permute-start.3) | collective-permute-done | bytes 8224 | tf_op jit(solution)/shard_map/ppermute | solution.py:492
  46.7 2.7 %sent.1 = f32[72,256]{1,0:T(8,128)S(1)} custom-call(s32[2]{0:T(128)} %lengths_hbm.5, f32[8,256]{1,0:T(8,128)S(1)} %get-tuple-element.15.start_ref.refs_0_, f32[8,256]{1,0:T(8,128)S(1)} %collective-permute-done.1.v_ref.refs_1_, f32[8,256]{1,0:T(8,128)S(1)} %collective-permute-done.2.v_ref.refs_2_, f32[8,256]{1,0:T(8,128)S(1)} %collective-permute-done.3.refs_3_, ...), custom_call_target="tpu_custom_call" | custom-call | tf_op jit(solution)/shard_map/sent/pallas_call | solution.py:451
  49.4 0.3 collective-permute-start.4
  49.7 2.7 %kept.1.kept_ref = f32[72,256]{1,0:T(8,128)S(1)} custom-call(s32[2]{0:T(128)} %lengths_hbm.5, f32[8,256]{1,0:T(8,128)S(1)} %get-tuple-element.15.start_ref.refs_0_, f32[8,256]{1,0:T(8,128)S(1)} %collective-permute-done.1.v_ref.refs_1_, f32[8,256]{1,0:T(8,128)S(1)} %collective-permute-done.2.v_ref.refs_2_, f32[8,256]{1,0:T(8,128)S(1)} %collective-permute-done.3.refs_3_, ...), custom_call_target="tpu_custom_call" | custom-call | tf_op jit(solution)/shard_map/kept/pallas_call | solution.py:451
  52.4 1.4 %collective-permute-done.4.got_ref = f32[72,256]{1,0:T(8,128)S(1)} collective-permute-done((f32[72,256]{1,0:T(8,128)S(1)}, f32[72,256]{1,0:T(8,128)S(1)}, u32[]{:S(2)}, u32[]{:S(2)}) %collective-permute-start.4) | collective-permute-done | bytes 73760 | tf_op jit(solution)/shard_map/ppermute | solution.py:497
  53.8 0.7 %join.1 = (f32[2,64,256]{2,1,0:T(8,128)}, f32[2,64]{1,0:T(2,128)}) custom-call(f32[72,256]{1,0:T(8,128)S(1)} %kept.1.kept_ref, f32[72,256]{1,0:T(8,128)S(1)} %collective-permute-done.4.got_ref), custom_call_target="tpu_custom_call" | custom-call | tf_op jit(solution)/shard_map/join/pallas_call | solution.py:329
Async XLA Ops:
  34.6 2.0 %collective-permute-start = (f32[2,256,256]{2,1,0:T(8,128)S(1)}, f32[2,256,256]{2,1,0:T(8,128)S(1)}, u32[]{:S(2)}, u32[]{:S(2)}) collective-permute-start(f32[2,256,256]{2,1,0:T(8,128)S(1)} %get-tuple-element.16.own_ref), channel_id=1, source_target_pairs={{0,1},{1,0},{2,3},{3,2},{4,5},{5,4},{6,7},{7,6},{8,9},{9,8},{10,11... | collective-permute-start | bytes 1572872 | tf_op jit(solution)/shard_map/ppermute | solution.py:485
  37.1 3.1 %collective-permute-start.1 = (f32[8,256]{1,0:T(8,128)S(1)}, f32[8,256]{1,0:T(8,128)S(1)}, u32[]{:S(2)}, u32[]{:S(2)}) collective-permute-start(f32[8,256]{1,0:T(8,128)S(1)} %first.1), channel_id=1, source_target_pairs={{0,5},{1,4},{2,7},{3,6},{4,1},{5,0},{6,3},{7,2},{8,13},{9,12},{10,... | collective-permute-start | bytes 24584 | tf_op jit(solution)/shard_map/ppermute | solution.py:492
  40.3 3.1 %collective-permute-start.2 = (f32[8,256]{1,0:T(8,128)S(1)}, f32[8,256]{1,0:T(8,128)S(1)}, u32[]{:S(2)}, u32[]{:S(2)}) collective-permute-start(f32[8,256]{1,0:T(8,128)S(1)} %hop.2), channel_id=1, source_target_pairs={{0,3},{1,2},{2,1},{3,0},{4,9},{5,8},{6,11},{7,10},{8,5},{9,4},{10,... | collective-permute-start | bytes 24584 | tf_op jit(solution)/shard_map/ppermute | solution.py:492
  43.6 3.1 %collective-permute-start.3 = (f32[8,256]{1,0:T(8,128)S(1)}, f32[8,256]{1,0:T(8,128)S(1)}, u32[]{:S(2)}, u32[]{:S(2)}) collective-permute-start(f32[8,256]{1,0:T(8,128)S(1)} %hop.3), channel_id=1, source_target_pairs={{0,5},{1,4},{2,7},{3,6},{4,1},{5,0},{6,3},{7,2},{8,13},{9,12},{10,... | collective-permute-start | bytes 24584 | tf_op jit(solution)/shard_map/ppermute | solution.py:492
  49.4 4.4 %collective-permute-start.4 = (f32[72,256]{1,0:T(8,128)S(1)}, f32[72,256]{1,0:T(8,128)S(1)}, u32[]{:S(2)}, u32[]{:S(2)}) collective-permute-start(f32[72,256]{1,0:T(8,128)S(1)} %sent.1), channel_id=1, source_target_pairs={{0,2},{1,3},{2,0},{3,1},{4,6},{5,7},{6,4},{7,5},{8,10},{9,11},{10,... | collective-permute-start | bytes 221192 | tf_op jit(solution)/shard_map/ppermute | solution.py:497

commit v8 on v6

--- a/solution.py
+++ b/solution.py
@@ -33,11 +33,11 @@
 def transfer_kernel(
     frames,
     lengths_hbm,
-    mask_hbm,
-    weight_hbm,
-    map_hbm,
     init_hbm,
     cols_ref,
+    map_ref,
+    weight_ref,
+    mask_ref,
     mats_ref,
     pre_ref,
     e_ref,
@@ -53,9 +53,6 @@
     bh,
     bl,
     lengths_ref,
-    mask_ref,
-    weight_ref,
-    map_ref,
     init_ref,
     sems,
 ):
@@ -63,9 +60,6 @@
         pltpu.make_async_copy(src, dst, sems.at[i])
         for i, (src, dst) in enumerate(
             (
-                (map_hbm, map_ref),
-                (weight_hbm, weight_ref),
-                (mask_hbm, mask_ref),
                 (lengths_hbm, lengths_ref),
                 (init_hbm, init_ref),
             )
@@ -79,7 +73,6 @@
     blocks = half // SUB
     utt, slots = place(half)
     cols = cols_ref[...].T
-    copies[0].wait()
     pick = (lax.broadcasted_iota(jnp.int32, (cols.shape[1], states), 0) == map_ref[...]).astype(F32).astype(BF16)
     p1 = cols.astype(BF16)
     rest = cols - p1.astype(F32)
@@ -106,24 +99,24 @@
             e_ref[i, k] = e[i * half : (i + 1) * half, k * 128 : (k + 1) * 128]
         top_ref[i] = jnp.broadcast_to(top[i * half : (i + 1) * half], (half, 128))
 
-    for copy in copies[1:]:
-        copy.wait()
-    alive = [lengths_ref[utt] - slot for slot in slots]
-    start_ref[...] = jnp.broadcast_to(unit(init_ref[...]), start_ref.shape)
 
     nb = mask_ref.shape[0]
+    mask = mask_ref[...].astype(F32)
     width = states // nb
     lane = lax.broadcasted_iota(jnp.int32, (1, states), 1) // width
     for r in range(nb):
         row = jnp.zeros((1, states), F32)
         for c in range(nb):
-            row = jnp.where(lane == c, mask_ref[r, c].astype(F32), row)
+            row = jnp.where(lane == c, mask[r : r + 1, c : c + 1], row)
         part = weight_ref[r * width : (r + 1) * width, :] * row
         t_scr[r * width : (r + 1) * width, :] = part / jnp.sum(part, axis=1, keepdims=True)
     th, tl = halves(t_scr[...])
     th_ref[...] = th
     tl_ref[...] = tl
 
+    for copy in copies:
+        copy.wait()
+    alive = [lengths_ref[utt] - slot for slot in slots]
     eye = (
         lax.broadcasted_iota(jnp.int32, (states, states), 0) == lax.broadcasted_iota(jnp.int32, (states, states), 1)
     ).astype(F32)
@@ -212,6 +205,7 @@
         for r in range(1, SUB):
             peaks = step((blocks - 1) * SUB + r, r, peaks, True, r == SUB - 1)
         keep(blocks - 1)
+        start_ref[...] = jnp.broadcast_to(unit(init_ref[...]), start_ref.shape)
         for i, (mh, ml) in enumerate(mats):
             mats_ref[i] = mh[0:states, :].astype(F32) + ml[0:states, :].astype(F32)
 
@@ -237,7 +231,7 @@
     return pltpu.with_memory_space_constraint(x, pltpu.MemorySpace.HBM)
 
 
-def transfer(cols, weight, mask, lengths, pdf_map, init):
+def transfer(cols, columns_of, weight, mask, lengths, init):
     columns, frames = cols.shape
     states = weight.shape[0]
     blocks = frames // 2 // SUB
@@ -253,30 +247,27 @@
             out((states, states), BF16),
             out((8, states), F32),
         ),
-        in_specs=[hbm()] * 5 + [vmem()],
+        in_specs=[hbm()] * 2 + [vmem()] * 4,
         out_specs=[vmem()] * 7,
         scratch_shapes=[pltpu.VMEM((frames, states), F32)] * 2
         + [pltpu.VMEM((states, states), F32)]
         + [pltpu.VMEM((states, states), BF16)] * 4
         + [
             pltpu.SMEM(lengths.shape, jnp.int32),
-            pltpu.SMEM(mask.shape, jnp.int32),
-            pltpu.VMEM(weight.shape, F32),
-            pltpu.VMEM((1, states), jnp.int32),
             pltpu.VMEM((1, states), F32),
-            pltpu.SemaphoreType.DMA((5,)),
+            pltpu.SemaphoreType.DMA((2,)),
         ],
         compiler_params=pltpu.CompilerParams(vmem_limit_bytes=6 << 20),
         name="transfer",
-    )(*map(pinned, (lengths, mask, weight, pdf_map[None, :], init[None, :])), cols)
+    )(*map(pinned, (lengths, init[None, :])), cols, columns_of, weight, mask)
 
 
 def row_dot(v, matrix_high, matrix_low):
     n = v.shape[0]
-    vh, vl = halves(v)
-    both = jnp.concatenate([vh, vl], axis=0)
+    both = jnp.concatenate(halves(v), axis=0)
     x = dot(both, matrix_high)
-    return x[0:n] + x[n:] + dot(vh, matrix_low)
+    y = dot(both, matrix_low)
+    return x[0:n] + x[n:] + y[0:n]
 
 
 def unit(v):
@@ -340,32 +331,42 @@
     )(*args)
 
 
-def pack_kernel(x_hbm, out_ref, x_ref, sem):
-    copy = pltpu.make_async_copy(x_hbm, x_ref, sem)
-    copy.start()
-    copy.wait()
+def pack_kernel(x_hbm, map_hbm, weight_hbm, mask_hbm, out_ref, map_ref, weight_ref, mask_ref, x_ref, sems):
     groups = out_ref.shape[0]
+    pairs = [(x_hbm.at[:, :, pl.ds(g * 256, 256)], x_ref.at[:, :, pl.ds(g * 256, 256)]) for g in range(groups)]
+    pairs += [(map_hbm, map_ref), (weight_hbm, weight_ref), (mask_hbm, mask_ref)]
+    copies = [pltpu.make_async_copy(src, dst, sems.at[i]) for i, (src, dst) in enumerate(pairs)]
+    for copy in copies:
+        copy.start()
     local = out_ref.shape[2]
     low = lax.broadcasted_iota(jnp.int32, (local, 128), 1) < 64
     for g in range(groups):
+        copies[g].wait()
         for u in range(2):
             early = x_ref[u, :, g * 256 : g * 256 + 128]
             late = x_ref[u, :, g * 256 + 128 : g * 256 + 256]
             out_ref[g, 2 * u] = jnp.where(low, early, pltpu.roll(late, 64, 1))
             out_ref[g, 2 * u + 1] = jnp.where(low, pltpu.roll(early, 64, 1), late)
-
-
-def pack(x, groups):
+    for copy in copies[groups:]:
+        copy.wait()
+
+
+def pack(x, pdf_map, weight, mask, groups):
     local = x.shape[1]
     return pl.pallas_call(
         pack_kernel,
-        out_shape=jax.ShapeDtypeStruct((groups, 4, local, 128), F32),
-        in_specs=[hbm()],
-        out_specs=vmem(),
-        scratch_shapes=[pltpu.VMEM(x.shape, F32), pltpu.SemaphoreType.DMA],
+        out_shape=(
+            jax.ShapeDtypeStruct((groups, 4, local, 128), F32),
+            jax.ShapeDtypeStruct((1, pdf_map.shape[0]), jnp.int32),
+            jax.ShapeDtypeStruct(weight.shape, F32),
+            jax.ShapeDtypeStruct(mask.shape, jnp.int32),
+        ),
+        in_specs=[hbm()] * 4,
+        out_specs=[vmem()] * 4,
+        scratch_shapes=[pltpu.VMEM(x.shape, F32), pltpu.SemaphoreType.DMA((groups + 3,))],
         compiler_params=pltpu.CompilerParams(vmem_limit_bytes=4 << 20),
         name="pack",
-    )(pinned(x))
+    )(pinned(x), pinned(pdf_map[None, :]), pinned(weight), pinned(mask))
 
 
 def slot_kernel(sent, lengths_hbm, *refs):
@@ -451,11 +452,11 @@
 def shards(size, loglik, trans_weight, block_mask, init_weight, lengths, pdf_map):
     local = loglik.shape[2]
     groups = size // 4
-    x = pack(jnp.transpose(loglik, (0, 2, 1)), groups)
+    x, *tables = pack(jnp.transpose(loglik, (0, 2, 1)), pdf_map, trans_weight, block_mask, groups)
     frames = x.shape[3]
     x = x.reshape(size, local, frames)
     cols = lax.all_to_all(x, "tm", 0, 0, tiled=True).reshape(size * local, frames)
-    own, pre, e, top, th, tl, start = transfer(cols, trans_weight, block_mask, lengths, pdf_map, init_weight)
+    own, pre, e, top, th, tl, start = transfer(cols, *tables, lengths, init_weight)
     other = lax.ppermute(own, "tm", [(i, i ^ 1) for i in range(size)])
     (v,) = small(first_kernel, "first", [start.shape], start, own, other)
     square = own.shape[1:]

time: 53.8 us -> 53.4 us (level)
  transfers between devices with their start and end apart: 5 -> 5, of which waited for: 5 -> 5; matrix products, arithmetic and copies ran while one was open for 0% -> 0% of each run, Pallas kernels for 5% -> 6%
where the time goes in v8:
time: 53.4 us; the launch traced here: 53.2 us
  Pallas kernels  22.6 us (42%)
  blocking collectives  17.2 us (32%)
  waiting for transfers between devices  11.6 us (22%)
  starting transfers between devices  1.11 us (2%)
  between operations  0.68 us (1%)
    all_to_all x1, blocking collectives, shards(): lax.all_to_all(x, 'tm', 0, 0, tiled=True).reshape(size * local, frames)  17.2 us
    pallas_call x1, Pallas kernels, transfer(): pl.pallas_call(functools.partial(transfer_kernel, frames), out_shape=(out...  15.1 us
    ppermute x3, waiting for transfers between devices, shards(): vs.append(lax.ppermute(v, 'tm', pairs))  7.34 us
    pallas_call x2, Pallas kernels, slot_pass(): pl.pallas_call(functools.partial(slot_kernel, sent), out_shape=jax.ShapeD...  3.63 us
    pallas_call x5, Pallas kernels, small(): pl.pallas_call(kernel, out_shape=tuple((jax.ShapeDtypeStruct(shape, F32)...  2.61 us
    ppermute x1, waiting for transfers between devices, shards(): got = lax.ppermute(sent, 'tm', [(i, i ^ 2) for i in range(size)])  2.34 us
    ppermute x1, waiting for transfers between devices, shards(): other = lax.ppermute(own, 'tm', [(i, i ^ 1) for i in range(size)])  1.9 us
    pallas_call x1, Pallas kernels, pack(): pl.pallas_call(pack_kernel, out_shape=(jax.ShapeDtypeStruct((groups, 4, l...  1.25 us
  transfers between devices with their start and end apart: 5, of which 5 were waited for; matrix products, arithmetic and copies ran while one was open for 0% of the time, Pallas kernels for 6%

profile of v8, /device:TPU:0, one launch (start us, length us, event | category | flops | bytes accessed | tf_op | source)
XLA Modules:
  0.0 53.2 jit_solution(13665089102434923947)
XLA Ops:
  0.6 1.2 %pack.1 = (f32[4,4,32,128]{3,2,1,0:T(8,128)S(1)}, s32[1,256]{1,0:T(1,128)S(1)}, f32[256,256]{1,0:T(8,128)S(1)}, s32[4,4]{1,0:T(4,128)S(1)}) custom-call(f32[2,32,1024]{2,1,0:T(8,128)} %bitcast.7, s32[1,256]{1,0:T(1,128)} %bitcast.8, f32[256,256]{1,0:T(8,128)} %weight_hbm.1, s32[4,4]{1,0:T(4,128)} %mask_hbm.1), custom_call_target="tpu_custom_call" | custom-call | tf_op jit(solution)/shard_map/pack/pallas_call | solution.py:356
  1.9 17.2 %all_to_all.5 = f32[16,32,128]{2,1,0:T(8,128)S(1)} all-to-all(f32[16,32,128]{2,1,0:T(8,128)S(1)} %bitcast.6), channel_id=1, replica_groups=mesh['groups'=2,'tm'=16] {'tm'}, dimensions={0} | all-to-all | bytes 524288 | tf_op jit(solution)/shard_map/all_to_all | solution.py:458
  19.1 15.1 %transfer.1 = (f32[2,256,256]{2,1,0:T(8,128)S(1)}, bf16[2,8,2,256,256]{4,3,2,1,0:T(8,128)(2,1)S(1)}, f32[2,2,64,128]{3,2,1,0:T(8,128)S(1)}, f32[2,64,128]{2,1,0:...) custom-call(s32[2]{0:T(128)} %lengths_hbm.5, f32[1,256]{1,0:T(1,128)} %bitcast.9, ...), custom_call_target="tpu_custom_call" | custom-call | tf_op jit(solution)/shard_map/transfer/pallas_call | solution.py:239
  34.3 0.1 collective-permute-start
  34.3 1.9 %collective-permute-done.other_ref.refs_4_ = f32[2,256,256]{2,1,0:T(8,128)S(1)} collective-permute-done((f32[2,256,256]{2,1,0:T(8,128)S(1)}, f32[2,256,256]{2,1,0:T(8,128)S(1)}, u32[]{:S(2)}, u32[]{:S(2)}) %collective-permute-start) | collective-permute-done | bytes 524320 | tf_op jit(solution)/shard_map/ppermute | solution.py:460
  36.2 0.5 first.1
  36.8 0.3 collective-permute-start.1
  37.1 1.1 %group.1 = (f32[256,256]{1,0:T(8,128)S(1)}, f32[256,256]{1,0:T(8,128)S(1)}) custom-call(f32[2,256,256]{2,1,0:T(8,128)S(1)} %get-tuple-element.20.own_ref, f32[2,256,256]{2,1,0:T(8,128)S(1)} %collective-permute-done.other_ref.refs_4_), custom_call_target="tpu_custom_call" | custom-call | tf_op jit(solution)/shard_map/group/pallas_call | solution.py:324
  38.2 1.6 %collective-permute-done.1.v_ref.refs_1_ = f32[8,256]{1,0:T(8,128)S(1)} collective-permute-done((f32[8,256]{1,0:T(8,128)S(1)}, f32[8,256]{1,0:T(8,128)S(1)}, u32[]{:S(2)}, u32[]{:S(2)}) %collective-permute-start.1) | collective-permute-done | bytes 8224 | tf_op jit(solution)/shard_map/ppermute | solution.py:467
  39.9 0.1 hop.2
  40.0 0.1 collective-permute-start.2
  40.1 2.9 %collective-permute-done.2.v_ref.refs_2_ = f32[8,256]{1,0:T(8,128)S(1)} collective-permute-done((f32[8,256]{1,0:T(8,128)S(1)}, f32[8,256]{1,0:T(8,128)S(1)}, u32[]{:S(2)}, u32[]{:S(2)}) %collective-permute-start.2) | collective-permute-done | bytes 8224 | tf_op jit(solution)/shard_map/ppermute | solution.py:467
  43.1 0.1 hop.3
  43.2 0.3 collective-permute-start.3
  43.6 2.8 %collective-permute-done.3.refs_3_ = f32[8,256]{1,0:T(8,128)S(1)} collective-permute-done((f32[8,256]{1,0:T(8,128)S(1)}, f32[8,256]{1,0:T(8,128)S(1)}, u32[]{:S(2)}, u32[]{:S(2)}) %collective-permute-start.3) | collective-permute-done | bytes 8224 | tf_op jit(solution)/shard_map/ppermute | solution.py:467
  46.3 1.8 %sent.1 = f32[72,256]{1,0:T(8,128)S(1)} custom-call(s32[2]{0:T(128)} %lengths_hbm.5, f32[8,256]{1,0:T(8,128)S(1)} %get-tuple-element.19.start_ref.refs_0_, f32[8,256]{1,0:T(8,128)S(1)} %collective-permute-done.1.v_ref.refs_1_, f32[8,256]{1,0:T(8,128)S(1)} %collective-permute-done.2.v_ref.refs_2_, f32[8,256]{1,0:T(8,128)S(1)} %collective-permute-done.3.refs_3_, ...), custom_call_target="tpu_custom_call" | custom-call | tf_op jit(solution)/shard_map/sent/pallas_call | solution.py:426
  48.1 0.3 collective-permute-start.4
  48.4 1.8 %kept.1.kept_ref = f32[72,256]{1,0:T(8,128)S(1)} custom-call(s32[2]{0:T(128)} %lengths_hbm.5, f32[8,256]{1,0:T(8,128)S(1)} %get-tuple-element.19.start_ref.refs_0_, f32[8,256]{1,0:T(8,128)S(1)} %collective-permute-done.1.v_ref.refs_1_, f32[8,256]{1,0:T(8,128)S(1)} %collective-permute-done.2.v_ref.refs_2_, f32[8,256]{1,0:T(8,128)S(1)} %collective-permute-done.3.refs_3_, ...), custom_call_target="tpu_custom_call" | custom-call | tf_op jit(solution)/shard_map/kept/pallas_call | solution.py:426
  50.2 2.3 %collective-permute-done.4.got_ref = f32[72,256]{1,0:T(8,128)S(1)} collective-permute-done((f32[72,256]{1,0:T(8,128)S(1)}, f32[72,256]{1,0:T(8,128)S(1)}, u32[]{:S(2)}, u32[]{:S(2)}) %collective-permute-start.4) | collective-permute-done | bytes 73760 | tf_op jit(solution)/shard_map/ppermute | solution.py:472
  52.6 0.7 %join.1 = (f32[2,64,256]{2,1,0:T(8,128)}, f32[2,64]{1,0:T(2,128)}) custom-call(f32[72,256]{1,0:T(8,128)S(1)} %kept.1.kept_ref, f32[72,256]{1,0:T(8,128)S(1)} %collective-permute-done.4.got_ref), custom_call_target="tpu_custom_call" | custom-call | tf_op jit(solution)/shard_map/join/pallas_call | solution.py:324
Async XLA Ops:
  34.3 2.0 %collective-permute-start = (f32[2,256,256]{2,1,0:T(8,128)S(1)}, f32[2,256,256]{2,1,0:T(8,128)S(1)}, u32[]{:S(2)}, u32[]{:S(2)}) collective-permute-start(f32[2,256,256]{2,1,0:T(8,128)S(1)} %get-tuple-element.20.own_ref), channel_id=1, source_target_pairs={{0,1},{1,0},{2,3},{3,2},{4,5},{5,4},{6,7},{7,6},{8,9},{9,8},{10,11... | collective-permute-start | bytes 1572872 | tf_op jit(solution)/shard_map/ppermute | solution.py:460
  36.8 3.1 %collective-permute-start.1 = (f32[8,256]{1,0:T(8,128)S(1)}, f32[8,256]{1,0:T(8,128)S(1)}, u32[]{:S(2)}, u32[]{:S(2)}) collective-permute-start(f32[8,256]{1,0:T(8,128)S(1)} %first.1), channel_id=1, source_target_pairs={{0,5},{1,4},{2,7},{3,6},{4,1},{5,0},{6,3},{7,2},{8,13},{9,12},{10,... | collective-permute-start | bytes 24584 | tf_op jit(solution)/shard_map/ppermute | solution.py:467
  40.0 3.1 %collective-permute-start.2 = (f32[8,256]{1,0:T(8,128)S(1)}, f32[8,256]{1,0:T(8,128)S(1)}, u32[]{:S(2)}, u32[]{:S(2)}) collective-permute-start(f32[8,256]{1,0:T(8,128)S(1)} %hop.2), channel_id=1, source_target_pairs={{0,3},{1,2},{2,1},{3,0},{4,9},{5,8},{6,11},{7,10},{8,5},{9,4},{10,... | collective-permute-start | bytes 24584 | tf_op jit(solution)/shard_map/ppermute | solution.py:467
  43.2 3.1 %collective-permute-start.3 = (f32[8,256]{1,0:T(8,128)S(1)}, f32[8,256]{1,0:T(8,128)S(1)}, u32[]{:S(2)}, u32[]{:S(2)}) collective-permute-start(f32[8,256]{1,0:T(8,128)S(1)} %hop.3), channel_id=1, source_target_pairs={{0,5},{1,4},{2,7},{3,6},{4,1},{5,0},{6,3},{7,2},{8,13},{9,12},{10,... | collective-permute-start | bytes 24584 | tf_op jit(solution)/shard_map/ppermute | solution.py:467
  48.1 4.4 %collective-permute-start.4 = (f32[72,256]{1,0:T(8,128)S(1)}, f32[72,256]{1,0:T(8,128)S(1)}, u32[]{:S(2)}, u32[]{:S(2)}) collective-permute-start(f32[72,256]{1,0:T(8,128)S(1)} %sent.1), channel_id=1, source_target_pairs={{0,2},{1,3},{2,0},{3,1},{4,6},{5,7},{6,4},{7,5},{8,10},{9,11},{10,... | collective-permute-start | bytes 221192 | tf_op jit(solution)/shard_map/ppermute | solution.py:472

commit v9 on v8

--- a/solution.py
+++ b/solution.py
@@ -17,6 +17,12 @@
     return (index // 2) % 2, (first, first + 2 * half)
 
 
+def frames_of(lengths_ref, utt):
+    row = lengths_ref[...].astype(F32)
+    here = lax.broadcasted_iota(jnp.int32, row.shape, 1) == utt
+    return jnp.sum(jnp.where(here, row, 0.0)).astype(jnp.int32)
+
+
 def halves(x):
     high = x.astype(BF16)
     return high, (x - high.astype(F32)).astype(BF16)
@@ -32,12 +38,12 @@
 
 def transfer_kernel(
     frames,
-    lengths_hbm,
-    init_hbm,
     cols_ref,
     map_ref,
     weight_ref,
     mask_ref,
+    lengths_ref,
+    init_ref,
     mats_ref,
     pre_ref,
     e_ref,
@@ -52,21 +58,7 @@
     al,
     bh,
     bl,
-    lengths_ref,
-    init_ref,
-    sems,
 ):
-    copies = [
-        pltpu.make_async_copy(src, dst, sems.at[i])
-        for i, (src, dst) in enumerate(
-            (
-                (lengths_hbm, lengths_ref),
-                (init_hbm, init_ref),
-            )
-        )
-    ]
-    for copy in copies:
-        copy.start()
     states = weight_ref.shape[0]
     half = frames // 2
     rows = states // 2
@@ -114,9 +106,7 @@
     th_ref[...] = th
     tl_ref[...] = tl
 
-    for copy in copies:
-        copy.wait()
-    alive = [lengths_ref[utt] - slot for slot in slots]
+    alive = [frames_of(lengths_ref, utt) - slot for slot in slots]
     eye = (
         lax.broadcasted_iota(jnp.int32, (states, states), 0) == lax.broadcasted_iota(jnp.int32, (states, states), 1)
     ).astype(F32)
@@ -150,7 +140,8 @@
                 pltpu.matmul_acc_lhs(accs[1][m], bh[sl, :], 0)
                 pltpu.matmul_acc_lhs(accs[1][m], bl[sl, :], None)
 
-        def post(k, s, r, peak, freeze):
+        def post(k, j, r, peak, freeze):
+            s = j * SUB + r
             look, use = r % 4 == 1 + 2 * k, r % 4 == (2 + 2 * k) % 4
             mh, ml = mats[k]
             er = e_scr[pl.ds(s + k * half, 1), :]
@@ -167,35 +158,32 @@
                     l = jnp.where(live, l, ml[sl, :])
                 mh[sl, :] = h
                 ml[sl, :] = l
+                if r == SUB - 1:
+                    pre_ref[k, j, 0, sl, :] = h
+                    pre_ref[k, j, 1, sl, :] = l
                 if look:
                     y = jnp.max(h.reshape(rows // 16, 16, states), axis=0)
                     new = y if new is None else jnp.maximum(new, y)
             return new if look else peak
 
-        def keep(j):
-            for k in range(2):
-                for i in range(2):
-                    pre_ref[k, j, i] = mats[k][i][0:states, :]
-
         for m in range(2):
             pltpu.matmul_push_rhs(th_ref[...], 0, m)
         issue_a(0)
         one = jnp.ones((16, states), BF16)
 
-        def step(s, r, peaks, freeze, last=False):
+        def step(j, r, peaks, freeze, last=False):
             pa, pb = peaks
             issue_b()
-            pa = post(0, s, r, pa, freeze)
+            pa = post(0, j, r, pa, freeze)
             if not last:
                 issue_a(None)
-            pb = post(1, s, r, pb, freeze)
+            pb = post(1, j, r, pb, freeze)
             return pa, pb
 
         def eight(j, peaks, freeze):
             for r in range(1, SUB):
-                peaks = step(j * SUB + r, r, peaks, freeze)
-            keep(j)
-            return step(j * SUB + SUB, SUB, peaks, freeze)
+                peaks = step(j, r, peaks, freeze)
+            return step(j, SUB, peaks, freeze)
 
         def block(j, peaks):
             full = jnp.minimum(alive[0], alive[1]) > j * SUB + SUB
@@ -203,8 +191,7 @@
 
         peaks = lax.fori_loop(0, blocks - 1, block, (one, one))
         for r in range(1, SUB):
-            peaks = step((blocks - 1) * SUB + r, r, peaks, True, r == SUB - 1)
-        keep(blocks - 1)
+            peaks = step(blocks - 1, r, peaks, True, r == SUB - 1)
         start_ref[...] = jnp.broadcast_to(unit(init_ref[...]), start_ref.shape)
         for i, (mh, ml) in enumerate(mats):
             mats_ref[i] = mh[0:states, :].astype(F32) + ml[0:states, :].astype(F32)
@@ -247,19 +234,14 @@
             out((states, states), BF16),
             out((8, states), F32),
         ),
-        in_specs=[hbm()] * 2 + [vmem()] * 4,
+        in_specs=[vmem()] * 6,
         out_specs=[vmem()] * 7,
         scratch_shapes=[pltpu.VMEM((frames, states), F32)] * 2
         + [pltpu.VMEM((states, states), F32)]
-        + [pltpu.VMEM((states, states), BF16)] * 4
-        + [
-            pltpu.SMEM(lengths.shape, jnp.int32),
-            pltpu.VMEM((1, states), F32),
-            pltpu.SemaphoreType.DMA((2,)),
-        ],
+        + [pltpu.VMEM((states, states), BF16)] * 4,
         compiler_params=pltpu.CompilerParams(vmem_limit_bytes=6 << 20),
         name="transfer",
-    )(*map(pinned, (lengths, init[None, :])), cols, columns_of, weight, mask)
+    )(cols, columns_of, weight, mask, lengths, init)
 
 
 def row_dot(v, matrix_high, matrix_low):
@@ -331,10 +313,11 @@
     )(*args)
 
 
-def pack_kernel(x_hbm, map_hbm, weight_hbm, mask_hbm, out_ref, map_ref, weight_ref, mask_ref, x_ref, sems):
+def pack_kernel(tables, x_hbm, *refs):
+    table_hbms, out_ref, table_refs, (x_ref, sems) = refs[:tables], refs[tables], refs[tables + 1 : -2], refs[-2:]
     groups = out_ref.shape[0]
     pairs = [(x_hbm.at[:, :, pl.ds(g * 256, 256)], x_ref.at[:, :, pl.ds(g * 256, 256)]) for g in range(groups)]
-    pairs += [(map_hbm, map_ref), (weight_hbm, weight_ref), (mask_hbm, mask_ref)]
+    pairs += zip(table_hbms, table_refs)
     copies = [pltpu.make_async_copy(src, dst, sems.at[i]) for i, (src, dst) in enumerate(pairs)]
     for copy in copies:
         copy.start()
@@ -351,30 +334,24 @@
         copy.wait()
 
 
-def pack(x, pdf_map, weight, mask, groups):
+def pack(x, groups, *tables):
     local = x.shape[1]
+    n = len(tables)
+    packed = jax.ShapeDtypeStruct((groups, 4, local, 128), F32)
     return pl.pallas_call(
-        pack_kernel,
-        out_shape=(
-            jax.ShapeDtypeStruct((groups, 4, local, 128), F32),
-            jax.ShapeDtypeStruct((1, pdf_map.shape[0]), jnp.int32),
-            jax.ShapeDtypeStruct(weight.shape, F32),
-            jax.ShapeDtypeStruct(mask.shape, jnp.int32),
-        ),
-        in_specs=[hbm()] * 4,
-        out_specs=[vmem()] * 4,
-        scratch_shapes=[pltpu.VMEM(x.shape, F32), pltpu.SemaphoreType.DMA((groups + 3,))],
+        functools.partial(pack_kernel, n),
+        out_shape=(packed, *(jax.ShapeDtypeStruct(t.shape, t.dtype) for t in tables)),
+        in_specs=[hbm()] * (n + 1),
+        out_specs=[vmem()] * (n + 1),
+        scratch_shapes=[pltpu.VMEM(x.shape, F32), pltpu.SemaphoreType.DMA((groups + n,))],
         compiler_params=pltpu.CompilerParams(vmem_limit_bytes=4 << 20),
         name="pack",
-    )(pinned(x), pinned(pdf_map[None, :]), pinned(weight), pinned(mask))
-
-
-def slot_kernel(sent, lengths_hbm, *refs):
-    start_ref, *v_refs = refs[:-11]
-    other_ref, mid_ref, pre_ref, e_ref, top_ref, th_ref, tl_ref, out_ref, *scratch = refs[len(v_refs) + 1 :]
-    alpha_scr, lengths_ref, sem = scratch
-    copy = pltpu.make_async_copy(lengths_hbm, lengths_ref, sem)
-    copy.start()
+    )(*map(pinned, (x, *tables)))
+
+
+def slot_kernel(sent, lengths_ref, *refs):
+    start_ref, *v_refs = refs[:-9]
+    other_ref, mid_ref, pre_ref, e_ref, top_ref, th_ref, tl_ref, out_ref, alpha_scr = refs[len(v_refs) + 1 :]
     states = th_ref.shape[0]
     half = top_ref.shape[1]
     blocks = half // SUB
@@ -396,8 +373,7 @@
     lane = lax.broadcasted_iota(jnp.int32, (blocks, 128), 1)
     sub = lax.broadcasted_iota(jnp.int32, (blocks, 128), 0)
     gains = jnp.zeros((blocks, 128), F32)
-    copy.wait()
-    left = lengths_ref[utt] - jnp.where(slot == 0, slots[0], slots[1])
+    left = frames_of(lengths_ref, utt) - jnp.where(slot == 0, slots[0], slots[1])
     tiles = range(states // 128)
     for r in range(SUB):
         every = pl.ds(r, blocks, stride=SUB)
@@ -426,16 +402,12 @@
     return pl.pallas_call(
         functools.partial(slot_kernel, sent),
         out_shape=jax.ShapeDtypeStruct((half + 8, states), F32),
-        in_specs=[hbm()] + [vmem()] * (len(vs) + 7),
+        in_specs=[vmem()] * (len(vs) + 8),
         out_specs=vmem(),
-        scratch_shapes=[
-            pltpu.VMEM((states // 128, half, 128), F32),
-            pltpu.SMEM(lengths.shape, jnp.int32),
-            pltpu.SemaphoreType.DMA,
-        ],
+        scratch_shapes=[pltpu.VMEM((states // 128, half, 128), F32)],
         compiler_params=pltpu.CompilerParams(vmem_limit_bytes=6 << 20),
         name="sent" if sent else "kept",
-    )(pinned(lengths), *vs, other, mid, pre, e, top, th, tl)
+    )(lengths, *vs, other, mid, pre, e, top, th, tl)
 
 
 def join_kernel(kept_ref, got_ref, log_ref, gain_ref):
@@ -452,11 +424,12 @@
 def shards(size, loglik, trans_weight, block_mask, init_weight, lengths, pdf_map):
     local = loglik.shape[2]
     groups = size // 4
-    x, *tables = pack(jnp.transpose(loglik, (0, 2, 1)), pdf_map, trans_weight, block_mask, groups)
+    tables = (pdf_map[None, :], trans_weight, block_mask, lengths[None, :], init_weight[None, :])
+    x, *tables = pack(jnp.transpose(loglik, (0, 2, 1)), groups, *tables)
     frames = x.shape[3]
     x = x.reshape(size, local, frames)
     cols = lax.all_to_all(x, "tm", 0, 0, tiled=True).reshape(size * local, frames)
-    own, pre, e, top, th, tl, start = transfer(cols, *tables, lengths, init_weight)
+    own, pre, e, top, th, tl, start = transfer(cols, *tables)
     other = lax.ppermute(own, "tm", [(i, i ^ 1) for i in range(size)])
     (v,) = small(first_kernel, "first", [start.shape], start, own, other)
     square = own.shape[1:]
@@ -467,7 +440,7 @@
         vs.append(lax.ppermute(v, "tm", pairs))
         if g < groups - 1:
             (v,) = small(hop_kernel, "hop", [v.shape], vs[-1], whole)
-    given = (lengths, vs, other, mid, pre, e, top, th, tl)
+    given = (tables[3], vs, other, mid, pre, e, top, th, tl)
     sent = slot_pass(True, *given)
     got = lax.ppermute(sent, "tm", [(i, i ^ 2) for i in range(size)])
     kept = slot_pass(False, *given)

time: 53.4 us -> 52.8 us (0.989)
  Pallas kernels: 22.6 us -> 21.8 us
  transfers between devices with their start and end apart: 5 -> 5, of which waited for: 5 -> 5; matrix products, arithmetic and copies ran while one was open for 0% -> 0% of each run, Pallas kernels for 6% -> 5%
where the time goes in v9:
time: 52.8 us; the launch traced here: 52.6 us
  Pallas kernels  21.8 us (41%)
  blocking collectives  17.2 us (33%)
  waiting for transfers between devices  11.8 us (22%)
  starting transfers between devices  1.11 us (2%)
  between operations  0.69 us (1%)
    all_to_all x1, blocking collectives, shards(): lax.all_to_all(x, 'tm', 0, 0, tiled=True).reshape(size * local, frames)  17.2 us
    pallas_call x1, Pallas kernels, transfer(): pl.pallas_call(functools.partial(transfer_kernel, frames), out_shape=(out...  14.7 us
    ppermute x3, waiting for transfers between devices, shards(): vs.append(lax.ppermute(v, 'tm', pairs))  7.33 us
    pallas_call x2, Pallas kernels, slot_pass(): pl.pallas_call(functools.partial(slot_kernel, sent), out_shape=jax.ShapeD...  3.24 us
    pallas_call x5, Pallas kernels, small(): pl.pallas_call(kernel, out_shape=tuple((jax.ShapeDtypeStruct(shape, F32)...  2.61 us
    ppermute x1, waiting for transfers between devices, shards(): got = lax.ppermute(sent, 'tm', [(i, i ^ 2) for i in range(size)])  2.54 us
    ppermute x1, waiting for transfers between devices, shards(): other = lax.ppermute(own, 'tm', [(i, i ^ 1) for i in range(size)])  1.9 us
    pallas_call x1, Pallas kernels, pack(): pl.pallas_call(functools.partial(pack_kernel, n), out_shape=(packed, *(ja...  1.27 us
  transfers between devices with their start and end apart: 5, of which 5 were waited for; matrix products, arithmetic and copies ran while one was open for 0% of the time, Pallas kernels for 5%

profile of v9, /device:TPU:0, one launch (start us, length us, event | category | flops | bytes accessed | tf_op | source)
XLA Modules:
  0.0 52.6 jit_solution(17602040239132109354)
XLA Ops:
  0.6 1.3 %pack.1 = (f32[4,4,32,128]{3,2,1,0:T(8,128)S(1)}, s32[1,256]{1,0:T(1,128)S(1)}, f32[256,256]{1,0:T(8,128)S(1)}, s32[4,4]{1,0:T(4,128)S(1)}, s32[1,2]{1,0:T(1,128)S(1)}, /*index=5*/f32[1,256]{1,0:T(1,128)S(1)}) custom-call(f32[2,32,1024]{2,1,0:T(8,128)} %bitcast.8, s32[1,256]{1,0:T(1,128)} %bitcast.9, f32[256,256]{1,0:T(8,128)} %refs_1_.1, s32[4,4]{1,0:T(4,128)} %refs_2_.1, ...), custom_call_target="tpu_custom_call" | custom-call | tf_op jit(solution)/shard_map/pack/pallas_call | solution.py:341
  1.9 17.2 %all_to_all.5 = f32[16,32,128]{2,1,0:T(8,128)S(1)} all-to-all(f32[16,32,128]{2,1,0:T(8,128)S(1)} %bitcast.7), channel_id=1, replica_groups=mesh['groups'=2,'tm'=16] {'tm'}, dimensions={0} | all-to-all | bytes 524288 | tf_op jit(solution)/shard_map/all_to_all | solution.py:431
  19.1 14.7 %transfer.1 = (f32[2,256,256]{2,1,0:T(8,128)S(1)}, bf16[2,8,2,256,256]{4,3,2,1,0:T(8,128)(2,1)S(1)}, f32[2,2,64,128]{3,2,1,0:T(8,128)S(1)}, f32[2,64,128]{2,1,0:...) custom-call(f32[512,128]{1,0:T(8,128)S(1)} %bitcast.6, ...), custom_call_target="tpu_custom_call" | custom-call | tf_op jit(solution)/shard_map/transfer/pallas_call | solution.py:226
  33.8 0.1 collective-permute-start
  33.9 1.9 %collective-permute-done.other_ref.refs_4_ = f32[2,256,256]{2,1,0:T(8,128)S(1)} collective-permute-done((f32[2,256,256]{2,1,0:T(8,128)S(1)}, f32[2,256,256]{2,1,0:T(8,128)S(1)}, u32[]{:S(2)}, u32[]{:S(2)}) %collective-permute-start) | collective-permute-done | bytes 524320 | tf_op jit(solution)/shard_map/ppermute | solution.py:433
  35.8 0.5 first.1
  36.3 0.3 collective-permute-start.1
  36.6 1.1 %group.1 = (f32[256,256]{1,0:T(8,128)S(1)}, f32[256,256]{1,0:T(8,128)S(1)}) custom-call(f32[2,256,256]{2,1,0:T(8,128)S(1)} %get-tuple-element.24.own_ref, f32[2,256,256]{2,1,0:T(8,128)S(1)} %collective-permute-done.other_ref.refs_4_), custom_call_target="tpu_custom_call" | custom-call | tf_op jit(solution)/shard_map/group/pallas_call | solution.py:306
  37.8 1.6 %collective-permute-done.1.v_ref.refs_1_ = f32[8,256]{1,0:T(8,128)S(1)} collective-permute-done((f32[8,256]{1,0:T(8,128)S(1)}, f32[8,256]{1,0:T(8,128)S(1)}, u32[]{:S(2)}, u32[]{:S(2)}) %collective-permute-start.1) | collective-permute-done | bytes 8224 | tf_op jit(solution)/shard_map/ppermute | solution.py:440
  39.4 0.1 hop.2
  39.6 0.1 collective-permute-start.2
  39.7 2.9 %collective-permute-done.2.v_ref.refs_2_ = f32[8,256]{1,0:T(8,128)S(1)} collective-permute-done((f32[8,256]{1,0:T(8,128)S(1)}, f32[8,256]{1,0:T(8,128)S(1)}, u32[]{:S(2)}, u32[]{:S(2)}) %collective-permute-start.2) | collective-permute-done | bytes 8224 | tf_op jit(solution)/shard_map/ppermute | solution.py:440
  42.6 0.1 hop.3
  42.8 0.3 collective-permute-start.3
  43.1 2.8 %collective-permute-done.3.refs_3_ = f32[8,256]{1,0:T(8,128)S(1)} collective-permute-done((f32[8,256]{1,0:T(8,128)S(1)}, f32[8,256]{1,0:T(8,128)S(1)}, u32[]{:S(2)}, u32[]{:S(2)}) %collective-permute-start.3) | collective-permute-done | bytes 8224 | tf_op jit(solution)/shard_map/ppermute | solution.py:440
  45.9 1.6 %sent.1 = f32[72,256]{1,0:T(8,128)S(1)} custom-call(s32[1,2]{1,0:T(1,128)S(1)} %get-tuple-element.17.lengths_ref, f32[8,256]{1,0:T(8,128)S(1)} %get-tuple-element.23.start_ref.refs_0_, f32[8,256]{1,0:T(8,128)S(1)} %collective-permute-done.1.v_ref.refs_1_, f32[8,256]{1,0:T(8,128)S(1)} %collective-permute-done.2.v_ref.refs_2_, ...), custom_call_target="tpu_custom_call" | custom-call | tf_op jit(solution)/shard_map/sent/pallas_call | solution.py:402
  47.5 0.2 collective-permute-start.4
  47.8 1.6 %kept.1.kept_ref = f32[72,256]{1,0:T(8,128)S(1)} custom-call(s32[1,2]{1,0:T(1,128)S(1)} %get-tuple-element.17.lengths_ref, f32[8,256]{1,0:T(8,128)S(1)} %get-tuple-element.23.start_ref.refs_0_, f32[8,256]{1,0:T(8,128)S(1)} %collective-permute-done.1.v_ref.refs_1_, f32[8,256]{1,0:T(8,128)S(1)} %collective-permute-done.2.v_ref.refs_2_, ...), custom_call_target="tpu_custom_call" | custom-call | tf_op jit(solution)/shard_map/kept/pallas_call | solution.py:402
  49.4 2.5 %collective-permute-done.4.got_ref = f32[72,256]{1,0:T(8,128)S(1)} collective-permute-done((f32[72,256]{1,0:T(8,128)S(1)}, f32[72,256]{1,0:T(8,128)S(1)}, u32[]{:S(2)}, u32[]{:S(2)}) %collective-permute-start.4) | collective-permute-done | bytes 73760 | tf_op jit(solution)/shard_map/ppermute | solution.py:445
  51.9 0.7 %join.1 = (f32[2,64,256]{2,1,0:T(8,128)}, f32[2,64]{1,0:T(2,128)}) custom-call(f32[72,256]{1,0:T(8,128)S(1)} %kept.1.kept_ref, f32[72,256]{1,0:T(8,128)S(1)} %collective-permute-done.4.got_ref), custom_call_target="tpu_custom_call" | custom-call | tf_op jit(solution)/shard_map/join/pallas_call | solution.py:306
Async XLA Ops:
  33.8 2.0 %collective-permute-start = (f32[2,256,256]{2,1,0:T(8,128)S(1)}, f32[2,256,256]{2,1,0:T(8,128)S(1)}, u32[]{:S(2)}, u32[]{:S(2)}) collective-permute-start(f32[2,256,256]{2,1,0:T(8,128)S(1)} %get-tuple-element.24.own_ref), channel_id=1, source_target_pairs={{0,1},{1,0},{2,3},{3,2},{4,5},{5,4},{6,7},{7,6},{8,9},{9,8},{10,11... | collective-permute-start | bytes 1572872 | tf_op jit(solution)/shard_map/ppermute | solution.py:433
  36.3 3.1 %collective-permute-start.1 = (f32[8,256]{1,0:T(8,128)S(1)}, f32[8,256]{1,0:T(8,128)S(1)}, u32[]{:S(2)}, u32[]{:S(2)}) collective-permute-start(f32[8,256]{1,0:T(8,128)S(1)} %first.1), channel_id=1, source_target_pairs={{0,5},{1,4},{2,7},{3,6},{4,1},{5,0},{6,3},{7,2},{8,13},{9,12},{10,... | collective-permute-start | bytes 24584 | tf_op jit(solution)/shard_map/ppermute | solution.py:440
  39.6 3.1 %collective-permute-start.2 = (f32[8,256]{1,0:T(8,128)S(1)}, f32[8,256]{1,0:T(8,128)S(1)}, u32[]{:S(2)}, u32[]{:S(2)}) collective-permute-start(f32[8,256]{1,0:T(8,128)S(1)} %hop.2), channel_id=1, source_target_pairs={{0,3},{1,2},{2,1},{3,0},{4,9},{5,8},{6,11},{7,10},{8,5},{9,4},{10,... | collective-permute-start | bytes 24584 | tf_op jit(solution)/shard_map/ppermute | solution.py:440
  42.8 3.1 %collective-permute-start.3 = (f32[8,256]{1,0:T(8,128)S(1)}, f32[8,256]{1,0:T(8,128)S(1)}, u32[]{:S(2)}, u32[]{:S(2)}) collective-permute-start(f32[8,256]{1,0:T(8,128)S(1)} %hop.3), channel_id=1, source_target_pairs={{0,5},{1,4},{2,7},{3,6},{4,1},{5,0},{6,3},{7,2},{8,13},{9,12},{10,... | collective-permute-start | bytes 24584 | tf_op jit(solution)/shard_map/ppermute | solution.py:440
  47.5 4.4 %collective-permute-start.4 = (f32[72,256]{1,0:T(8,128)S(1)}, f32[72,256]{1,0:T(8,128)S(1)}, u32[]{:S(2)}, u32[]{:S(2)}) collective-permute-start(f32[72,256]{1,0:T(8,128)S(1)} %sent.1), channel_id=1, source_target_pairs={{0,2},{1,3},{2,0},{3,1},{4,6},{5,7},{6,4},{7,5},{8,10},{9,11},{10,... | collective-permute-start | bytes 221192 | tf_op jit(solution)/shard_map/ppermute | solution.py:445

commit v10 on v9

--- a/solution.py
+++ b/solution.py
@@ -190,8 +190,13 @@
             return lax.cond(full, lambda p: eight(j, p, False), lambda p: eight(j, p, True), peaks)
 
         peaks = lax.fori_loop(0, blocks - 1, block, (one, one))
-        for r in range(1, SUB):
-            peaks = step(blocks - 1, r, peaks, True, r == SUB - 1)
+        def tail(peaks, freeze):
+            for r in range(1, SUB):
+                peaks = step(blocks - 1, r, peaks, freeze, r == SUB - 1)
+            return peaks
+
+        full = jnp.minimum(alive[0], alive[1]) >= half
+        lax.cond(full, lambda p: tail(p, False), lambda p: tail(p, True), peaks)
         start_ref[...] = jnp.broadcast_to(unit(init_ref[...]), start_ref.shape)
         for i, (mh, ml) in enumerate(mats):
             mats_ref[i] = mh[0:states, :].astype(F32) + ml[0:states, :].astype(F32)
@@ -316,21 +321,21 @@
 def pack_kernel(tables, x_hbm, *refs):
     table_hbms, out_ref, table_refs, (x_ref, sems) = refs[:tables], refs[tables], refs[tables + 1 : -2], refs[-2:]
     groups = out_ref.shape[0]
-    pairs = [(x_hbm.at[:, :, pl.ds(g * 256, 256)], x_ref.at[:, :, pl.ds(g * 256, 256)]) for g in range(groups)]
-    pairs += zip(table_hbms, table_refs)
+    pairs = [(x_hbm, x_ref), *zip(table_hbms, table_refs)]
     copies = [pltpu.make_async_copy(src, dst, sems.at[i]) for i, (src, dst) in enumerate(pairs)]
     for copy in copies:
         copy.start()
     local = out_ref.shape[2]
     low = lax.broadcasted_iota(jnp.int32, (local, 128), 1) < 64
     for g in range(groups):
-        copies[g].wait()
+        if g == 0:
+            copies[0].wait()
         for u in range(2):
             early = x_ref[u, :, g * 256 : g * 256 + 128]
             late = x_ref[u, :, g * 256 + 128 : g * 256 + 256]
             out_ref[g, 2 * u] = jnp.where(low, early, pltpu.roll(late, 64, 1))
             out_ref[g, 2 * u + 1] = jnp.where(low, pltpu.roll(early, 64, 1), late)
-    for copy in copies[groups:]:
+    for copy in copies[1:]:
         copy.wait()
 
 

time: 52.8 us -> 52.7 us (level)
  no operation moved by 1% of the time
where the time goes in v10:
time: 52.7 us; the launch traced here: 52.5 us
  Pallas kernels  21.7 us (41%)
  blocking collectives  17.2 us (33%)
  waiting for transfers between devices  11.8 us (22%)
  starting transfers between devices  1.11 us (2%)
  between operations  0.68 us (1%)
    all_to_all x1, blocking collectives, shards(): lax.all_to_all(x, 'tm', 0, 0, tiled=True).reshape(size * local, frames)  17.2 us
    pallas_call x1, Pallas kernels, transfer(): pl.pallas_call(functools.partial(transfer_kernel, frames), out_shape=(out...  14.7 us
    ppermute x3, waiting for transfers between devices, shards(): vs.append(lax.ppermute(v, 'tm', pairs))  7.33 us
    pallas_call x2, Pallas kernels, slot_pass(): pl.pallas_call(functools.partial(slot_kernel, sent), out_shape=jax.ShapeD...  3.24 us
    pallas_call x5, Pallas kernels, small(): pl.pallas_call(kernel, out_shape=tuple((jax.ShapeDtypeStruct(shape, F32)...  2.61 us
    ppermute x1, waiting for transfers between devices, shards(): got = lax.ppermute(sent, 'tm', [(i, i ^ 2) for i in range(size)])  2.54 us
    ppermute x1, waiting for transfers between devices, shards(): other = lax.ppermute(own, 'tm', [(i, i ^ 1) for i in range(size)])  1.9 us
    pallas_call x1, Pallas kernels, pack(): pl.pallas_call(functools.partial(pack_kernel, n), out_shape=(packed, *(ja...  1.17 us
  transfers between devices with their start and end apart: 5, of which 5 were waited for; matrix products, arithmetic and copies ran while one was open for 0% of the time, Pallas kernels for 5%

profile of v10, /device:TPU:0, one launch (start us, length us, event | category | flops | bytes accessed | tf_op | source)
XLA Modules:
  0.0 52.5 jit_solution(5012775637555705644)
XLA Ops:
  0.6 1.2 %pack.1 = (f32[4,4,32,128]{3,2,1,0:T(8,128)S(1)}, s32[1,256]{1,0:T(1,128)S(1)}, f32[256,256]{1,0:T(8,128)S(1)}, s32[4,4]{1,0:T(4,128)S(1)}, s32[1,2]{1,0:T(1,128)S(1)}, /*index=5*/f32[1,256]{1,0:T(1,128)S(1)}) custom-call(f32[2,32,1024]{2,1,0:T(8,128)} %bitcast.8, s32[1,256]{1,0:T(1,128)} %bitcast.9, f32[256,256]{1,0:T(8,128)} %refs_1_.1, s32[4,4]{1,0:T(4,128)} %refs_2_.1, ...), custom_call_target="tpu_custom_call" | custom-call | tf_op jit(solution)/shard_map/pack/pallas_call | solution.py:346
  1.8 17.2 %all_to_all.5 = f32[16,32,128]{2,1,0:T(8,128)S(1)} all-to-all(f32[16,32,128]{2,1,0:T(8,128)S(1)} %bitcast.7), channel_id=1, replica_groups=mesh['groups'=2,'tm'=16] {'tm'}, dimensions={0} | all-to-all | bytes 524288 | tf_op jit(solution)/shard_map/all_to_all | solution.py:436
  19.0 14.7 %transfer.1 = (f32[2,256,256]{2,1,0:T(8,128)S(1)}, bf16[2,8,2,256,256]{4,3,2,1,0:T(8,128)(2,1)S(1)}, f32[2,2,64,128]{3,2,1,0:T(8,128)S(1)}, f32[2,64,128]{2,1,0:...) custom-call(f32[512,128]{1,0:T(8,128)S(1)} %bitcast.6, ...), custom_call_target="tpu_custom_call" | custom-call | tf_op jit(solution)/shard_map/transfer/pallas_call | solution.py:231
  33.7 0.1 collective-permute-start
  33.8 1.9 %collective-permute-done.other_ref.refs_4_ = f32[2,256,256]{2,1,0:T(8,128)S(1)} collective-permute-done((f32[2,256,256]{2,1,0:T(8,128)S(1)}, f32[2,256,256]{2,1,0:T(8,128)S(1)}, u32[]{:S(2)}, u32[]{:S(2)}) %collective-permute-start) | collective-permute-done | bytes 524320 | tf_op jit(solution)/shard_map/ppermute | solution.py:438
  35.7 0.5 first.1
  36.2 0.3 collective-permute-start.1
  36.5 1.1 %group.1 = (f32[256,256]{1,0:T(8,128)S(1)}, f32[256,256]{1,0:T(8,128)S(1)}) custom-call(f32[2,256,256]{2,1,0:T(8,128)S(1)} %get-tuple-element.24.own_ref, f32[2,256,256]{2,1,0:T(8,128)S(1)} %collective-permute-done.other_ref.refs_4_), custom_call_target="tpu_custom_call" | custom-call | tf_op jit(solution)/shard_map/group/pallas_call | solution.py:311
  37.7 1.6 %collective-permute-done.1.v_ref.refs_1_ = f32[8,256]{1,0:T(8,128)S(1)} collective-permute-done((f32[8,256]{1,0:T(8,128)S(1)}, f32[8,256]{1,0:T(8,128)S(1)}, u32[]{:S(2)}, u32[]{:S(2)}) %collective-permute-start.1) | collective-permute-done | bytes 8224 | tf_op jit(solution)/shard_map/ppermute | solution.py:445
  39.3 0.1 hop.2
  39.4 0.1 collective-permute-start.2
  39.6 2.9 %collective-permute-done.2.v_ref.refs_2_ = f32[8,256]{1,0:T(8,128)S(1)} collective-permute-done((f32[8,256]{1,0:T(8,128)S(1)}, f32[8,256]{1,0:T(8,128)S(1)}, u32[]{:S(2)}, u32[]{:S(2)}) %collective-permute-start.2) | collective-permute-done | bytes 8224 | tf_op jit(solution)/shard_map/ppermute | solution.py:445
  42.5 0.1 hop.3
  42.7 0.3 collective-permute-start.3
  43.0 2.8 %collective-permute-done.3.refs_3_ = f32[8,256]{1,0:T(8,128)S(1)} collective-permute-done((f32[8,256]{1,0:T(8,128)S(1)}, f32[8,256]{1,0:T(8,128)S(1)}, u32[]{:S(2)}, u32[]{:S(2)}) %collective-permute-start.3) | collective-permute-done | bytes 8224 | tf_op jit(solution)/shard_map/ppermute | solution.py:445
  45.8 1.6 %sent.1 = f32[72,256]{1,0:T(8,128)S(1)} custom-call(s32[1,2]{1,0:T(1,128)S(1)} %get-tuple-element.17.lengths_ref, f32[8,256]{1,0:T(8,128)S(1)} %get-tuple-element.23.start_ref.refs_0_, f32[8,256]{1,0:T(8,128)S(1)} %collective-permute-done.1.v_ref.refs_1_, f32[8,256]{1,0:T(8,128)S(1)} %collective-permute-done.2.v_ref.refs_2_, ...), custom_call_target="tpu_custom_call" | custom-call | tf_op jit(solution)/shard_map/sent/pallas_call | solution.py:407
  47.4 0.2 collective-permute-start.4
  47.6 1.6 %kept.1.kept_ref = f32[72,256]{1,0:T(8,128)S(1)} custom-call(s32[1,2]{1,0:T(1,128)S(1)} %get-tuple-element.17.lengths_ref, f32[8,256]{1,0:T(8,128)S(1)} %get-tuple-element.23.start_ref.refs_0_, f32[8,256]{1,0:T(8,128)S(1)} %collective-permute-done.1.v_ref.refs_1_, f32[8,256]{1,0:T(8,128)S(1)} %collective-permute-done.2.v_ref.refs_2_, ...), custom_call_target="tpu_custom_call" | custom-call | tf_op jit(solution)/shard_map/kept/pallas_call | solution.py:407
  49.3 2.5 %collective-permute-done.4.got_ref = f32[72,256]{1,0:T(8,128)S(1)} collective-permute-done((f32[72,256]{1,0:T(8,128)S(1)}, f32[72,256]{1,0:T(8,128)S(1)}, u32[]{:S(2)}, u32[]{:S(2)}) %collective-permute-start.4) | collective-permute-done | bytes 73760 | tf_op jit(solution)/shard_map/ppermute | solution.py:450
  51.8 0.7 %join.1 = (f32[2,64,256]{2,1,0:T(8,128)}, f32[2,64]{1,0:T(2,128)}) custom-call(f32[72,256]{1,0:T(8,128)S(1)} %kept.1.kept_ref, f32[72,256]{1,0:T(8,128)S(1)} %collective-permute-done.4.got_ref), custom_call_target="tpu_custom_call" | custom-call | tf_op jit(solution)/shard_map/join/pallas_call | solution.py:311
Async XLA Ops:
  33.7 2.0 %collective-permute-start = (f32[2,256,256]{2,1,0:T(8,128)S(1)}, f32[2,256,256]{2,1,0:T(8,128)S(1)}, u32[]{:S(2)}, u32[]{:S(2)}) collective-permute-start(f32[2,256,256]{2,1,0:T(8,128)S(1)} %get-tuple-element.24.own_ref), channel_id=1, source_target_pairs={{0,1},{1,0},{2,3},{3,2},{4,5},{5,4},{6,7},{7,6},{8,9},{9,8},{10,11... | collective-permute-start | bytes 1572872 | tf_op jit(solution)/shard_map/ppermute | solution.py:438
  36.2 3.1 %collective-permute-start.1 = (f32[8,256]{1,0:T(8,128)S(1)}, f32[8,256]{1,0:T(8,128)S(1)}, u32[]{:S(2)}, u32[]{:S(2)}) collective-permute-start(f32[8,256]{1,0:T(8,128)S(1)} %first.1), channel_id=1, source_target_pairs={{0,5},{1,4},{2,7},{3,6},{4,1},{5,0},{6,3},{7,2},{8,13},{9,12},{10,... | collective-permute-start | bytes 24584 | tf_op jit(solution)/shard_map/ppermute | solution.py:445
  39.4 3.1 %collective-permute-start.2 = (f32[8,256]{1,0:T(8,128)S(1)}, f32[8,256]{1,0:T(8,128)S(1)}, u32[]{:S(2)}, u32[]{:S(2)}) collective-permute-start(f32[8,256]{1,0:T(8,128)S(1)} %hop.2), channel_id=1, source_target_pairs={{0,3},{1,2},{2,1},{3,0},{4,9},{5,8},{6,11},{7,10},{8,5},{9,4},{10,... | collective-permute-start | bytes 24584 | tf_op jit(solution)/shard_map/ppermute | solution.py:445
  42.7 3.1 %collective-permute-start.3 = (f32[8,256]{1,0:T(8,128)S(1)}, f32[8,256]{1,0:T(8,128)S(1)}, u32[]{:S(2)}, u32[]{:S(2)}) collective-permute-start(f32[8,256]{1,0:T(8,128)S(1)} %hop.3), channel_id=1, source_target_pairs={{0,5},{1,4},{2,7},{3,6},{4,1},{5,0},{6,3},{7,2},{8,13},{9,12},{10,... | collective-permute-start | bytes 24584 | tf_op jit(solution)/shard_map/ppermute | solution.py:445
  47.4 4.4 %collective-permute-start.4 = (f32[72,256]{1,0:T(8,128)S(1)}, f32[72,256]{1,0:T(8,128)S(1)}, u32[]{:S(2)}, u32[]{:S(2)}) collective-permute-start(f32[72,256]{1,0:T(8,128)S(1)} %sent.1), channel_id=1, source_target_pairs={{0,2},{1,3},{2,0},{3,1},{4,6},{5,7},{6,4},{7,5},{8,10},{9,11},{10,... | collective-permute-start | bytes 221192 | tf_op jit(solution)/shard_map/ppermute | solution.py:450

commit v11 on v10

--- a/solution.py
+++ b/solution.py
@@ -9,6 +9,7 @@
 F32 = jnp.float32
 BF16 = jnp.bfloat16
 SUB = 8
+LARGE, LARGEST, SMALL = 2.0**100, 2.0**126, 2.0**-20
 
 
 def place(half):
@@ -110,12 +111,6 @@
     eye = (
         lax.broadcasted_iota(jnp.int32, (states, states), 0) == lax.broadcasted_iota(jnp.int32, (states, states), 1)
     ).astype(F32)
-    for k, (mh, ml) in enumerate(((ah, al), (bh, bl))):
-        off = k * half
-        h, l = halves(jnp.where(alive[k] > 0, t_scr[...] * e_scr[off : off + 1, :], eye))
-        mh[0:states, :] = h
-        ml[0:states, :] = l
-
     def body(a0, a1, b0, b1):
         accs = ((a0, a1), (b0, b1))
         mats = ((ah, al), (bh, bl))
@@ -140,13 +135,16 @@
                 pltpu.matmul_acc_lhs(accs[1][m], bh[sl, :], 0)
                 pltpu.matmul_acc_lhs(accs[1][m], bl[sl, :], None)
 
-        def post(k, j, r, peak, freeze):
+        def post(k, j, r, carried, freeze, period):
             s = j * SUB + r
-            look, use = r % 4 == 1 + 2 * k, r % 4 == (2 + 2 * k) % 4
+            peak, low = carried
+            look, use = r % period == (1 + 2 * k) % period, r % period == (2 + 2 * k) % period
             mh, ml = mats[k]
             er = e_scr[pl.ds(s + k * half, 1), :]
             if use:
-                er = er * (1.0 / jnp.max(peak.astype(F32), keepdims=True)[:, :1])
+                size = jnp.max(peak.astype(F32), keepdims=True)[:, :1]
+                low = jnp.minimum(low, size)
+                er = er * jnp.minimum(LARGE / size, LARGEST)
             live = s < alive[k]
             new = None
             for m in range(2):
@@ -164,42 +162,63 @@
                 if look:
                     y = jnp.max(h.reshape(rows // 16, 16, states), axis=0)
                     new = y if new is None else jnp.maximum(new, y)
-            return new if look else peak
-
-        for m in range(2):
-            pltpu.matmul_push_rhs(th_ref[...], 0, m)
-        issue_a(0)
-        one = jnp.ones((16, states), BF16)
-
-        def step(j, r, peaks, freeze, last=False):
+            return (new if look else peak), low
+
+        def step(j, r, peaks, freeze, period, last=False):
             pa, pb = peaks
             issue_b()
-            pa = post(0, j, r, pa, freeze)
+            pa = post(0, j, r, pa, freeze, period)
             if not last:
                 issue_a(None)
-            pb = post(1, j, r, pb, freeze)
+            pb = post(1, j, r, pb, freeze, period)
             return pa, pb
 
-        def eight(j, peaks, freeze):
+        def eight(j, peaks, freeze, period):
             for r in range(1, SUB):
-                peaks = step(j, r, peaks, freeze)
-            return step(j, SUB, peaks, freeze)
-
-        def block(j, peaks):
-            full = jnp.minimum(alive[0], alive[1]) > j * SUB + SUB
-            return lax.cond(full, lambda p: eight(j, p, False), lambda p: eight(j, p, True), peaks)
-
-        peaks = lax.fori_loop(0, blocks - 1, block, (one, one))
-        def tail(peaks, freeze):
-            for r in range(1, SUB):
-                peaks = step(blocks - 1, r, peaks, freeze, r == SUB - 1)
-            return peaks
-
-        full = jnp.minimum(alive[0], alive[1]) >= half
-        lax.cond(full, lambda p: tail(p, False), lambda p: tail(p, True), peaks)
+                peaks = step(j, r, peaks, freeze, period)
+            return step(j, SUB, peaks, freeze, period)
+
+        def run(period):
+            for k, (mh, ml) in enumerate(((ah, al), (bh, bl))):
+                off = k * half
+                h, l = halves(jnp.where(alive[k] > 0, t_scr[...] * (e_scr[off : off + 1, :] * LARGE), eye))
+                mh[0:states, :] = h
+                ml[0:states, :] = l
+
+            for m in range(2):
+                pltpu.matmul_push_rhs(th_ref[...], 0, m)
+            issue_a(0)
+            one = jnp.full((16, states), LARGE, BF16), jnp.ones((1, 1), F32)
+
+            def block(j, peaks):
+                full = jnp.minimum(alive[0], alive[1]) > j * SUB + SUB
+                return lax.cond(
+                    full, lambda p: eight(j, p, False, period), lambda p: eight(j, p, True, period), peaks
+                )
+
+            def tail(peaks, freeze):
+                for r in range(1, SUB):
+                    peaks = step(blocks - 1, r, peaks, freeze, period, r == SUB - 1)
+                return peaks
+
+            peaks = lax.fori_loop(0, blocks - 1, block, (one, one))
+            full = jnp.minimum(alive[0], alive[1]) >= half
+            (_, low_a), (_, low_b) = lax.cond(full, lambda p: tail(p, False), lambda p: tail(p, True), peaks)
+            low = jnp.minimum(low_a, low_b)
+            for mh, _ in mats:
+                low = jnp.minimum(low, jnp.max(mh[...].astype(F32), keepdims=True)[:, :1])
+            return jnp.min(low)
+
+        lowest = run(4)
+
+        @pl.when(lowest < SMALL)
+        def _():
+            run(1)
+
         start_ref[...] = jnp.broadcast_to(unit(init_ref[...]), start_ref.shape)
         for i, (mh, ml) in enumerate(mats):
-            mats_ref[i] = mh[0:states, :].astype(F32) + ml[0:states, :].astype(F32)
+            full = mh[...].astype(F32) + ml[...].astype(F32)
+            mats_ref[i] = full * (1.0 / jnp.max(full, keepdims=True)[:, :1])
 
     shape = (rows, states)
     pl.run_scoped(
@@ -372,8 +391,7 @@
     rows = [v[0:1]]
     for j in range(blocks - 1):
         rows.append(row_dot(v, pre_ref[slot, j, 0], pre_ref[slot, j, 1])[0:1])
-    x = jnp.concatenate(rows, axis=0)
-    total = jnp.sum(x, axis=1, keepdims=True)
+    x = unit(jnp.concatenate(rows, axis=0))
     th, tl = th_ref[...], tl_ref[...]
     lane = lax.broadcasted_iota(jnp.int32, (blocks, 128), 1)
     sub = lax.broadcasted_iota(jnp.int32, (blocks, 128), 0)
@@ -382,7 +400,9 @@
     tiles = range(states // 128)
     for r in range(SUB):
         every = pl.ds(r, blocks, stride=SUB)
-        factor = jnp.concatenate([e_ref[slot, k, every, :] for k in tiles], axis=1) * (1.0 / total)
+        factor = jnp.concatenate([e_ref[slot, k, every, :] for k in tiles], axis=1)
+        if r:
+            factor = factor * (1.0 / total)
         x = row_dot(x, th, tl) * factor
         total = jnp.sum(x, axis=1, keepdims=True)
         alpha = x * (1.0 / total)

time: 52.7 us -> 53.2 us (level)
  Pallas kernels: 21.7 us -> 22.3 us
where the time goes in v11:
time: 53.2 us; the launch traced here: 53 us
  Pallas kernels  22.3 us (42%)
  blocking collectives  17.2 us (32%)
  waiting for transfers between devices  11.6 us (22%)
  starting transfers between devices  1.17 us (2%)
  between operations  0.69 us (1%)
    all_to_all x1, blocking collectives, shards(): lax.all_to_all(x, 'tm', 0, 0, tiled=True).reshape(size * local, frames)  17.2 us
    pallas_call x1, Pallas kernels, transfer(): pl.pallas_call(functools.partial(transfer_kernel, frames), out_shape=(out...  15.1 us
    ppermute x3, waiting for transfers between devices, shards(): vs.append(lax.ppermute(v, 'tm', pairs))  7.29 us
    pallas_call x2, Pallas kernels, slot_pass(): pl.pallas_call(functools.partial(slot_kernel, sent), out_shape=jax.ShapeD...  3.41 us
    pallas_call x5, Pallas kernels, small(): pl.pallas_call(kernel, out_shape=tuple((jax.ShapeDtypeStruct(shape, F32)...  2.61 us
    ppermute x1, waiting for transfers between devices, shards(): got = lax.ppermute(sent, 'tm', [(i, i ^ 2) for i in range(size)])  2.44 us
    ppermute x1, waiting for transfers between devices, shards(): other = lax.ppermute(own, 'tm', [(i, i ^ 1) for i in range(size)])  1.9 us
    pallas_call x1, Pallas kernels, pack(): pl.pallas_call(functools.partial(pack_kernel, n), out_shape=(packed, *(ja...  1.17 us
  transfers between devices with their start and end apart: 5, of which 5 were waited for; matrix products, arithmetic and copies ran while one was open for 0% of the time, Pallas kernels for 5%

profile of v11, /device:TPU:0, one launch (start us, length us, event | category | flops | bytes accessed | tf_op | source)
XLA Modules:
  0.0 53.0 jit_solution(10798689138760334498)
XLA Ops:
  0.6 1.2 %pack.1 = (f32[4,4,32,128]{3,2,1,0:T(8,128)S(1)}, s32[1,256]{1,0:T(1,128)S(1)}, f32[256,256]{1,0:T(8,128)S(1)}, s32[4,4]{1,0:T(4,128)S(1)}, s32[1,2]{1,0:T(1,128)S(1)}, /*index=5*/f32[1,256]{1,0:T(1,128)S(1)}) custom-call(f32[2,32,1024]{2,1,0:T(8,128)} %bitcast.8, s32[1,256]{1,0:T(1,128)} %bitcast.9, f32[256,256]{1,0:T(8,128)} %refs_1_.1, s32[4,4]{1,0:T(4,128)} %refs_2_.1, ...), custom_call_target="tpu_custom_call" | custom-call | tf_op jit(solution)/shard_map/pack/pallas_call | solution.py:365
  1.8 17.2 %all_to_all.5 = f32[16,32,128]{2,1,0:T(8,128)S(1)} all-to-all(f32[16,32,128]{2,1,0:T(8,128)S(1)} %bitcast.7), channel_id=1, replica_groups=mesh['groups'=2,'tm'=16] {'tm'}, dimensions={0} | all-to-all | bytes 524288 | tf_op jit(solution)/shard_map/all_to_all | solution.py:456
  19.0 15.1 %transfer.1 = (f32[2,256,256]{2,1,0:T(8,128)S(1)}, bf16[2,8,2,256,256]{4,3,2,1,0:T(8,128)(2,1)S(1)}, f32[2,2,64,128]{3,2,1,0:T(8,128)S(1)}, f32[2,64,128]{2,1,0:...) custom-call(f32[512,128]{1,0:T(8,128)S(1)} %bitcast.6, ...), custom_call_target="tpu_custom_call" | custom-call | tf_op jit(solution)/shard_map/transfer/pallas_call | solution.py:250
  34.2 0.1 collective-permute-start
  34.3 1.9 %collective-permute-done.other_ref.refs_4_ = f32[2,256,256]{2,1,0:T(8,128)S(1)} collective-permute-done((f32[2,256,256]{2,1,0:T(8,128)S(1)}, f32[2,256,256]{2,1,0:T(8,128)S(1)}, u32[]{:S(2)}, u32[]{:S(2)}) %collective-permute-start) | collective-permute-done | bytes 524320 | tf_op jit(solution)/shard_map/ppermute | solution.py:458
  36.2 0.5 first.1
  36.7 0.3 collective-permute-start.1
  37.0 1.1 %group.1 = (f32[256,256]{1,0:T(8,128)S(1)}, f32[256,256]{1,0:T(8,128)S(1)}) custom-call(f32[2,256,256]{2,1,0:T(8,128)S(1)} %get-tuple-element.24.own_ref, f32[2,256,256]{2,1,0:T(8,128)S(1)} %collective-permute-done.other_ref.refs_4_), custom_call_target="tpu_custom_call" | custom-call | tf_op jit(solution)/shard_map/group/pallas_call | solution.py:330
  38.2 1.6 %collective-permute-done.1.v_ref.refs_1_ = f32[8,256]{1,0:T(8,128)S(1)} collective-permute-done((f32[8,256]{1,0:T(8,128)S(1)}, f32[8,256]{1,0:T(8,128)S(1)}, u32[]{:S(2)}, u32[]{:S(2)}) %collective-permute-start.1) | collective-permute-done | bytes 8224 | tf_op jit(solution)/shard_map/ppermute | solution.py:465
  39.8 0.1 hop.2
  39.9 0.2 collective-permute-start.2
  40.1 2.9 %collective-permute-done.2.v_ref.refs_2_ = f32[8,256]{1,0:T(8,128)S(1)} collective-permute-done((f32[8,256]{1,0:T(8,128)S(1)}, f32[8,256]{1,0:T(8,128)S(1)}, u32[]{:S(2)}, u32[]{:S(2)}) %collective-permute-start.2) | collective-permute-done | bytes 8224 | tf_op jit(solution)/shard_map/ppermute | solution.py:465
  43.0 0.1 hop.3
  43.2 0.3 collective-permute-start.3
  43.5 2.7 %collective-permute-done.3.refs_3_ = f32[8,256]{1,0:T(8,128)S(1)} collective-permute-done((f32[8,256]{1,0:T(8,128)S(1)}, f32[8,256]{1,0:T(8,128)S(1)}, u32[]{:S(2)}, u32[]{:S(2)}) %collective-permute-start.3) | collective-permute-done | bytes 8224 | tf_op jit(solution)/shard_map/ppermute | solution.py:465
  46.2 1.7 %sent.1 = f32[72,256]{1,0:T(8,128)S(1)} custom-call(s32[1,2]{1,0:T(1,128)S(1)} %get-tuple-element.17.lengths_ref, f32[8,256]{1,0:T(8,128)S(1)} %get-tuple-element.23.start_ref.refs_0_, f32[8,256]{1,0:T(8,128)S(1)} %collective-permute-done.1.v_ref.refs_1_, f32[8,256]{1,0:T(8,128)S(1)} %collective-permute-done.2.v_ref.refs_2_, ...), custom_call_target="tpu_custom_call" | custom-call | tf_op jit(solution)/shard_map/sent/pallas_call | solution.py:427
  48.0 0.3 collective-permute-start.4
  48.2 1.7 %kept.1.kept_ref = f32[72,256]{1,0:T(8,128)S(1)} custom-call(s32[1,2]{1,0:T(1,128)S(1)} %get-tuple-element.17.lengths_ref, f32[8,256]{1,0:T(8,128)S(1)} %get-tuple-element.23.start_ref.refs_0_, f32[8,256]{1,0:T(8,128)S(1)} %collective-permute-done.1.v_ref.refs_1_, f32[8,256]{1,0:T(8,128)S(1)} %collective-permute-done.2.v_ref.refs_2_, ...), custom_call_target="tpu_custom_call" | custom-call | tf_op jit(solution)/shard_map/kept/pallas_call | solution.py:427
  49.9 2.4 %collective-permute-done.4.got_ref = f32[72,256]{1,0:T(8,128)S(1)} collective-permute-done((f32[72,256]{1,0:T(8,128)S(1)}, f32[72,256]{1,0:T(8,128)S(1)}, u32[]{:S(2)}, u32[]{:S(2)}) %collective-permute-start.4) | collective-permute-done | bytes 73760 | tf_op jit(solution)/shard_map/ppermute | solution.py:470
  52.4 0.7 %join.1 = (f32[2,64,256]{2,1,0:T(8,128)}, f32[2,64]{1,0:T(2,128)}) custom-call(f32[72,256]{1,0:T(8,128)S(1)} %kept.1.kept_ref, f32[72,256]{1,0:T(8,128)S(1)} %collective-permute-done.4.got_ref), custom_call_target="tpu_custom_call" | custom-call | tf_op jit(solution)/shard_map/join/pallas_call | solution.py:330
Async XLA Ops:
  34.2 2.0 %collective-permute-start = (f32[2,256,256]{2,1,0:T(8,128)S(1)}, f32[2,256,256]{2,1,0:T(8,128)S(1)}, u32[]{:S(2)}, u32[]{:S(2)}) collective-permute-start(f32[2,256,256]{2,1,0:T(8,128)S(1)} %get-tuple-element.24.own_ref), channel_id=1, source_target_pairs={{0,1},{1,0},{2,3},{3,2},{4,5},{5,4},{6,7},{7,6},{8,9},{9,8},{10,11... | collective-permute-start | bytes 1572872 | tf_op jit(solution)/shard_map/ppermute | solution.py:458
  36.7 3.1 %collective-permute-start.1 = (f32[8,256]{1,0:T(8,128)S(1)}, f32[8,256]{1,0:T(8,128)S(1)}, u32[]{:S(2)}, u32[]{:S(2)}) collective-permute-start(f32[8,256]{1,0:T(8,128)S(1)} %first.1), channel_id=1, source_target_pairs={{0,5},{1,4},{2,7},{3,6},{4,1},{5,0},{6,3},{7,2},{8,13},{9,12},{10,... | collective-permute-start | bytes 24584 | tf_op jit(solution)/shard_map/ppermute | solution.py:465
  39.9 3.1 %collective-permute-start.2 = (f32[8,256]{1,0:T(8,128)S(1)}, f32[8,256]{1,0:T(8,128)S(1)}, u32[]{:S(2)}, u32[]{:S(2)}) collective-permute-start(f32[8,256]{1,0:T(8,128)S(1)} %hop.2), channel_id=1, source_target_pairs={{0,3},{1,2},{2,1},{3,0},{4,9},{5,8},{6,11},{7,10},{8,5},{9,4},{10,... | collective-permute-start | bytes 24584 | tf_op jit(solution)/shard_map/ppermute | solution.py:465
  43.2 3.1 %collective-permute-start.3 = (f32[8,256]{1,0:T(8,128)S(1)}, f32[8,256]{1,0:T(8,128)S(1)}, u32[]{:S(2)}, u32[]{:S(2)}) collective-permute-start(f32[8,256]{1,0:T(8,128)S(1)} %hop.3), channel_id=1, source_target_pairs={{0,5},{1,4},{2,7},{3,6},{4,1},{5,0},{6,3},{7,2},{8,13},{9,12},{10,... | collective-permute-start | bytes 24584 | tf_op jit(solution)/shard_map/ppermute | solution.py:465
  48.0 4.4 %collective-permute-start.4 = (f32[72,256]{1,0:T(8,128)S(1)}, f32[72,256]{1,0:T(8,128)S(1)}, u32[]{:S(2)}, u32[]{:S(2)}) collective-permute-start(f32[72,256]{1,0:T(8,128)S(1)} %sent.1), channel_id=1, source_target_pairs={{0,2},{1,3},{2,0},{3,1},{4,6},{5,7},{6,4},{7,5},{8,10},{9,11},{10,... | collective-permute-start | bytes 221192 | tf_op jit(solution)/shard_map/ppermute | solution.py:470

commit v12 on v11

--- a/solution.py
+++ b/solution.py
@@ -205,20 +205,20 @@
             full = jnp.minimum(alive[0], alive[1]) >= half
             (_, low_a), (_, low_b) = lax.cond(full, lambda p: tail(p, False), lambda p: tail(p, True), peaks)
             low = jnp.minimum(low_a, low_b)
-            for mh, _ in mats:
-                low = jnp.minimum(low, jnp.max(mh[...].astype(F32), keepdims=True)[:, :1])
+            for i, (mh, ml) in enumerate(mats):
+                both = mh[...].astype(F32) + ml[...].astype(F32)
+                size = jnp.max(both, keepdims=True)[:, :1]
+                mats_ref[i] = both * (1.0 / size)
+                low = jnp.minimum(low, size)
             return jnp.min(low)
 
+        start_ref[...] = jnp.broadcast_to(unit(init_ref[...]), start_ref.shape)
         lowest = run(4)
 
         @pl.when(lowest < SMALL)
         def _():
             run(1)
 
-        start_ref[...] = jnp.broadcast_to(unit(init_ref[...]), start_ref.shape)
-        for i, (mh, ml) in enumerate(mats):
-            full = mh[...].astype(F32) + ml[...].astype(F32)
-            mats_ref[i] = full * (1.0 / jnp.max(full, keepdims=True)[:, :1])
 
     shape = (rows, states)
     pl.run_scoped(

time: 53.2 us -> 53 us (level)
  no operation moved by 1% of the time
where the time goes in v12:
time: 53 us; the launch traced here: 52.9 us
  Pallas kernels  22.2 us (42%)
  blocking collectives  17.2 us (32%)
  waiting for transfers between devices  11.7 us (22%)
  starting transfers between devices  1.11 us (2%)
  between operations  0.69 us (1%)
    all_to_all x1, blocking collectives, shards(): lax.all_to_all(x, 'tm', 0, 0, tiled=True).reshape(size * local, frames)  17.2 us
    pallas_call x1, Pallas kernels, transfer(): pl.pallas_call(functools.partial(transfer_kernel, frames), out_shape=(out...  15 us
    ppermute x3, waiting for transfers between devices, shards(): vs.append(lax.ppermute(v, 'tm', pairs))  7.34 us
    pallas_call x2, Pallas kernels, slot_pass(): pl.pallas_call(functools.partial(slot_kernel, sent), out_shape=jax.ShapeD...  3.41 us
    pallas_call x5, Pallas kernels, small(): pl.pallas_call(kernel, out_shape=tuple((jax.ShapeDtypeStruct(shape, F32)...  2.61 us
    ppermute x1, waiting for transfers between devices, shards(): got = lax.ppermute(sent, 'tm', [(i, i ^ 2) for i in range(size)])  2.46 us
    ppermute x1, waiting for transfers between devices, shards(): other = lax.ppermute(own, 'tm', [(i, i ^ 1) for i in range(size)])  1.9 us
    pallas_call x1, Pallas kernels, pack(): pl.pallas_call(functools.partial(pack_kernel, n), out_shape=(packed, *(ja...  1.17 us
  transfers between devices with their start and end apart: 5, of which 5 were waited for; matrix products, arithmetic and copies ran while one was open for 0% of the time, Pallas kernels for 5%

profile of v12, /device:TPU:0, one launch (start us, length us, event | category | flops | bytes accessed | tf_op | source)
XLA Modules:
  0.0 52.9 jit_solution(12286633878305875015)
XLA Ops:
  0.6 1.2 %pack.1 = (f32[4,4,32,128]{3,2,1,0:T(8,128)S(1)}, s32[1,256]{1,0:T(1,128)S(1)}, f32[256,256]{1,0:T(8,128)S(1)}, s32[4,4]{1,0:T(4,128)S(1)}, s32[1,2]{1,0:T(1,128)S(1)}, /*index=5*/f32[1,256]{1,0:T(1,128)S(1)}) custom-call(f32[2,32,1024]{2,1,0:T(8,128)} %bitcast.8, s32[1,256]{1,0:T(1,128)} %bitcast.9, f32[256,256]{1,0:T(8,128)} %refs_1_.1, s32[4,4]{1,0:T(4,128)} %refs_2_.1, ...), custom_call_target="tpu_custom_call" | custom-call | tf_op jit(solution)/shard_map/pack/pallas_call | solution.py:365
  1.8 17.2 %all_to_all.5 = f32[16,32,128]{2,1,0:T(8,128)S(1)} all-to-all(f32[16,32,128]{2,1,0:T(8,128)S(1)} %bitcast.7), channel_id=1, replica_groups=mesh['groups'=2,'tm'=16] {'tm'}, dimensions={0} | all-to-all | bytes 524288 | tf_op jit(solution)/shard_map/all_to_all | solution.py:456
  19.0 15.0 %transfer.1 = (f32[2,256,256]{2,1,0:T(8,128)S(1)}, bf16[2,8,2,256,256]{4,3,2,1,0:T(8,128)(2,1)S(1)}, f32[2,2,64,128]{3,2,1,0:T(8,128)S(1)}, f32[2,64,128]{2,1,0:...) custom-call(f32[512,128]{1,0:T(8,128)S(1)} %bitcast.6, ...), custom_call_target="tpu_custom_call" | custom-call | tf_op jit(solution)/shard_map/transfer/pallas_call | solution.py:250
  34.0 0.1 collective-permute-start
  34.1 1.9 %collective-permute-done.other_ref.refs_4_ = f32[2,256,256]{2,1,0:T(8,128)S(1)} collective-permute-done((f32[2,256,256]{2,1,0:T(8,128)S(1)}, f32[2,256,256]{2,1,0:T(8,128)S(1)}, u32[]{:S(2)}, u32[]{:S(2)}) %collective-permute-start) | collective-permute-done | bytes 524320 | tf_op jit(solution)/shard_map/ppermute | solution.py:458
  36.0 0.5 first.1
  36.5 0.3 collective-permute-start.1
  36.8 1.1 %group.1 = (f32[256,256]{1,0:T(8,128)S(1)}, f32[256,256]{1,0:T(8,128)S(1)}) custom-call(f32[2,256,256]{2,1,0:T(8,128)S(1)} %get-tuple-element.24.own_ref, f32[2,256,256]{2,1,0:T(8,128)S(1)} %collective-permute-done.other_ref.refs_4_), custom_call_target="tpu_custom_call" | custom-call | tf_op jit(solution)/shard_map/group/pallas_call | solution.py:330
  38.0 1.6 %collective-permute-done.1.v_ref.refs_1_ = f32[8,256]{1,0:T(8,128)S(1)} collective-permute-done((f32[8,256]{1,0:T(8,128)S(1)}, f32[8,256]{1,0:T(8,128)S(1)}, u32[]{:S(2)}, u32[]{:S(2)}) %collective-permute-start.1) | collective-permute-done | bytes 8224 | tf_op jit(solution)/shard_map/ppermute | solution.py:465
  39.6 0.1 hop.2
  39.7 0.1 collective-permute-start.2
  39.9 2.9 %collective-permute-done.2.v_ref.refs_2_ = f32[8,256]{1,0:T(8,128)S(1)} collective-permute-done((f32[8,256]{1,0:T(8,128)S(1)}, f32[8,256]{1,0:T(8,128)S(1)}, u32[]{:S(2)}, u32[]{:S(2)}) %collective-permute-start.2) | collective-permute-done | bytes 8224 | tf_op jit(solution)/shard_map/ppermute | solution.py:465
  42.8 0.1 hop.3
  43.0 0.3 collective-permute-start.3
  43.3 2.8 %collective-permute-done.3.refs_3_ = f32[8,256]{1,0:T(8,128)S(1)} collective-permute-done((f32[8,256]{1,0:T(8,128)S(1)}, f32[8,256]{1,0:T(8,128)S(1)}, u32[]{:S(2)}, u32[]{:S(2)}) %collective-permute-start.3) | collective-permute-done | bytes 8224 | tf_op jit(solution)/shard_map/ppermute | solution.py:465
  46.1 1.7 %sent.1 = f32[72,256]{1,0:T(8,128)S(1)} custom-call(s32[1,2]{1,0:T(1,128)S(1)} %get-tuple-element.17.lengths_ref, f32[8,256]{1,0:T(8,128)S(1)} %get-tuple-element.23.start_ref.refs_0_, f32[8,256]{1,0:T(8,128)S(1)} %collective-permute-done.1.v_ref.refs_1_, f32[8,256]{1,0:T(8,128)S(1)} %collective-permute-done.2.v_ref.refs_2_, ...), custom_call_target="tpu_custom_call" | custom-call | tf_op jit(solution)/shard_map/sent/pallas_call | solution.py:427
  47.8 0.2 collective-permute-start.4
  48.0 1.7 %kept.1.kept_ref = f32[72,256]{1,0:T(8,128)S(1)} custom-call(s32[1,2]{1,0:T(1,128)S(1)} %get-tuple-element.17.lengths_ref, f32[8,256]{1,0:T(8,128)S(1)} %get-tuple-element.23.start_ref.refs_0_, f32[8,256]{1,0:T(8,128)S(1)} %collective-permute-done.1.v_ref.refs_1_, f32[8,256]{1,0:T(8,128)S(1)} %collective-permute-done.2.v_ref.refs_2_, ...), custom_call_target="tpu_custom_call" | custom-call | tf_op jit(solution)/shard_map/kept/pallas_call | solution.py:427
  49.7 2.5 %collective-permute-done.4.got_ref = f32[72,256]{1,0:T(8,128)S(1)} collective-permute-done((f32[72,256]{1,0:T(8,128)S(1)}, f32[72,256]{1,0:T(8,128)S(1)}, u32[]{:S(2)}, u32[]{:S(2)}) %collective-permute-start.4) | collective-permute-done | bytes 73760 | tf_op jit(solution)/shard_map/ppermute | solution.py:470
  52.2 0.7 %join.1 = (f32[2,64,256]{2,1,0:T(8,128)}, f32[2,64]{1,0:T(2,128)}) custom-call(f32[72,256]{1,0:T(8,128)S(1)} %kept.1.kept_ref, f32[72,256]{1,0:T(8,128)S(1)} %collective-permute-done.4.got_ref), custom_call_target="tpu_custom_call" | custom-call | tf_op jit(solution)/shard_map/join/pallas_call | solution.py:330
Async XLA Ops:
  34.0 2.0 %collective-permute-start = (f32[2,256,256]{2,1,0:T(8,128)S(1)}, f32[2,256,256]{2,1,0:T(8,128)S(1)}, u32[]{:S(2)}, u32[]{:S(2)}) collective-permute-start(f32[2,256,256]{2,1,0:T(8,128)S(1)} %get-tuple-element.24.own_ref), channel_id=1, source_target_pairs={{0,1},{1,0},{2,3},{3,2},{4,5},{5,4},{6,7},{7,6},{8,9},{9,8},{10,11... | collective-permute-start | bytes 1572872 | tf_op jit(solution)/shard_map/ppermute | solution.py:458
  36.5 3.1 %collective-permute-start.1 = (f32[8,256]{1,0:T(8,128)S(1)}, f32[8,256]{1,0:T(8,128)S(1)}, u32[]{:S(2)}, u32[]{:S(2)}) collective-permute-start(f32[8,256]{1,0:T(8,128)S(1)} %first.1), channel_id=1, source_target_pairs={{0,5},{1,4},{2,7},{3,6},{4,1},{5,0},{6,3},{7,2},{8,13},{9,12},{10,... | collective-permute-start | bytes 24584 | tf_op jit(solution)/shard_map/ppermute | solution.py:465
  39.7 3.1 %collective-permute-start.2 = (f32[8,256]{1,0:T(8,128)S(1)}, f32[8,256]{1,0:T(8,128)S(1)}, u32[]{:S(2)}, u32[]{:S(2)}) collective-permute-start(f32[8,256]{1,0:T(8,128)S(1)} %hop.2), channel_id=1, source_target_pairs={{0,3},{1,2},{2,1},{3,0},{4,9},{5,8},{6,11},{7,10},{8,5},{9,4},{10,... | collective-permute-start | bytes 24584 | tf_op jit(solution)/shard_map/ppermute | solution.py:465
  43.0 3.1 %collective-permute-start.3 = (f32[8,256]{1,0:T(8,128)S(1)}, f32[8,256]{1,0:T(8,128)S(1)}, u32[]{:S(2)}, u32[]{:S(2)}) collective-permute-start(f32[8,256]{1,0:T(8,128)S(1)} %hop.3), channel_id=1, source_target_pairs={{0,5},{1,4},{2,7},{3,6},{4,1},{5,0},{6,3},{7,2},{8,13},{9,12},{10,... | collective-permute-start | bytes 24584 | tf_op jit(solution)/shard_map/ppermute | solution.py:465
  47.8 4.4 %collective-permute-start.4 = (f32[72,256]{1,0:T(8,128)S(1)}, f32[72,256]{1,0:T(8,128)S(1)}, u32[]{:S(2)}, u32[]{:S(2)}) collective-permute-start(f32[72,256]{1,0:T(8,128)S(1)} %sent.1), channel_id=1, source_target_pairs={{0,2},{1,3},{2,0},{3,1},{4,6},{5,7},{6,4},{7,5},{8,10},{9,11},{10,... | collective-permute-start | bytes 221192 | tf_op jit(solution)/shard_map/ppermute | solution.py:470
